TPU v7x, 128 devices: a whole 4x4x4 slice. The times are simulated.
128 devices in a mesh: lon: 8 (over y_lo, z), lat: 16 (over y_hi, x, core).
Axes of the slice: x: 4, y: 4 (y_hi: 2, y_lo: 2; y = y_hi * 2 + y_lo), z: 4, core: 2. Of those that a mesh axis runs over, the one named last changes fastest.
Arguments:
- costate: float32 [72, 8, 128, 2048], P(None, None, 'lat', 'lon'), may hold values from -6 to 6
- diffusion: float32 [2, 71, 128, 2048], P(None, None, 'lat', 'lon'), may hold values from 0.025 to 400
- east_courant: float32 [2, 128, 2048], P(None, 'lat', 'lon'), may hold values from 0.05 to 0.9
- north_courant: float32 [2, 128, 2048], P(None, 'lat', 'lon'), may hold values from 0.02 to 0.45
- south_courant: float32 [2, 128, 2048], P(None, 'lat', 'lon'), may hold values from 0.02 to 0.45
- polar_shift: int32 [2, 128], replicated, may hold values from -1024 to 1024
- owners: int32 [2, 163840, 1], P(None, ('lon', 'lat')), may hold values from 0 to 127; in each aligned block of 1280 rows (0 to 1279, 1280 to 2559, ..., all dimensions but the last counted through in order) at most 16 rows name the same one
- columns: int32 [2, 163840], P(None, ('lon', 'lat')), may hold values from 0 to 2047
- sounding_counts: int32 [2, 128], P(None, ('lon', 'lat')), may hold values from 640 to 1280, as said below
- kernels: float32 [2, 72, 163840], P(None, None, ('lon', 'lat')), may hold values from 0.1 to 2
- misfits: float32 [2, 8, 163840], P(None, None, ('lon', 'lat')), may hold values from -6 to 6
Outputs:
- adjoint_state: float32 [72, 8, 128, 2048], P(None, None, 'lat', 'lon')
- flux_gradient: float32 [8, 128, 2048], P(None, 'lat', 'lon')
Inputs may be any that keep to these rules, and one draw needn't show every extreme that they name: `owners`: in every step no owner is named by more than 16 of one device's 1280 soundings, and in every step some owner is named by exactly 16 of some device's soundings. `sounding_counts`: in every step some device is full and some holds exactly 640 live soundings.
All inputs are finite; a program needn't handle non-finite values.
Results may differ from a plain program's by a relative error of at most 0.0001.
Values sent between devices are 32-bit elements; how exact they have to be, the bound alone decides.
No kernel may reach another device: no remote copies, remote signals or barrier semaphores. Data moves between devices by JAX's collectives and lax.ppermute only.
A program may use at most 128 MiB of HBM per device.

v0:
```python
import functools

import jax
import jax.numpy as jnp
from jax import lax
from jax.experimental import pallas as pl
from jax.experimental.pallas import tpu as pltpu
from jax.sharding import PartitionSpec as P

AXES = ("lon", "lat")
LANES = 128
CAP = 16
GROUP = 8
F32 = jnp.float32
BF16 = jnp.bfloat16
MIB = 1024 * 1024


def vmem():
    return pl.BlockSpec(memory_space=pltpu.VMEM)


def smem():
    return pl.BlockSpec(memory_space=pltpu.SMEM)


def hbm():
    return pl.BlockSpec(memory_space=pltpu.HBM)


def params(limit):
    return pltpu.CompilerParams(vmem_limit_bytes=limit * MIB)


def held(x):
    return pltpu.with_memory_space_constraint(x, pltpu.VMEM)


def pinned(x):
    return pltpu.with_memory_space_constraint(x, pltpu.HBM)


def resident(*shape):
    return pltpu.VMEM(shape, F32)


def chunk(source, target, done, g):
    at = pl.ds(g * GROUP, GROUP)
    return pltpu.make_async_copy(source.at[at], target.at[at], done.at[g])


def start_all(source, target, done):
    for g in range(source.shape[0] // GROUP):
        chunk(source, target, done, g).start()


def wait_all(source, target, done):
    for g in range(source.shape[0] // GROUP):
        chunk(source, target, done, g).wait()


def dot(a, b, contract=((1,), (0,))):
    return lax.dot_general(a, b, (contract, ((), ())), preferred_element_type=F32)


def halves(x):
    high = x.astype(BF16)
    return high, (x - high.astype(F32)).astype(BF16)


def pack_kernel(
    counts, owners, columns, kernels, misfits, out, payload, target, staged, done
):
    steps, levels, held = kernels.shape
    tracers = misfits.shape[1]
    shape = (LANES, LANES)
    device = lax.broadcasted_iota(jnp.int32, shape, 0)
    table = counting_table()
    for step in range(steps):
        owner = owners[step]
        live = lax.broadcasted_iota(jnp.int32, owner.shape, 1) < counts[step, 0]
        owner = jnp.where(live, owner, -1)
        seen = jnp.zeros(shape, F32)
        for start in range(0, held, LANES):
            here = owner[:, start : start + LANES]
            hot = device == here
            counted = dot(jnp.where(hot, 1.0, 0.0).astype(BF16), table)
            rank = jnp.sum(
                jnp.where(hot, counted[:, :LANES] + seen, 0.0), axis=0, keepdims=True
            )
            seen = seen + counted[:, LANES:]
            target[step : step + 1, start : start + LANES] = jnp.where(
                here >= 0, here * CAP + rank.astype(jnp.int32), -1
            )
        column = columns[step : step + 1, :].astype(F32) + 1.0
        column = jnp.where(lax.broadcasted_iota(jnp.int32, (8, held), 0) == 0, column, 0.0)
        unused = jnp.zeros((LANES - levels - tracers - 8, held), F32)
        high, low = halves(
            jnp.concatenate([kernels[step], misfits[step], column, unused], axis=0)
        )
        payload[step, :LANES, :] = high
        payload[step, LANES:, :] = low
    owned = 256 // CAP
    tiles = out.shape[0] // owned

    def copy(i):
        at = pl.ds(i * owned, owned)
        return pltpu.make_async_copy(staged.at[at], out.at[at], done.at[i])

    def place(i, carry):
        slot = lax.broadcasted_iota(jnp.int32, (owned * CAP, held), 0) + i * owned * CAP
        for step in range(steps):
            hot = jnp.where(slot == target[step : step + 1, :], 1.0, 0.0).astype(BF16)
            both = dot(hot, payload[step], ((1,), (1,)))
            both = both[:, :LANES] + both[:, LANES:]
            staged[pl.ds(i * owned, owned), step * CAP : (step + 1) * CAP, :] = both.reshape(
                owned, CAP, LANES
            )
        copy(i).start()
        return carry

    lax.fori_loop(0, tiles, place, 0)
    for i in range(tiles):
        copy(i).wait()


def counting_table():
    shape = (LANES, LANES)
    earlier = lax.broadcasted_iota(jnp.int32, shape, 0) < lax.broadcasted_iota(
        jnp.int32, shape, 1
    )
    return jnp.concatenate(
        [jnp.where(earlier, 1.0, 0.0), jnp.ones(shape, F32)], axis=1
    ).astype(BF16)


def packed(counts, owners, columns, kernels, misfits):
    steps, slots = columns.shape
    devices = lax.axis_size("lon") * lax.axis_size("lat")
    return pl.pallas_call(
        pack_kernel,
        out_shape=pltpu.HBM((devices, steps * CAP, LANES), F32),
        in_specs=[smem()] + [vmem()] * 4,
        out_specs=hbm(),
        scratch_shapes=[
            pltpu.VMEM((steps, 2 * LANES, slots), BF16),
            pltpu.VMEM((steps, slots), jnp.int32),
            pltpu.VMEM((devices, steps * CAP, LANES), F32),
            pltpu.SemaphoreType.DMA((devices * CAP // 256,)),
        ],
        compiler_params=params(8),
        name="pack",
    )(counts, held(owners), held(columns), held(kernels), held(misfits))


def forcing_kernel(step, received, result, out, fields, hots, place, ordered, done):
    levels, rows, tracers, cells = out.shape
    slots = received.shape[0] * CAP
    blocks = slots // LANES
    sources = LANES // CAP
    sub = lax.broadcasted_iota(jnp.int32, (rows, LANES), 0)
    at_column = levels + tracers
    for b in range(blocks):
        span = slice(b * LANES, (b + 1) * LANES)
        block = received[b * sources : (b + 1) * sources, step * CAP : (step + 1) * CAP, :]
        turned = block.reshape(LANES, LANES).T
        high, low = halves(turned)
        fields[:LANES, span] = high
        fields[LANES:, span] = low
        row = (turned[at_column : at_column + 1].astype(jnp.int32) - 1) >> 8
        hots[b * rows : (b + 1) * rows, :] = jnp.where(sub == row, 1.0, 0.0)
    counted = dot(hots[...].astype(BF16), counting_table())
    run = jnp.zeros((rows, LANES), F32)
    runs = []
    for b in range(blocks):
        runs.append(run)
        run = run + counted[b * rows : (b + 1) * rows, LANES:]
    filled = jnp.floor((run + (LANES - 1.0)) * (1.0 / LANES))
    start = jnp.zeros((rows, LANES), F32)
    for j in range(1, rows):
        start = start + jnp.where(sub >= j, pltpu.roll(filled, j, 0), 0.0)
    for b in range(blocks):
        hot = hots[b * rows : (b + 1) * rows, :]
        at = counted[b * rows : (b + 1) * rows, :LANES] + runs[b] + start * float(LANES)
        at = jnp.sum(hot * at, axis=0, keepdims=True)
        live = jnp.sum(hot, axis=0, keepdims=True) > 0.0
        place[:, b * LANES : (b + 1) * LANES] = jnp.where(live, at, -1.0)
    counts = [jnp.max(filled[r : r + 1, :]).astype(jnp.int32) for r in range(rows)]
    used = sum(counts)
    wide = 2 * LANES

    def sort(i, carry):
        slot = (lax.broadcasted_iota(jnp.int32, (wide, slots), 0) + i * wide).astype(F32)
        hot = jnp.where(slot == place[...], 1.0, 0.0).astype(BF16)
        both = dot(fields[...], hot, ((1,), (1,)))
        ordered[:, pl.ds(pl.multiple_of(i * wide, wide), wide)] = both[:LANES] + both[LANES:]
        return carry

    lax.fori_loop(0, (used + 1) // 2, sort, 0)
    out[...] = jnp.zeros_like(out)
    cell = lax.broadcasted_iota(jnp.int32, (cells, LANES), 0)
    first = jnp.int32(0)
    for r in range(rows):
        names = (cell + (r * cells + 1)).astype(F32)

        def add(p, carry):
            block = ordered[:, pl.ds(pl.multiple_of(p * LANES, LANES), LANES)]
            hot = jnp.where(names == block[at_column : at_column + 1], 1.0, 0.0).astype(BF16)
            product = block[:levels][:, None, :] * block[levels:at_column][None]
            high, low = halves(product.reshape(levels * tracers, LANES))
            total = dot(high, hot, ((1,), (1,))) + dot(low, hot, ((1,), (1,)))
            out[:, r, :, :] += total.reshape(levels, tracers, cells)
            return carry

        lax.fori_loop(first, first + counts[r], add, 0)
        first = first + counts[r]
        pltpu.make_async_copy(out.at[:, r], result.at[:, r], done.at[r]).start()
    for r in range(rows):
        pltpu.make_async_copy(out.at[:, r], result.at[:, r], done.at[r]).wait()


def forcing(step, received, levels, tracers, rows, cells):
    slots = received.shape[0] * CAP
    return pl.pallas_call(
        functools.partial(forcing_kernel, step),
        out_shape=pltpu.HBM((levels, rows, tracers, cells), F32),
        in_specs=[vmem()],
        out_specs=hbm(),
        scratch_shapes=[
            pltpu.VMEM((levels, rows, tracers, cells), F32),
            pltpu.VMEM((2 * LANES, slots), BF16),
            pltpu.VMEM((slots // LANES * rows, LANES), F32),
            pltpu.VMEM((1, slots), F32),
            pltpu.VMEM((LANES, slots + rows * LANES), F32),
            pltpu.SemaphoreType.DMA((rows,)),
        ],
        compiler_params=params(14),
        name="forcing",
    )(held(received))


def spread(x, row, tracers):
    return jnp.broadcast_to(x[row : row + 1, :], (tracers, x.shape[1]))


def eliminate(level, above, carry, rights, ratios):
    below, ratio, values = carry
    if above is None:
        above = jnp.zeros_like(below)
    inverse = 1.0 / (1.0 + below + above + below * ratio)
    lower = below * inverse
    ratio = -above * inverse
    ratios[level] = ratio
    tracers = rights[0].shape[0]
    fresh = [
        spread(inverse, r, tracers) * rights[r] + spread(lower, r, tracers) * values[r]
        for r in range(len(rights))
    ]
    return (above, ratio, fresh)


def substitute(step, ratios, couplings, column, fields, results, done):
    diffused, first, last, polar = fields
    levels, rows, tracers, cells = diffused.shape
    lat = lax.axis_index("lat")
    at_start = lat == 0

    def picked(x):
        return jnp.where(at_start, x[step, 0:1, :], x[step, rows - 1 : rows, :])

    north, south, east = [picked(x) for x in couplings]
    own = jnp.broadcast_to(1.0 - north - south, (tracers, cells))
    side = jnp.broadcast_to(jnp.where(at_start, north, south), (tracers, cells))
    polar[levels] = jnp.broadcast_to(east, (tracers, cells))
    groups = levels // GROUP
    top = pl.ds(levels, 1)
    weight = pltpu.make_async_copy(polar.at[top], results[3].at[top], done.at[3, groups])
    weight.start()
    lane = lax.broadcasted_iota(jnp.int32, (tracers, LANES), 1)

    def group(i, solved):
        at = groups - 1 - i
        west = jnp.zeros((tracers, LANES), F32)
        for j in range(GROUP - 1, -1, -1):
            level = at * GROUP + j
            ratio = ratios[level]
            fresh = []
            for r in range(rows):
                value = diffused[level, r] - spread(ratio, r, tracers) * solved[r]
                diffused[level, r] = value
                fresh.append(value)
                lanes = j * rows + r
                moved = pltpu.roll(value[:, :LANES], lanes, 1) if lanes else value[:, :LANES]
                west = jnp.where(lane == lanes, moved, west)
            solved = fresh
            first[level] = solved[0]
            last[level] = solved[rows - 1]
            polar[level] = own * jnp.where(
                at_start, solved[0], solved[rows - 1]
            ) + side * jnp.where(at_start, solved[1], solved[rows - 2])
        column[at] = west
        for k, (field, result) in enumerate(zip(fields, results)):
            chunk(field, result, done.at[k], at).start()
        return solved

    lax.fori_loop(0, groups, group, [jnp.zeros((tracers, cells), F32)] * rows)
    weight.wait()
    for k, (field, result) in enumerate(zip(fields, results)):
        for g in range(groups):
            chunk(field, result, done.at[k], g).wait()


def forward_sweep(levels, rows, tracers, cells, diffusion, right_of):
    zero = jnp.zeros((rows, cells), F32)
    carry = (zero, zero, [jnp.zeros((tracers, cells), F32)] * rows)
    groups = levels // GROUP

    def one(g, j, above, carry):
        rights, ratios, store = right_of(g, j, above is None)
        carry = eliminate(g * GROUP + j, above, carry, rights, ratios)
        store(carry[2])
        return carry

    def group(g, carry):
        for j in range(GROUP):
            carry = one(g, j, diffusion(g * GROUP + j), carry)
        return carry

    carry = lax.fori_loop(0, groups - 1, group, carry)
    for j in range(GROUP):
        level = levels - GROUP + j
        carry = one(groups - 1, j, diffusion(level) if level < levels - 1 else None, carry)


def first_kernel(
    step,
    costate,
    diffusion_in,
    north_in,
    south_in,
    east_in,
    result,
    first_out,
    last_out,
    polar_out,
    column,
    staged,
    ratios,
    diffused,
    first,
    last,
    polar,
    diffusion,
    couplings,
    arrived,
    sent,
    ready,
):
    levels, tracers, rows, cells = costate.shape
    small = [pltpu.make_async_copy(diffusion_in.at[step], diffusion, ready.at[0])]
    for k, coupling in enumerate((north_in, south_in, east_in)):
        small.append(pltpu.make_async_copy(coupling, couplings.at[k], ready.at[1 + k]))
    chunk(costate, staged, arrived, 0).start()
    for copy in small:
        copy.start()
    for g in range(1, levels // GROUP):
        chunk(costate, staged, arrived, g).start()
    for copy in small:
        copy.wait()

    def right_of(g, j, final):
        if j == 0:
            chunk(costate, staged, arrived, g).wait()
        level = g * GROUP + j
        rights = [staged[level, :, r, :] for r in range(rows)]

        def store(values):
            for r in range(rows):
                diffused[level, r] = values[r]

        return rights, ratios, store

    forward_sweep(levels, rows, tracers, cells, lambda level: diffusion[level], right_of)
    views = [couplings.at[k] for k in range(3)]
    fields = (diffused, first, last, polar)
    results = (result, first_out, last_out, polar_out)
    substitute(step, ratios, views, column, fields, results, sent)


def meridional(level, row, diffused, after, before, coefs):
    rows = diffused.shape[1]
    own, north, south = coefs
    up = diffused[level, row + 1] if row < rows - 1 else after[level]
    down = diffused[level, row - 1] if row > 0 else before[level]
    return own * diffused[level, row] + north * up + south * down


def borders_kernel(
    step,
    shift,
    column,
    north,
    south,
    nearby,
    after,
    before,
    polar_in,
    turned_out,
    edge,
    polar,
    turned,
    ready,
):
    groups, tracers, lanes = column.shape
    rows, cells = north.shape[1:]
    fetch = pltpu.make_async_copy(polar_in, polar, ready.at[0])
    lat = lax.axis_index("lat")
    last_lat = lax.axis_size("lat") - 1
    at_pole = (lat == 0) | (lat == last_lat)

    @pl.when(at_pole)
    def _():
        fetch.start()

    lane = lax.broadcasted_iota(jnp.int32, (tracers, lanes), 1)

    def along_lanes(x):
        shape = (rows, lanes)
        own_lane = (lax.broadcasted_iota(jnp.int32, shape, 1) & (rows - 1)) == (
            lax.broadcasted_iota(jnp.int32, shape, 0)
        )
        picked = jnp.where(own_lane, jnp.broadcast_to(x[step, :, :1], shape), 0.0)
        return jnp.broadcast_to(jnp.sum(picked, axis=0, keepdims=True), (tracers, lanes))

    n, s = along_lanes(north), along_lanes(south)
    own = 1.0 - n - s

    def group(i, carry):
        here = column[i]
        up = pltpu.roll(here, lanes - 1, 1)
        down = pltpu.roll(here, 1, 1)
        for j in range(GROUP):
            level = i * GROUP + j
            bottom, top = j * rows, j * rows + rows - 1
            up = jnp.where(lane == top, pltpu.roll(after[level, :, :LANES], top, 1), up)
            moved = before[level, :, :LANES]
            moved = pltpu.roll(moved, bottom, 1) if bottom else moved
            down = jnp.where(lane == bottom, moved, down)
        edge[i] = own * here + n * up + s * down
        return carry

    sending = pltpu.make_async_copy(turned, turned_out, ready.at[1])

    @pl.when(at_pole)
    def _():
        fetch.wait()
        levels = turned.shape[0]
        circle = cells * lax.axis_size("lon")
        amount = jnp.where(lat == 0, shift[step, 0], shift[step, rows * last_lat + rows - 1])
        back = 2 * cells - (lax.rem(amount + 2 * circle, circle) & (cells - 1))
        weight = jnp.concatenate([polar[levels], nearby[levels]], axis=1)

        def one(i, carry):
            for j in range(GROUP):
                level = i * GROUP + j
                row = jnp.concatenate([polar[level], nearby[level]], axis=1)
                moved = row + weight * (pltpu.roll(row, 2 * cells - 1, 1) - row)
                turned[level] = pltpu.roll(moved, back, 1)[:, :cells]
            return carry

        lax.fori_loop(0, groups, one, 0)
        sending.start()

    lax.fori_loop(0, groups, group, 0)

    @pl.when(at_pole)
    def _():
        sending.wait()


def prepare_stencil(step, north, south, east, coefs):
    rows, cells = north.shape[1:]
    tracers = coefs.shape[2]
    for r in range(rows):
        n = north[step, r : r + 1, :]
        s = south[step, r : r + 1, :]
        coefs[0, r] = jnp.broadcast_to(1.0 - n - s, (tracers, cells))
        coefs[1, r] = jnp.broadcast_to(n, (tracers, cells))
        coefs[2, r] = jnp.broadcast_to(s, (tracers, cells))
        coefs[3, r] = jnp.broadcast_to(east[step, r : r + 1, :], (tracers, cells))


def transported(level, lane_at, diffused, after, before, edge_row, coefs, pole):
    rows, tracers, cells = diffused.shape[1:]
    lat = lax.axis_index("lat")
    last = lax.broadcasted_iota(jnp.int32, (tracers, cells), 1) == cells - 1
    result = []
    for r in range(rows):
        mer = meridional(level, r, diffused, after, before, [coefs[k, r] for k in range(3)])
        arrived = pltpu.roll(edge_row, LANES - 1 - (lane_at * rows + r), 1)
        arrived = jnp.concatenate([arrived] * (cells // LANES), axis=1)
        following = jnp.where(last, arrived, pltpu.roll(mer, cells - 1, 1))
        result.append(mer + coefs[3, r] * (following - mer))
    polar = pole[level]
    result[0] = jnp.where(lat == 0, polar, result[0])
    result[rows - 1] = jnp.where(lat == lax.axis_size("lat") - 1, polar, result[rows - 1])
    return result


def streams(sources, south_pole, north_pole, targets, pole, done):
    lat = lax.axis_index("lat")
    last_lat = lax.axis_size("lat") - 1
    last = len(sources)
    groups = pole.shape[0] // GROUP
    for g in range(groups):
        for k, (source, target) in enumerate(zip(sources, targets)):
            chunk(source, target, done.at[k], g).start()

        @pl.when(lat == 0)
        def _():
            chunk(south_pole, pole, done.at[last], g).start()

        @pl.when(lat == last_lat)
        def _():
            chunk(north_pole, pole, done.at[last], g).start()

    def wait(g):
        for k, (source, target) in enumerate(zip(sources, targets)):
            chunk(source, target, done.at[k], g).wait()

        @pl.when((lat == 0) | (lat == last_lat))
        def _():
            chunk(south_pole, pole, done.at[last], g).wait()

    return wait


def middle_kernel(
    step,
    before_step,
    forcing_in,
    after_in,
    before_in,
    south_pole,
    north_pole,
    edge,
    diffusion,
    north,
    south,
    east,
    result,
    first_out,
    last_out,
    polar_out,
    column,
    surface,
    coefs,
    ratios,
    diffused,
    forced,
    after,
    before,
    pole,
    solved,
    first,
    last,
    polar,
    arrived,
    sent,
):
    levels, rows, tracers, cells = diffused.shape
    wait = streams(
        (before_step, forcing_in, after_in, before_in),
        south_pole,
        north_pole,
        (diffused, forced, after, before),
        pole,
        arrived,
    )
    prepare_stencil(step, north, south, east, coefs)

    def right_of(g, j, final):
        if j == 0:
            wait(g)
        level = g * GROUP + j
        rights = transported(level, j, diffused, after, before, edge[g], coefs, pole)
        rights = [rights[r] + forced[level, r] for r in range(rows)]
        if final:
            for r in range(rows):
                surface[r] = rights[r]

        def store(values):
            for r in range(rows):
                solved[level, r] = values[r]

        return rights, ratios, store

    forward_sweep(
        levels, rows, tracers, cells, lambda level: diffusion[step - 1, level], right_of
    )
    couplings = (north, south, east)
    fields = (solved, first, last, polar)
    results = (result, first_out, last_out, polar_out)
    substitute(step - 1, ratios, couplings, column, fields, results, sent)


def last_kernel(
    step,
    before_step,
    forcing_in,
    after_in,
    before_in,
    south_pole,
    north_pole,
    edge,
    north,
    south,
    east,
    surface,
    state,
    gradient,
    coefs,
    diffused,
    forced,
    after,
    before,
    pole,
    staged,
    arrived,
    sent,
):
    levels, rows, tracers, cells = diffused.shape
    wait = streams(
        (before_step, forcing_in, after_in, before_in),
        south_pole,
        north_pole,
        (diffused, forced, after, before),
        pole,
        arrived,
    )
    prepare_stencil(step, north, south, east, coefs)

    def group(g, carry):
        wait(g)
        edge_row = edge[g]
        for j in range(GROUP):
            level = g * GROUP + j
            values = transported(level, j, diffused, after, before, edge_row, coefs, pole)
            for r in range(rows):
                staged[level, :, r, :] = values[r] + forced[level, r]
        chunk(staged, state, sent, g).start()
        return carry

    lax.fori_loop(0, levels // GROUP, group, 0)
    for r in range(rows):
        gradient[:, r, :] = surface[r] + staged[levels - 1, :, r, :]
    wait_all(staged, state, sent)


def boundaries(first, last, polar):
    lat_count = lax.axis_size("lat")
    up = [(i, i + 1) for i in range(lat_count - 1)]
    down = [(j, i) for i, j in up]
    nearby = lax.ppermute(polar, AXES, circles((0, lat_count - 1), 1))
    return lax.ppermute(first, "lat", down), lax.ppermute(last, "lat", up), nearby


def circles(lats, hops):
    lat_count = lax.axis_size("lat")
    lon_count = lax.axis_size("lon")
    return [
        (((j + hops) % lon_count) * lat_count + lat, j * lat_count + lat)
        for lat in lats
        for j in range(lon_count)
    ]


def exchange(after, before, nearby, polar, column, north, south, shift, step):
    lat_count = lax.axis_size("lat")
    lon_count = lax.axis_size("lon")
    poles = (0, lat_count - 1)
    levels, tracers, cells = after.shape
    turned, edge = pl.pallas_call(
        functools.partial(borders_kernel, step),
        out_shape=[pltpu.HBM((levels, tracers, cells), F32), resident(*column.shape)],
        in_specs=[smem()] + [vmem()] * 6 + [hbm()],
        out_specs=[hbm(), vmem()],
        scratch_shapes=[
            pltpu.VMEM(polar.shape, F32),
            pltpu.VMEM((levels, tracers, cells), F32),
            pltpu.SemaphoreType.DMA((2,)),
        ],
        compiler_params=params(4),
        name="borders",
    )(shift, column, north, south, *[held(x) for x in (nearby, after, before)], pinned(polar))
    west = [(i, (i - 1) % lon_count) for i in range(lon_count)]
    edge = lax.ppermute(edge, "lon", west)
    moved = []
    for lat, row in zip(poles, (0, shift.shape[1] - 1)):
        hops = jnp.mod(shift[step, row], cells * lon_count) // cells
        moved.append(
            lax.switch(
                hops,
                [
                    functools.partial(
                        lambda k, lat, x: lax.ppermute(x, AXES, circles((lat,), k)), k, lat
                    )
                    for k in range(lon_count)
                ],
                turned,
            )
        )
    return pinned(after), pinned(before), pinned(moved[0]), pinned(moved[1]), held(edge)


def per_device(
    costate,
    diffusion,
    east_courant,
    north_courant,
    south_courant,
    polar_shift,
    owners,
    columns,
    sounding_counts,
    kernels,
    misfits,
):
    levels, tracers, rows, cells = costate.shape
    owner_rows = owners.reshape(owners.shape[0], 1, owners.shape[1])
    couplings = (north_courant, south_courant, east_courant)
    groups = levels // GROUP

    solved_shapes = [
        pltpu.HBM((levels, rows, tracers, cells), F32),
        pltpu.HBM((levels, tracers, cells), F32),
        pltpu.HBM((levels, tracers, cells), F32),
        pltpu.HBM((levels + 1, tracers, cells), F32),
        resident(groups, tracers, LANES),
    ]
    ratios = pltpu.VMEM((levels, rows, cells), F32)
    coefs = pltpu.VMEM((4, rows, tracers, cells), F32)
    field = pltpu.VMEM((levels, rows, tracers, cells), F32)
    line = pltpu.VMEM((levels, tracers, cells), F32)
    solved_scratch = [field, line, line, pltpu.VMEM((levels + 1, tracers, cells), F32)]
    solved_specs = [hbm()] * 4 + [vmem()]
    leaving = pltpu.SemaphoreType.DMA((4, groups + 1))
    output = pltpu.VMEM(costate.shape, F32)
    semaphores = pltpu.SemaphoreType.DMA((groups,))
    diffused, first, last, polar, column = pl.pallas_call(
        functools.partial(first_kernel, 1),
        out_shape=solved_shapes,
        in_specs=[hbm()] * 5,
        out_specs=solved_specs,
        scratch_shapes=[
            output,
            ratios,
            *solved_scratch,
            pltpu.VMEM(diffusion.shape[1:], F32),
            pltpu.VMEM((3,) + east_courant.shape, F32),
            semaphores,
            leaving,
            pltpu.SemaphoreType.DMA((4,)),
        ],
        compiler_params=params(16),
        name="first",
    )(*[pinned(x) for x in (costate, diffusion, *couplings)])
    couplings = [held(x) for x in couplings]
    diffusion = held(diffusion)
    counts, column = lax.optimization_barrier((sounding_counts, column))
    around = boundaries(first, last, polar)
    sent = packed(counts, owner_rows, columns, kernels, misfits)
    sent, *around = lax.optimization_barrier((sent, *around))
    got = lax.all_to_all(sent, AXES, 0, 0, tiled=True)
    forced = pinned(forcing(1, got, levels, tracers, rows, cells))
    around = exchange(*around, polar, column, *couplings[:2], polar_shift, 1)
    scratch = [field, field, line, line, line]
    transfers = pltpu.SemaphoreType.DMA((5, groups))
    solved, first, last, polar, column, surface = pl.pallas_call(
        functools.partial(middle_kernel, 1),
        out_shape=solved_shapes + [resident(rows, tracers, cells)],
        in_specs=[hbm()] * 6 + [vmem()] * 5,
        out_specs=solved_specs + [vmem()],
        scratch_shapes=[coefs, ratios, *scratch, *solved_scratch, transfers, leaving],
        compiler_params=params(26),
        name="middle",
    )(pinned(diffused), forced, *around, diffusion, *couplings)
    around = boundaries(first, last, polar)
    got, column = lax.optimization_barrier((got, column))
    forced = pinned(forcing(0, got, levels, tracers, rows, cells))
    forced, *around = lax.optimization_barrier((forced, *around))
    around = exchange(*around, polar, column, *couplings[:2], polar_shift, 0)
    return tuple(
        pl.pallas_call(
            functools.partial(last_kernel, 0),
            out_shape=[
                pltpu.HBM(costate.shape, F32),
                jax.ShapeDtypeStruct((tracers, rows, cells), F32),
            ],
            in_specs=[hbm()] * 6 + [vmem()] * 5,
            out_specs=[hbm(), vmem()],
            scratch_shapes=[coefs, *scratch, output, transfers, semaphores],
            compiler_params=params(22),
            name="last",
        )(pinned(solved), pinned(forced), *around, *couplings, surface)
    )


def solution(mesh):
    return jax.shard_map(
        per_device,
        mesh=mesh,
        in_specs=(
            P(None, None, "lat", "lon"),
            P(None, None, "lat", "lon"),
            P(None, "lat", "lon"),
            P(None, "lat", "lon"),
            P(None, "lat", "lon"),
            P(),
            P(None, ("lon", "lat"), None),
            P(None, ("lon", "lat")),
            P(None, ("lon", "lat")),
            P(None, None, ("lon", "lat")),
            P(None, None, ("lon", "lat")),
        ),
        out_specs=(P(None, None, "lat", "lon"), P(None, "lat", "lon")),
        check_vma=False,
    )
```

profile of v0, /device:TPU:0, one launch (start us, length us, event | category | flops | bytes accessed | tf_op | source)
XLA Modules:
  0.0 143.7 jit_solution(6249600778103723185)
XLA Ops:
  0.7 7.9 %first.1 = (f32[72,8,8,256]{3,2,1,0:T(8,128)}, f32[72,8,256]{2,1,0:T(8,128)}, f32[72,8,256]{2,1,0:T(8,128)}, f32[73,8,256]{2,1,0:T(8,128)}, f32[9,8,128]{2,1,0:T(8,128)S(1)}) custom-call(f32[72,8,8,256]{3,2,1,0:T(8,128)} %costate.1, f32[2,71,8,256]{3,2,1,0:T(8,128)} %diffusion.1, f32[2,8,256]{2,1,0:T(8,128)} %north.7, f32[2,8,256]{2,1,0:T(8,128)} %south.7, ...), custom_call_target="tpu_custom_call" | custom-call | tf_op jit(solution)/shard_map/first/pallas_call | solution.py:750
  8.6 7.2 %collective-permute-start.34 = (f32[73,8,256]{2,1,0:T(8,128)}, f32[73,8,256]{2,1,0:T(8,128)S(1)}, u32[]{:S(2)}, u32[]{:S(2)}) collective-permute-start(f32[73,8,256]{2,1,0:T(8,128)} %get-tuple-element.102.polar_in), channel_id=1, source_target_pairs={{16,0},{32,16},{48,32},{64,48},{80,64},{96,80},{112,96},{0,112},{3... | collective-permute-start | bytes 1794056 | tf_op jit(solution)/shard_map/ppermute | solution.py:664
  15.8 1.3 collective-permute-start.32
  17.1 3.1 %collective-permute-start.33 = (f32[72,8,256]{2,1,0:T(8,128)}, f32[72,8,256]{2,1,0:T(8,128)S(1)}, u32[]{:S(2)}, u32[]{:S(2)}) collective-permute-start(f32[72,8,256]{2,1,0:T(8,128)} %get-tuple-element.101), channel_id=1, source_target_pairs={{0,1},{1,2},{2,3},{3,4},{4,5},{5,6},{6,7},{7,8},{8,9},{9,10},{10,1... | collective-permute-start | bytes 1769480 | tf_op jit(solution)/shard_map/ppermute | solution.py:665
  20.3 6.4 %pack.1 = f32[128,32,128]{2,1,0:T(8,128)} custom-call(s32[2,1]{1,0:T(2,128)S(1)} %copy.13.counts, s32[2,1,1280]{2,1,0:T(1,128)S(1)} %bitcast.5, s32[2,1280]{1,0:T(2,128)S(1)} %copy-done.16, f32[2,72,1280]{2,1,0:T(8,128)S(1)} %copy-done.7, f32[2,8,1280]{2,1,0:T(8,128)S(1)} %copy-done.13), custom_call_target="tpu_custom_call" | custom-call | tf_op jit(solution)/shard_map/pack/pallas_call | solution.py:140
  27.5 0.8 copy-done.3
  28.4 1.5 %collective-permute-done.34.nearby = f32[73,8,256]{2,1,0:T(8,128)S(1)} collective-permute-done((f32[73,8,256]{2,1,0:T(8,128)}, f32[73,8,256]{2,1,0:T(8,128)S(1)}, u32[]{:S(2)}, u32[]{:S(2)}) %collective-permute-start.34) | collective-permute-done | bytes 598048 | tf_op jit(solution)/shard_map/ppermute | solution.py:664
  30.7 8.7 %all-to-all-start = ((f32[128,32,128]{2,1,0:T(8,128)}), f32[128,32,128]{2,1,0:T(8,128)S(1)}, u32[]{:S(2)}, u32[]{:S(2)}) async-start(f32[128,32,128]{2,1,0:T(8,128)} %pack.1), calls=%async_computation | async-start | bytes 4194304 | tf_op jit(solution)/shard_map/all_to_all | solution.py:774
  39.5 1.1 copy-done.2
  40.5 1.1 copy-done.4
  41.6 1.1 copy-done.9
  42.7 4.0 %borders.2 = (f32[72,8,256]{2,1,0:T(8,128)}, f32[9,8,128]{2,1,0:T(8,128)S(1)}) custom-call(s32[2,128]{1,0:T(2,128)S(1)} %copy-done.14, f32[9,8,128]{2,1,0:T(8,128)S(1)} %get-tuple-element.106.column, f32[2,8,256]{2,1,0:T(8,128)S(1)} %copy-done.10, f32[2,8,256]{2,1,0:T(8,128)S(1)} %copy-done.11, f32[73,8,256]{2,1,0:T(8,128)S(1)} %copy-done.9, ...), custom_call_target="tpu_custom_call" | custom-call | tf_op jit(solution)/shard_map/borders/pallas_call | solution.py:683
  46.7 3.9 %collective-permute-start.35 = (f32[9,8,128]{2,1,0:T(8,128)S(1)}, f32[9,8,128]{2,1,0:T(8,128)S(1)}, u32[]{:S(2)}, u32[]{:S(2)}) collective-permute-start(f32[9,8,128]{2,1,0:T(8,128)S(1)} %get-tuple-element.109), channel_id=1, source_target_pairs={{0,112},{16,0},{32,16},{48,32},{64,48},{80,64},{96,80},{112,96},{1... | collective-permute-start | bytes 110600 | tf_op jit(solution)/shard_map/ppermute | solution.py:697
  55.3 1.5 %conditional.5 = (f32[72,8,256]{2,1,0:T(8,128)}) conditional(s32[]{:T(128)} %clamp.13, f32[72,8,256]{2,1,0:T(8,128)} %get-tuple-element.108, f32[72,8,256]{2,1,0:T(8,128)} %get-tuple-element.108, f32[72,8,256]{2,1,0:T(8,128)} %get-tuple-element.108, f32[72,8,256]{2,1,0:T(8,128)} %get-tuple-element.108, ...), branch_computations={%region_8.9_spmd, %region_9.10_spmd, %region_10.11_spmd, %region_1... | conditional | bytes 2359344 | solution.py:702
  55.3 1.5 %collective-permute-start.12 = (f32[72,8,256]{2,1,0:T(8,128)}, f32[72,8,256]{2,1,0:T(8,128)}, u32[]{:S(2)}, u32[]{:S(2)}) collective-permute-start(f32[72,8,256]{2,1,0:T(8,128)} %param.12), channel_id=1, source_target_pairs={{79,15},{95,31},{111,47},{127,63},{15,79},{31,95},{47,111},{63,127}} | collective-permute-start | bytes 1769480 | tf_op jit(solution)/shard_map/cond/branch_4_fun/ppermute | solution.py:706
  56.8 17.4 %conditional.4 = (f32[72,8,256]{2,1,0:T(8,128)}) conditional(s32[]{:T(128)} %clamp.12, f32[72,8,256]{2,1,0:T(8,128)} %get-tuple-element.108, f32[72,8,256]{2,1,0:T(8,128)} %get-tuple-element.108, f32[72,8,256]{2,1,0:T(8,128)} %get-tuple-element.108, f32[72,8,256]{2,1,0:T(8,128)} %get-tuple-element.108, ...), branch_computations={%region_0.1_spmd, %region_1.2_spmd, %region_2.3_spmd, %region_3.4_... | conditional | bytes 2359344 | solution.py:702
  56.8 2.2 %collective-permute-start.2 = (f32[72,8,256]{2,1,0:T(8,128)}, f32[72,8,256]{2,1,0:T(8,128)}, u32[]{:S(2)}, u32[]{:S(2)}) collective-permute-start(f32[72,8,256]{2,1,0:T(8,128)} %param.2), channel_id=1, source_target_pairs={{32,0},{48,16},{64,32},{80,48},{96,64},{112,80},{0,96},{16,112}} | collective-permute-start | bytes 1769480 | tf_op jit(solution)/shard_map/cond/branch_2_fun/ppermute | solution.py:706
  59.0 15.2 %collective-permute-done.2 = f32[72,8,256]{2,1,0:T(8,128)} collective-permute-done((f32[72,8,256]{2,1,0:T(8,128)}, f32[72,8,256]{2,1,0:T(8,128)}, u32[]{:S(2)}, u32[]{:S(2)}) %collective-permute-start.2) | collective-permute-done | bytes 589856 | tf_op jit(solution)/shard_map/cond/branch_2_fun/ppermute | solution.py:706
  74.2 11.0 %forcing.2.forcing_in = f32[72,8,8,256]{3,2,1,0:T(8,128)} custom-call(f32[128,32,128]{2,1,0:T(8,128)S(1)} %all-to-all-done.received), custom_call_target="tpu_custom_call" | custom-call | tf_op jit(solution)/shard_map/forcing/pallas_call | solution.py:224
  85.2 8.0 %middle.1 = (f32[72,8,8,256]{3,2,1,0:T(8,128)}, f32[72,8,256]{2,1,0:T(8,128)}, f32[72,8,256]{2,1,0:T(8,128)}, f32[73,8,256]{2,1,0:T(8,128)}, f32[9,8,128]{2,1,0:T(8,128)S(1)}, /*index=5*/f32[8,8,256]{2,1,0:T(8,128)S(1)}) custom-call(f32[72,8,8,256]{3,2,1,0:T(8,128)} %get-tuple-element.97.before_step, f32[72,8,8,256]{3,2,1,0:T(8,128)} %forcing.2.forcing_in, ...), custom_call_target="tpu_custom_call" | custom-call | tf_op jit(solution)/shard_map/middle/pallas_call | solution.py:779
  93.3 2.3 %collective-permute-start.38 = (f32[73,8,256]{2,1,0:T(8,128)}, f32[73,8,256]{2,1,0:T(8,128)S(1)}, u32[]{:S(2)}, u32[]{:S(2)}) collective-permute-start(f32[73,8,256]{2,1,0:T(8,128)} %get-tuple-element.115.polar_in), channel_id=1, source_target_pairs={{16,0},{32,16},{48,32},{64,48},{80,64},{96,80},{112,96},{0,112},{3... | collective-permute-start | bytes 1794056 | tf_op jit(solution)/shard_map/ppermute | solution.py:664
  95.6 1.3 collective-permute-start.36
  96.9 3.1 %collective-permute-start.37 = (f32[72,8,256]{2,1,0:T(8,128)}, f32[72,8,256]{2,1,0:T(8,128)S(1)}, u32[]{:S(2)}, u32[]{:S(2)}) collective-permute-start(f32[72,8,256]{2,1,0:T(8,128)} %get-tuple-element.114), channel_id=1, source_target_pairs={{0,1},{1,2},{2,3},{3,4},{4,5},{5,6},{6,7},{7,8},{8,9},{9,10},{10,1... | collective-permute-start | bytes 1769480 | tf_op jit(solution)/shard_map/ppermute | solution.py:665
  100.0 11.1 %forcing.3.forcing_in = f32[72,8,8,256]{3,2,1,0:T(8,128)} custom-call(f32[128,32,128]{2,1,0:T(8,128)S(1)} %all-to-all-done.received), custom_call_target="tpu_custom_call" | custom-call | tf_op jit(solution)/shard_map/forcing/pallas_call | solution.py:224
  111.1 4.0 %borders.3 = (f32[72,8,256]{2,1,0:T(8,128)}, f32[9,8,128]{2,1,0:T(8,128)S(1)}) custom-call(s32[2,128]{1,0:T(2,128)S(1)} %copy-done.14, f32[9,8,128]{2,1,0:T(8,128)S(1)} %get-tuple-element.119.column, f32[2,8,256]{2,1,0:T(8,128)S(1)} %copy-done.10, f32[2,8,256]{2,1,0:T(8,128)S(1)} %copy-done.11, f32[73,8,256]{2,1,0:T(8,128)S(1)} %collective-permute-done.38.nearby, ...), custom_call_target="tpu_custom_call" | custom-call | tf_op jit(solution)/shard_map/borders/pallas_call | solution.py:683
  115.2 3.3 %collective-permute-start.39 = (f32[9,8,128]{2,1,0:T(8,128)S(1)}, f32[9,8,128]{2,1,0:T(8,128)S(1)}, u32[]{:S(2)}, u32[]{:S(2)}) collective-permute-start(f32[9,8,128]{2,1,0:T(8,128)S(1)} %get-tuple-element.122), channel_id=1, source_target_pairs={{0,112},{16,0},{32,16},{48,32},{64,48},{80,64},{96,80},{112,96},{1... | collective-permute-start | bytes 110600 | tf_op jit(solution)/shard_map/ppermute | solution.py:697
  122.3 1.5 %conditional.7 = (f32[72,8,256]{2,1,0:T(8,128)}) conditional(s32[]{:T(128)} %clamp.15, f32[72,8,256]{2,1,0:T(8,128)} %get-tuple-element.121, f32[72,8,256]{2,1,0:T(8,128)} %get-tuple-element.121, f32[72,8,256]{2,1,0:T(8,128)} %get-tuple-element.121, f32[72,8,256]{2,1,0:T(8,128)} %get-tuple-element.121, ...), branch_computations={%region_24.25_spmd, %region_25.26_spmd, %region_26.27_spmd, %regio... | conditional | bytes 2359344 | solution.py:702
  122.4 1.5 %collective-permute-start.24 = (f32[72,8,256]{2,1,0:T(8,128)}, f32[72,8,256]{2,1,0:T(8,128)}, u32[]{:S(2)}, u32[]{:S(2)}) collective-permute-start(f32[72,8,256]{2,1,0:T(8,128)} %param.24), channel_id=1, source_target_pairs={{15,15},{31,31},{47,47},{63,63},{79,79},{95,95},{111,111},{127,127}} | collective-permute-start | bytes 1769480 | tf_op jit(solution)/shard_map/cond/branch_0_fun/ppermute | solution.py:706
  123.9 12.1 %conditional.6 = (f32[72,8,256]{2,1,0:T(8,128)}) conditional(s32[]{:T(128)} %clamp.14, f32[72,8,256]{2,1,0:T(8,128)} %get-tuple-element.121, f32[72,8,256]{2,1,0:T(8,128)} %get-tuple-element.121, f32[72,8,256]{2,1,0:T(8,128)} %get-tuple-element.121, f32[72,8,256]{2,1,0:T(8,128)} %get-tuple-element.121, ...), branch_computations={%region_16.17_spmd, %region_17.18_spmd, %region_18.19_spmd, %regio... | conditional | bytes 2359344 | solution.py:702
  123.9 1.9 %collective-permute-start.20 = (f32[72,8,256]{2,1,0:T(8,128)}, f32[72,8,256]{2,1,0:T(8,128)}, u32[]{:S(2)}, u32[]{:S(2)}) collective-permute-start(f32[72,8,256]{2,1,0:T(8,128)} %param.20), channel_id=1, source_target_pairs={{64,0},{80,16},{96,32},{112,48},{0,64},{16,80},{32,96},{48,112}} | collective-permute-start | bytes 1769480 | tf_op jit(solution)/shard_map/cond/branch_4_fun/ppermute | solution.py:706
  125.8 10.2 %collective-permute-done.20 = f32[72,8,256]{2,1,0:T(8,128)} collective-permute-done((f32[72,8,256]{2,1,0:T(8,128)}, f32[72,8,256]{2,1,0:T(8,128)}, u32[]{:S(2)}, u32[]{:S(2)}) %collective-permute-start.20) | collective-permute-done | bytes 589856 | tf_op jit(solution)/shard_map/cond/branch_4_fun/ppermute | solution.py:706
  136.0 7.6 %last.1 = (f32[72,8,8,256]{3,2,1,0:T(8,128)}, f32[8,8,256]{2,1,0:T(8,128)}) custom-call(f32[72,8,8,256]{3,2,1,0:T(8,128)} %get-tuple-element.110.before_step, f32[72,8,8,256]{3,2,1,0:T(8,128)} %forcing.3.forcing_in, f32[72,8,256]{2,1,0:T(8,128)} %copy-done.5, f32[72,8,256]{2,1,0:T(8,128)} %copy-done.6, f32[72,8,256]{2,1,0:T(8,128)} %get-tuple-element.130.south_pole, ...), custom_call_target="tpu_custom_call" | custom-call | tf_op jit(solution)/shard_map/last/pallas_call | solution.py:794
  (44 shorter events, 2.4 us)
Async XLA Ops:
  0.6 19.6 %copy-start.17 = (s32[2,1]{0,1:T(1,128)S(1)}, s32[2,1]{0,1:T(1,128)}, u32[]{:S(2)}) copy-start(s32[2,1]{0,1:T(1,128)} %param.51) | copy-start | bytes 28
  0.6 19.6 %copy-start.13 = (f32[2,8,1280]{2,1,0:T(8,128)S(1)}, f32[2,8,1280]{2,1,0:T(8,128)}, u32[]{:S(2)}) copy-start(f32[2,8,1280]{2,1,0:T(8,128)} %misfits.1) | copy-start | bytes 245764
  0.7 19.6 %copy-start.7 = (f32[2,72,1280]{2,1,0:T(8,128)S(1)}, f32[2,72,1280]{2,1,0:T(8,128)}, u32[]{:S(2)}) copy-start(f32[2,72,1280]{2,1,0:T(8,128)} %kernels.1) | copy-start | bytes 2211844
  0.7 19.6 %copy-start.16 = (s32[2,1280]{1,0:T(2,128)S(1)}, s32[2,1280]{1,0:T(2,128)}, u32[]{:S(2)}) copy-start(s32[2,1280]{1,0:T(2,128)} %columns.1) | copy-start | bytes 30724
  0.7 19.6 %copy-start.15 = (s32[2,1280,1]{1,2,0:T(1,128)S(1)}, s32[2,1280,1]{1,2,0:T(1,128)}, u32[]{:S(2)}) copy-start(s32[2,1280,1]{1,2,0:T(1,128)} %param.49) | copy-start | bytes 30724
  8.6 30.8 %copy-start.10 = (f32[2,8,256]{2,1,0:T(8,128)S(1)}, f32[2,8,256]{2,1,0:T(8,128)}, u32[]{:S(2)}) copy-start(f32[2,8,256]{2,1,0:T(8,128)} %north.7) | copy-start | bytes 49156
  8.6 30.8 %copy-start.11 = (f32[2,8,256]{2,1,0:T(8,128)S(1)}, f32[2,8,256]{2,1,0:T(8,128)}, u32[]{:S(2)}) copy-start(f32[2,8,256]{2,1,0:T(8,128)} %south.7) | copy-start | bytes 49156
  8.6 30.8 %copy-start.14 = (s32[2,128]{1,0:T(2,128)S(1)}, s32[2,128]{1,0:T(2,128)}, u32[]{:S(2)}) copy-start(s32[2,128]{1,0:T(2,128)} %shift.3) | copy-start | bytes 3076
  8.6 21.3 %collective-permute-start.34 = (f32[73,8,256]{2,1,0:T(8,128)}, f32[73,8,256]{2,1,0:T(8,128)S(1)}, u32[]{:S(2)}, u32[]{:S(2)}) collective-permute-start(f32[73,8,256]{2,1,0:T(8,128)} %get-tuple-element.102.polar_in), channel_id=1, source_target_pairs={{16,0},{32,16},{48,32},{64,48},{80,64},{96,80},{112,96},{0,112},{3... | collective-permute-start | bytes 1794056 | tf_op jit(solution)/shard_map/ppermute | solution.py:664
  15.8 10.9 %collective-permute-start.32 = (f32[72,8,256]{2,1,0:T(8,128)}, f32[72,8,256]{2,1,0:T(8,128)S(1)}, u32[]{:S(2)}, u32[]{:S(2)}) collective-permute-start(f32[72,8,256]{2,1,0:T(8,128)} %get-tuple-element.100), channel_id=1, source_target_pairs={{1,0},{2,1},{3,2},{4,3},{5,4},{6,5},{7,6},{8,7},{9,8},{10,9},{11,1... | collective-permute-start | bytes 1769480 | tf_op jit(solution)/shard_map/ppermute | solution.py:665
  17.1 10.4 %collective-permute-start.33 = (f32[72,8,256]{2,1,0:T(8,128)}, f32[72,8,256]{2,1,0:T(8,128)S(1)}, u32[]{:S(2)}, u32[]{:S(2)}) collective-permute-start(f32[72,8,256]{2,1,0:T(8,128)} %get-tuple-element.101), channel_id=1, source_target_pairs={{0,1},{1,2},{2,3},{3,4},{4,5},{5,6},{6,7},{7,8},{8,9},{9,10},{10,1... | collective-permute-start | bytes 1769480 | tf_op jit(solution)/shard_map/ppermute | solution.py:665
  26.7 0.8 copy-start.1
  27.5 0.8 copy-start.3
  29.9 0.8 copy-start.8
  30.7 43.5 %all-to-all-start = ((f32[128,32,128]{2,1,0:T(8,128)}), f32[128,32,128]{2,1,0:T(8,128)S(1)}, u32[]{:S(2)}, u32[]{:S(2)}) async-start(f32[128,32,128]{2,1,0:T(8,128)} %pack.1), calls=%async_computation | async-start | bytes 4194304 | tf_op jit(solution)/shard_map/all_to_all | solution.py:774
  39.5 1.1 copy-start.2
  40.5 1.1 copy-start.4
  41.6 1.1 copy-start.9
  42.7 42.6 %copy-start = (f32[2,71,8,256]{3,2,1,0:T(8,128)S(1)}, f32[2,71,8,256]{3,2,1,0:T(8,128)}, u32[]{:S(2)}) copy-start(f32[2,71,8,256]{3,2,1,0:T(8,128)} %diffusion.1) | copy-start | bytes 3489796
  42.7 42.6 %copy-start.12 = (f32[2,8,256]{2,1,0:T(8,128)S(1)}, f32[2,8,256]{2,1,0:T(8,128)}, u32[]{:S(2)}) copy-start(f32[2,8,256]{2,1,0:T(8,128)} %east.3) | copy-start | bytes 49156
  46.7 38.5 %collective-permute-start.35 = (f32[9,8,128]{2,1,0:T(8,128)S(1)}, f32[9,8,128]{2,1,0:T(8,128)S(1)}, u32[]{:S(2)}, u32[]{:S(2)}) collective-permute-start(f32[9,8,128]{2,1,0:T(8,128)S(1)} %get-tuple-element.109), channel_id=1, source_target_pairs={{0,112},{16,0},{32,16},{48,32},{64,48},{80,64},{96,80},{112,96},{1... | collective-permute-start | bytes 110600 | tf_op jit(solution)/shard_map/ppermute | solution.py:697
  55.3 1.5 %collective-permute-start.12 = (f32[72,8,256]{2,1,0:T(8,128)}, f32[72,8,256]{2,1,0:T(8,128)}, u32[]{:S(2)}, u32[]{:S(2)}) collective-permute-start(f32[72,8,256]{2,1,0:T(8,128)} %param.12), channel_id=1, source_target_pairs={{79,15},{95,31},{111,47},{127,63},{15,79},{31,95},{47,111},{63,127}} | collective-permute-start | bytes 1769480 | tf_op jit(solution)/shard_map/cond/branch_4_fun/ppermute | solution.py:706
  56.8 17.4 %collective-permute-start.2 = (f32[72,8,256]{2,1,0:T(8,128)}, f32[72,8,256]{2,1,0:T(8,128)}, u32[]{:S(2)}, u32[]{:S(2)}) collective-permute-start(f32[72,8,256]{2,1,0:T(8,128)} %param.2), channel_id=1, source_target_pairs={{32,0},{48,16},{64,32},{80,48},{96,64},{112,80},{0,96},{16,112}} | collective-permute-start | bytes 1769480 | tf_op jit(solution)/shard_map/cond/branch_2_fun/ppermute | solution.py:706
  93.3 17.8 %collective-permute-start.38 = (f32[73,8,256]{2,1,0:T(8,128)}, f32[73,8,256]{2,1,0:T(8,128)S(1)}, u32[]{:S(2)}, u32[]{:S(2)}) collective-permute-start(f32[73,8,256]{2,1,0:T(8,128)} %get-tuple-element.115.polar_in), channel_id=1, source_target_pairs={{16,0},{32,16},{48,32},{64,48},{80,64},{96,80},{112,96},{0,112},{3... | collective-permute-start | bytes 1794056 | tf_op jit(solution)/shard_map/ppermute | solution.py:664
  95.6 15.5 %collective-permute-start.36 = (f32[72,8,256]{2,1,0:T(8,128)}, f32[72,8,256]{2,1,0:T(8,128)S(1)}, u32[]{:S(2)}, u32[]{:S(2)}) collective-permute-start(f32[72,8,256]{2,1,0:T(8,128)} %get-tuple-element.113), channel_id=1, source_target_pairs={{1,0},{2,1},{3,2},{4,3},{5,4},{6,5},{7,6},{8,7},{9,8},{10,9},{11,1... | collective-permute-start | bytes 1769480 | tf_op jit(solution)/shard_map/ppermute | solution.py:665
  96.9 14.2 %collective-permute-start.37 = (f32[72,8,256]{2,1,0:T(8,128)}, f32[72,8,256]{2,1,0:T(8,128)S(1)}, u32[]{:S(2)}, u32[]{:S(2)}) collective-permute-start(f32[72,8,256]{2,1,0:T(8,128)} %get-tuple-element.114), channel_id=1, source_target_pairs={{0,1},{1,2},{2,3},{3,4},{4,5},{5,6},{6,7},{7,8},{8,9},{9,10},{10,1... | collective-permute-start | bytes 1769480 | tf_op jit(solution)/shard_map/ppermute | solution.py:665
  111.1 24.8 %copy-start.5 = (f32[72,8,256]{2,1,0:T(8,128)}, f32[72,8,256]{2,1,0:T(8,128)S(1)}, u32[]{:S(2)}) copy-start(f32[72,8,256]{2,1,0:T(8,128)S(1)} %collective-permute-done.36.after.after_in) | copy-start | bytes 1769476
  111.1 24.8 %copy-start.6 = (f32[72,8,256]{2,1,0:T(8,128)}, f32[72,8,256]{2,1,0:T(8,128)S(1)}, u32[]{:S(2)}) copy-start(f32[72,8,256]{2,1,0:T(8,128)S(1)} %collective-permute-done.37.before.before_in) | copy-start | bytes 1769476
  115.2 20.8 %collective-permute-start.39 = (f32[9,8,128]{2,1,0:T(8,128)S(1)}, f32[9,8,128]{2,1,0:T(8,128)S(1)}, u32[]{:S(2)}, u32[]{:S(2)}) collective-permute-start(f32[9,8,128]{2,1,0:T(8,128)S(1)} %get-tuple-element.122), channel_id=1, source_target_pairs={{0,112},{16,0},{32,16},{48,32},{64,48},{80,64},{96,80},{112,96},{1... | collective-permute-start | bytes 110600 | tf_op jit(solution)/shard_map/ppermute | solution.py:697
  122.4 1.5 %collective-permute-start.24 = (f32[72,8,256]{2,1,0:T(8,128)}, f32[72,8,256]{2,1,0:T(8,128)}, u32[]{:S(2)}, u32[]{:S(2)}) collective-permute-start(f32[72,8,256]{2,1,0:T(8,128)} %param.24), channel_id=1, source_target_pairs={{15,15},{31,31},{47,47},{63,63},{79,79},{95,95},{111,111},{127,127}} | collective-permute-start | bytes 1769480 | tf_op jit(solution)/shard_map/cond/branch_0_fun/ppermute | solution.py:706
  123.9 12.1 %collective-permute-start.20 = (f32[72,8,256]{2,1,0:T(8,128)}, f32[72,8,256]{2,1,0:T(8,128)}, u32[]{:S(2)}, u32[]{:S(2)}) collective-permute-start(f32[72,8,256]{2,1,0:T(8,128)} %param.20), channel_id=1, source_target_pairs={{64,0},{80,16},{96,32},{112,48},{0,64},{16,80},{32,96},{48,112}} | collective-permute-start | bytes 1769480 | tf_op jit(solution)/shard_map/cond/branch_4_fun/ppermute | solution.py:706
where the time goes:
time: 144 us
  Pallas kernels  60.1 us (42%)
  starting transfers between devices  41.1 us (29%)
  waiting for transfers between devices  26.9 us (19%)
  between operations  9.09 us (6%)
  local copies, waits for them, and re-layouts  6.43 us (4%)
    ppermute x4, waiting for transfers between devices, exchange(): lax.ppermute(x, AXES, circles((lat,), k))  25.3 us
    pallas_call x2, Pallas kernels, forcing(): pl.pallas_call(functools.partial(forcing_kernel, step), out_shape=pltpu.H...  22.1 us
    ppermute x2, starting transfers between devices, boundaries(): nearby = lax.ppermute(polar, AXES, circles((0, lat_count - 1), 1))  9.46 us
    all_to_all x1, starting transfers between devices, per_device(): got = lax.all_to_all(sent, AXES, 0, 0, tiled=True)  8.7 us
    pallas_call x2, Pallas kernels, exchange(): pl.pallas_call(functools.partial(borders_kernel, step), out_shape=[pltpu....  8.07 us
    pallas_call x1, Pallas kernels, per_device(): pl.pallas_call(functools.partial(middle_kernel, 1), out_shape=solved_shap...  8.05 us
    pallas_call x1, Pallas kernels, per_device(): pl.pallas_call(functools.partial(first_kernel, 1), out_shape=solved_shape...  7.9 us
    pallas_call x1, Pallas kernels, per_device(): pl.pallas_call(functools.partial(last_kernel, 0), out_shape=[pltpu.HBM(co...  7.58 us
  transfers between devices with their start and end apart: 13, of which 3 were waited for; matrix products, arithmetic and copies ran while one was open for 1% of the time, Pallas kernels for 23%

commit v1 on v0

--- a/solution.py
+++ b/solution.py
@@ -34,6 +34,10 @@
 
 def held(x):
     return pltpu.with_memory_space_constraint(x, pltpu.VMEM)
+
+
+def anywhere():
+    return pl.BlockSpec(memory_space=pl.ANY)
 
 
 def pinned(x):
@@ -108,9 +112,8 @@
         return pltpu.make_async_copy(staged.at[at], out.at[at], done.at[i])
 
     def place(i, carry):
-        slot = lax.broadcasted_iota(jnp.int32, (owned * CAP, held), 0) + i * owned * CAP
         for step in range(steps):
-            hot = jnp.where(slot == target[step : step + 1, :], 1.0, 0.0).astype(BF16)
+            hot = one_hot(target[step : step + 1, :] - i * owned * CAP, owned * CAP)
             both = dot(hot, payload[step], ((1,), (1,)))
             both = both[:, :LANES] + both[:, LANES:]
             staged[pl.ds(i * owned, owned), step * CAP : (step + 1) * CAP, :] = both.reshape(
@@ -122,6 +125,13 @@
     lax.fori_loop(0, tiles, place, 0)
     for i in range(tiles):
         copy(i).wait()
+
+
+def one_hot(at, size):
+    at = jnp.where((at >= 0) & (at < size), at, -1).astype(F32).astype(BF16)
+    shape = (size, at.shape[1])
+    row = lax.broadcasted_iota(jnp.int32, shape, 0).astype(F32).astype(BF16)
+    return jnp.where(row == at, jnp.ones(shape, BF16), jnp.zeros(shape, BF16))
 
 
 def counting_table():
@@ -190,8 +200,7 @@
     wide = 2 * LANES
 
     def sort(i, carry):
-        slot = (lax.broadcasted_iota(jnp.int32, (wide, slots), 0) + i * wide).astype(F32)
-        hot = jnp.where(slot == place[...], 1.0, 0.0).astype(BF16)
+        hot = one_hot(place[...] - (i * wide).astype(F32), wide)
         both = dot(fields[...], hot, ((1,), (1,)))
         ordered[:, pl.ds(pl.multiple_of(i * wide, wide), wide)] = both[:LANES] + both[LANES:]
         return carry
@@ -271,11 +280,22 @@
     north, south, east = [picked(x) for x in couplings]
     own = jnp.broadcast_to(1.0 - north - south, (tracers, cells))
     side = jnp.broadcast_to(jnp.where(at_start, north, south), (tracers, cells))
-    polar[levels] = jnp.broadcast_to(east, (tracers, cells))
     groups = levels // GROUP
-    top = pl.ds(levels, 1)
-    weight = pltpu.make_async_copy(polar.at[top], results[3].at[top], done.at[3, groups])
-    weight.start()
+    by_tracer = len(polar.shape) == 4
+    if by_tracer:
+        polar[:, groups, 0, :] = jnp.broadcast_to(east, (tracers, cells))
+    else:
+        polar[levels] = jnp.broadcast_to(east, (tracers, cells))
+
+    def polar_copy(g):
+        if by_tracer:
+            source, target = [x.at[:, g] for x in (polar, results[3])]
+        else:
+            at = pl.ds(g * GROUP, GROUP if not isinstance(g, int) else 1)
+            source, target = [x.at[at] for x in (polar, results[3])]
+        return pltpu.make_async_copy(source, target, done.at[3, g])
+
+    polar_copy(groups).start()
     lane = lax.broadcasted_iota(jnp.int32, (tracers, LANES), 1)
 
     def group(i, solved):
@@ -295,19 +315,25 @@
             solved = fresh
             first[level] = solved[0]
             last[level] = solved[rows - 1]
-            polar[level] = own * jnp.where(
-                at_start, solved[0], solved[rows - 1]
-            ) + side * jnp.where(at_start, solved[1], solved[rows - 2])
+            row = own * jnp.where(at_start, solved[0], solved[rows - 1]) + side * jnp.where(
+                at_start, solved[1], solved[rows - 2]
+            )
+            if by_tracer:
+                polar[:, at, j, :] = row
+            else:
+                polar[level] = row
         column[at] = west
-        for k, (field, result) in enumerate(zip(fields, results)):
-            chunk(field, result, done.at[k], at).start()
+        for k in range(3):
+            chunk(fields[k], results[k], done.at[k], at).start()
+        polar_copy(at).start()
         return solved
 
     lax.fori_loop(0, groups, group, [jnp.zeros((tracers, cells), F32)] * rows)
-    weight.wait()
-    for k, (field, result) in enumerate(zip(fields, results)):
-        for g in range(groups):
-            chunk(field, result, done.at[k], g).wait()
+    polar_copy(groups).wait()
+    for g in range(groups):
+        for k in range(3):
+            chunk(fields[k], results[k], done.at[k], g).wait()
+        polar_copy(jnp.int32(g)).wait()
 
 
 def forward_sweep(levels, rows, tracers, cells, diffusion, right_of):
@@ -401,27 +427,79 @@
     column,
     north,
     south,
-    nearby,
+    after_in,
+    before_in,
+    polar_in,
+    nearby_in,
+    edge,
+    turned_out,
     after,
     before,
-    polar_in,
-    turned_out,
-    edge,
     polar,
+    nearby,
     turned,
     ready,
 ):
-    groups, tracers, lanes = column.shape
     rows, cells = north.shape[1:]
-    fetch = pltpu.make_async_copy(polar_in, polar, ready.at[0])
+    fetches = [
+        pltpu.make_async_copy(source, target, ready.at[2 + k])
+        for k, (source, target) in enumerate(((polar_in, polar), (nearby_in, nearby)))
+    ]
+    sending = pltpu.make_async_copy(turned, turned_out, ready.at[4])
     lat = lax.axis_index("lat")
     last_lat = lax.axis_size("lat") - 1
     at_pole = (lat == 0) | (lat == last_lat)
 
     @pl.when(at_pole)
     def _():
-        fetch.start()
-
+        for fetch in fetches:
+            fetch.start()
+
+    finish = west_column(step, column, north, south, after_in, before_in, edge, after, before, ready)
+
+    @pl.when(at_pole)
+    def _():
+        for fetch in fetches:
+            fetch.wait()
+        levels = turned.shape[0]
+        circle = cells * lax.axis_size("lon")
+        amount = jnp.where(lat == 0, shift[step, 0], shift[step, rows * last_lat + rows - 1])
+        back = 2 * cells - (lax.rem(amount + 2 * circle, circle) & (cells - 1))
+        weight = jnp.concatenate([polar[levels], nearby[levels]], axis=1)
+
+        def one(i, carry):
+            for j in range(GROUP):
+                level = i * GROUP + j
+                row = jnp.concatenate([polar[level], nearby[level]], axis=1)
+                moved = row + weight * (pltpu.roll(row, 2 * cells - 1, 1) - row)
+                turned[level] = pltpu.roll(moved, back, 1)[:, :cells]
+            return carry
+
+        lax.fori_loop(0, levels // GROUP, one, 0)
+        sending.start()
+
+    finish()
+
+    @pl.when(at_pole)
+    def _():
+        sending.wait()
+
+
+def edge_kernel(
+    step, column, north, south, after_in, before_in, edge, after, before, ready
+):
+    west_column(step, column, north, south, after_in, before_in, edge, after, before, ready)()
+
+
+def west_column(step, column, north, south, after_in, before_in, edge, after, before, ready):
+    groups, tracers, lanes = column.shape
+    rows, cells = north.shape[1:]
+    tiles = [
+        pltpu.make_async_copy(source.at[:, :, pl.ds(0, lanes)], target, ready.at[k])
+        for k, (source, target) in enumerate(((after_in, after), (before_in, before)))
+    ]
+    for tile in tiles:
+        tile.start()
     lane = lax.broadcasted_iota(jnp.int32, (tracers, lanes), 1)
 
     def along_lanes(x):
@@ -442,40 +520,57 @@
         for j in range(GROUP):
             level = i * GROUP + j
             bottom, top = j * rows, j * rows + rows - 1
-            up = jnp.where(lane == top, pltpu.roll(after[level, :, :LANES], top, 1), up)
-            moved = before[level, :, :LANES]
+            up = jnp.where(lane == top, pltpu.roll(after[level], top, 1), up)
+            moved = before[level]
             moved = pltpu.roll(moved, bottom, 1) if bottom else moved
             down = jnp.where(lane == bottom, moved, down)
         edge[i] = own * here + n * up + s * down
         return carry
 
-    sending = pltpu.make_async_copy(turned, turned_out, ready.at[1])
-
-    @pl.when(at_pole)
+    def finish():
+        for tile in tiles:
+            tile.wait()
+        lax.fori_loop(0, groups, group, 0)
+
+    return finish
+
+
+def rotate_kernel(step, shift, circle_in, out, circle, moved, turned, ready):
+    parts, groups, group, cells = turned.shape
+    lat = lax.axis_index("lat")
+    last_lat = lax.axis_size("lat") - 1
+    rows = shift.shape[1] // lax.axis_size("lat")
+
+    @pl.when((lat == 0) | (lat == last_lat))
     def _():
+        fetch = pltpu.make_async_copy(circle_in, circle, ready.at[0])
+        fetch.start()
+        amount = jnp.where(lat == 0, shift[step, 0], shift[step, rows * last_lat + rows - 1])
+        amount = lax.rem(amount + 2 * parts * cells, parts * cells)
+        hops = amount // cells
+        inner = amount - hops * cells
+        shape = (group, cells)
+        lane = lax.broadcasted_iota(jnp.int32, shape, 1)
+        back = lax.rem(cells - inner, cells)
         fetch.wait()
-        levels = turned.shape[0]
-        circle = cells * lax.axis_size("lon")
-        amount = jnp.where(lat == 0, shift[step, 0], shift[step, rows * last_lat + rows - 1])
-        back = 2 * cells - (lax.rem(amount + 2 * circle, circle) & (cells - 1))
-        weight = jnp.concatenate([polar[levels], nearby[levels]], axis=1)
-
-        def one(i, carry):
-            for j in range(GROUP):
-                level = i * GROUP + j
-                row = jnp.concatenate([polar[level], nearby[level]], axis=1)
-                moved = row + weight * (pltpu.roll(row, 2 * cells - 1, 1) - row)
-                turned[level] = pltpu.roll(moved, back, 1)[:, :cells]
-            return carry
-
-        lax.fori_loop(0, groups, one, 0)
-        sending.start()
-
-    lax.fori_loop(0, groups, group, 0)
-
-    @pl.when(at_pole)
-    def _():
-        sending.wait()
+        for part in range(parts):
+            weight = jnp.broadcast_to(circle[part, groups, 0:1, :], shape)
+            for g in range(groups):
+                here = circle[part, g]
+                following = jnp.where(
+                    lane == cells - 1,
+                    pltpu.roll(circle[(part + 1) % parts, g], cells - 1, 1),
+                    pltpu.roll(here, cells - 1, 1),
+                )
+                moved[part, g] = pltpu.roll(here + weight * (following - here), back, 1)
+        for part in range(parts):
+            low = lax.rem(part + hops, parts)
+            high = lax.rem(part + hops + 1, parts)
+            for g in range(groups):
+                turned[part, g] = jnp.where(lane < cells - inner, moved[low, g], moved[high, g])
+        send = pltpu.make_async_copy(turned, out, ready.at[1])
+        send.start()
+        send.wait()
 
 
 def prepare_stencil(step, north, south, east, coefs):
@@ -490,7 +585,8 @@
         coefs[3, r] = jnp.broadcast_to(east[step, r : r + 1, :], (tracers, cells))
 
 
-def transported(level, lane_at, diffused, after, before, edge_row, coefs, pole):
+def transported(group, lane_at, diffused, after, before, edge_row, coefs, pole):
+    level = group * GROUP + lane_at
     rows, tracers, cells = diffused.shape[1:]
     lat = lax.axis_index("lat")
     last = lax.broadcasted_iota(jnp.int32, (tracers, cells), 1) == cells - 1
@@ -501,28 +597,33 @@
         arrived = jnp.concatenate([arrived] * (cells // LANES), axis=1)
         following = jnp.where(last, arrived, pltpu.roll(mer, cells - 1, 1))
         result.append(mer + coefs[3, r] * (following - mer))
-    polar = pole[level]
+    polar = pole[:, group, lane_at, :] if len(pole.shape) == 4 else pole[level]
     result[0] = jnp.where(lat == 0, polar, result[0])
     result[rows - 1] = jnp.where(lat == lax.axis_size("lat") - 1, polar, result[rows - 1])
     return result
 
 
-def streams(sources, south_pole, north_pole, targets, pole, done):
+def streams(sources, targets, poles, pole, done):
     lat = lax.axis_index("lat")
     last_lat = lax.axis_size("lat") - 1
     last = len(sources)
-    groups = pole.shape[0] // GROUP
-    for g in range(groups):
+
+    def polar_copy(source, g):
+        if len(pole.shape) == 4:
+            return pltpu.make_async_copy(source.at[:, g], pole.at[:, g], done.at[last, g])
+        return chunk(source, pole, done.at[last], g)
+
+    for g in range(targets[0].shape[0] // GROUP):
         for k, (source, target) in enumerate(zip(sources, targets)):
             chunk(source, target, done.at[k], g).start()
 
         @pl.when(lat == 0)
         def _():
-            chunk(south_pole, pole, done.at[last], g).start()
+            polar_copy(poles[0], g).start()
 
         @pl.when(lat == last_lat)
         def _():
-            chunk(north_pole, pole, done.at[last], g).start()
+            polar_copy(poles[-1], g).start()
 
     def wait(g):
         for k, (source, target) in enumerate(zip(sources, targets)):
@@ -530,7 +631,7 @@
 
         @pl.when((lat == 0) | (lat == last_lat))
         def _():
-            chunk(south_pole, pole, done.at[last], g).wait()
+            polar_copy(poles[0], g).wait()
 
     return wait
 
@@ -571,9 +672,8 @@
     levels, rows, tracers, cells = diffused.shape
     wait = streams(
         (before_step, forcing_in, after_in, before_in),
-        south_pole,
-        north_pole,
         (diffused, forced, after, before),
+        (south_pole, north_pole),
         pole,
         arrived,
     )
@@ -583,7 +683,7 @@
         if j == 0:
             wait(g)
         level = g * GROUP + j
-        rights = transported(level, j, diffused, after, before, edge[g], coefs, pole)
+        rights = transported(g, j, diffused, after, before, edge[g], coefs, pole)
         rights = [rights[r] + forced[level, r] for r in range(rows)]
         if final:
             for r in range(rows):
@@ -610,8 +710,7 @@
     forcing_in,
     after_in,
     before_in,
-    south_pole,
-    north_pole,
+    pole_in,
     edge,
     north,
     south,
@@ -632,9 +731,8 @@
     levels, rows, tracers, cells = diffused.shape
     wait = streams(
         (before_step, forcing_in, after_in, before_in),
-        south_pole,
-        north_pole,
         (diffused, forced, after, before),
+        (pole_in,),
         pole,
         arrived,
     )
@@ -645,7 +743,7 @@
         edge_row = edge[g]
         for j in range(GROUP):
             level = g * GROUP + j
-            values = transported(level, j, diffused, after, before, edge_row, coefs, pole)
+            values = transported(g, j, diffused, after, before, edge_row, coefs, pole)
             for r in range(rows):
                 staged[level, :, r, :] = values[r] + forced[level, r]
         chunk(staged, state, sent, g).start()
@@ -657,12 +755,10 @@
     wait_all(staged, state, sent)
 
 
-def boundaries(first, last, polar):
-    lat_count = lax.axis_size("lat")
-    up = [(i, i + 1) for i in range(lat_count - 1)]
+def boundary_rows(first, last):
+    up = [(i, i + 1) for i in range(lax.axis_size("lat") - 1)]
     down = [(j, i) for i, j in up]
-    nearby = lax.ppermute(polar, AXES, circles((0, lat_count - 1), 1))
-    return lax.ppermute(first, "lat", down), lax.ppermute(last, "lat", up), nearby
+    return lax.ppermute(first, "lat", down), lax.ppermute(last, "lat", up)
 
 
 def circles(lats, hops):
@@ -675,42 +771,81 @@
     ]
 
 
-def exchange(after, before, nearby, polar, column, north, south, shift, step):
-    lat_count = lax.axis_size("lat")
-    lon_count = lax.axis_size("lon")
-    poles = (0, lat_count - 1)
+def westward(edge):
+    count = lax.axis_size("lon")
+    return held(lax.ppermute(edge, "lon", [(i, (i - 1) % count) for i in range(count)]))
+
+
+def first_exchange(step, after, before, nearby, polar, column, north, south, shift, hops):
+    poles = (0, lax.axis_size("lat") - 1)
     levels, tracers, cells = after.shape
-    turned, edge = pl.pallas_call(
+    edge, turned = pl.pallas_call(
         functools.partial(borders_kernel, step),
-        out_shape=[pltpu.HBM((levels, tracers, cells), F32), resident(*column.shape)],
-        in_specs=[smem()] + [vmem()] * 6 + [hbm()],
-        out_specs=[hbm(), vmem()],
+        out_shape=[resident(*column.shape), pltpu.HBM((levels, tracers, cells), F32)],
+        in_specs=[smem()] + [vmem()] * 3 + [anywhere()] * 4,
+        out_specs=[vmem(), hbm()],
         scratch_shapes=[
+            pltpu.VMEM((levels, tracers, LANES), F32),
+            pltpu.VMEM((levels, tracers, LANES), F32),
+            pltpu.VMEM(polar.shape, F32),
             pltpu.VMEM(polar.shape, F32),
             pltpu.VMEM((levels, tracers, cells), F32),
-            pltpu.SemaphoreType.DMA((2,)),
+            pltpu.SemaphoreType.DMA((5,)),
         ],
-        compiler_params=params(4),
+        compiler_params=params(6),
         name="borders",
-    )(shift, column, north, south, *[held(x) for x in (nearby, after, before)], pinned(polar))
-    west = [(i, (i - 1) % lon_count) for i in range(lon_count)]
-    edge = lax.ppermute(edge, "lon", west)
+    )(shift, column, north, south, after, before, pinned(polar), nearby)
+    edge = westward(edge)
     moved = []
-    for lat, row in zip(poles, (0, shift.shape[1] - 1)):
-        hops = jnp.mod(shift[step, row], cells * lon_count) // cells
+    for lat, hop in zip(poles, hops):
         moved.append(
             lax.switch(
-                hops,
+                hop,
                 [
                     functools.partial(
                         lambda k, lat, x: lax.ppermute(x, AXES, circles((lat,), k)), k, lat
                     )
-                    for k in range(lon_count)
+                    for k in range(lax.axis_size("lon"))
                 ],
                 turned,
             )
         )
-    return pinned(after), pinned(before), pinned(moved[0]), pinned(moved[1]), held(edge)
+    return after, before, pinned(moved[0]), pinned(moved[1]), edge
+
+
+def last_exchange(step, after, before, circle, column, north, south, shift):
+    levels, tracers, cells = after.shape
+    parts, groups, group = circle.shape[:3]
+    shape = (parts, groups - 1, group, cells)
+    turned = pl.pallas_call(
+        functools.partial(rotate_kernel, step),
+        out_shape=pltpu.HBM(shape, F32),
+        in_specs=[smem(), anywhere()],
+        out_specs=hbm(),
+        scratch_shapes=[
+            pltpu.VMEM(circle.shape, F32),
+            pltpu.VMEM(shape, F32),
+            pltpu.VMEM(shape, F32),
+            pltpu.SemaphoreType.DMA((2,)),
+        ],
+        compiler_params=params(6),
+        name="rotate",
+    )(shift, circle)
+    pole = lax.all_to_all(turned, "lon", 0, 0, tiled=True)
+    edge = pl.pallas_call(
+        functools.partial(edge_kernel, step),
+        out_shape=resident(*column.shape),
+        in_specs=[vmem()] * 3 + [anywhere()] * 2,
+        out_specs=vmem(),
+        scratch_shapes=[
+            pltpu.VMEM((levels, tracers, LANES), F32),
+            pltpu.VMEM((levels, tracers, LANES), F32),
+            pltpu.SemaphoreType.DMA((2,)),
+        ],
+        compiler_params=params(4),
+        name="edge",
+    )(column, north, south, after, before)
+    return after, before, pole, westward(edge)
 
 
 def per_device(
@@ -768,28 +903,47 @@
     couplings = [held(x) for x in couplings]
     diffusion = held(diffusion)
     counts, column = lax.optimization_barrier((sounding_counts, column))
-    around = boundaries(first, last, polar)
+    lat_count, lon_count = lax.axis_size("lat"), lax.axis_size("lon")
+    ends = jnp.stack([polar_shift[1, 0], polar_shift[1, -1]])
+    hops = (ends & (cells * lon_count - 1)) >> (cells.bit_length() - 1)
+    nearby = lax.ppermute(polar, AXES, circles((0, lat_count - 1), 1))
+    around = (*boundary_rows(first, last), nearby)
     sent = packed(counts, owner_rows, columns, kernels, misfits)
     sent, *around = lax.optimization_barrier((sent, *around))
+    around = [pinned(x) for x in around]
     got = lax.all_to_all(sent, AXES, 0, 0, tiled=True)
     forced = pinned(forcing(1, got, levels, tracers, rows, cells))
-    around = exchange(*around, polar, column, *couplings[:2], polar_shift, 1)
-    scratch = [field, field, line, line, line]
+    around = first_exchange(1, *around, polar, column, *couplings[:2], polar_shift, hops)
+    scratch = [field, field, line, line]
     transfers = pltpu.SemaphoreType.DMA((5, groups))
     solved, first, last, polar, column, surface = pl.pallas_call(
         functools.partial(middle_kernel, 1),
-        out_shape=solved_shapes + [resident(rows, tracers, cells)],
-        in_specs=[hbm()] * 6 + [vmem()] * 5,
+        out_shape=[
+            *solved_shapes[:3],
+            pltpu.HBM((tracers, groups + 1, GROUP, cells), F32),
+            solved_shapes[4],
+            resident(rows, tracers, cells),
+        ],
+        in_specs=[hbm()] * 2 + [anywhere()] * 2 + [hbm()] * 2 + [vmem()] * 5,
         out_specs=solved_specs + [vmem()],
-        scratch_shapes=[coefs, ratios, *scratch, *solved_scratch, transfers, leaving],
+        scratch_shapes=[
+            coefs,
+            ratios,
+            *scratch,
+            line,
+            *solved_scratch[:3],
+            pltpu.VMEM((tracers, groups + 1, GROUP, cells), F32),
+            transfers,
+            leaving,
+        ],
         compiler_params=params(26),
         name="middle",
     )(pinned(diffused), forced, *around, diffusion, *couplings)
-    around = boundaries(first, last, polar)
+    around = (*boundary_rows(first, last), lax.all_to_all(polar, "lon", 0, 0, tiled=True))
     got, column = lax.optimization_barrier((got, column))
     forced = pinned(forcing(0, got, levels, tracers, rows, cells))
     forced, *around = lax.optimization_barrier((forced, *around))
-    around = exchange(*around, polar, column, *couplings[:2], polar_shift, 0)
+    around = last_exchange(0, *around, column, *couplings[:2], polar_shift)
     return tuple(
         pl.pallas_call(
             functools.partial(last_kernel, 0),
@@ -797,9 +951,16 @@
                 pltpu.HBM(costate.shape, F32),
                 jax.ShapeDtypeStruct((tracers, rows, cells), F32),
             ],
-            in_specs=[hbm()] * 6 + [vmem()] * 5,
+            in_specs=[hbm()] * 2 + [anywhere()] * 3 + [vmem()] * 5,
             out_specs=[hbm(), vmem()],
-            scratch_shapes=[coefs, *scratch, output, transfers, semaphores],
+            scratch_shapes=[
+                coefs,
+                *scratch,
+                pltpu.VMEM((tracers, groups, GROUP, cells), F32),
+                output,
+                transfers,
+                semaphores,
+            ],
             compiler_params=params(22),
             name="last",
         )(pinned(solved), pinned(forced), *around, *couplings, surface)

time: 144 us -> 140 us (0.972)
  between operations: 9.09 us -> 2.31 us
  starting transfers between devices: 41.1 us -> 45.6 us
  local copies, waits for them, and re-layouts: 6.43 us -> 2.2 us
  Pallas kernels: 60.1 us -> 63.8 us
  waiting for transfers between devices: 26.9 us -> 24.9 us
    all_to_all x0 -> x2, starting transfers between devices: none -> 8.9 us  [the longest x1 5.36 us: last_exchange(): pole = lax.all_to_all(turned, 'lon', 0, 0, tiled=True)]
    unnamed x36 -> x26, local copies, waits for them, and re-layouts: 5.69 us -> 0.88 us
    ppermute x12 -> x9, starting transfers between devices: 32.4 us -> 28.2 us  [the longest x4 9.52 us: boundary_rows(): return (lax.ppermute(first, 'lat', down), lax.ppermute(last, 'lat', up))]
    pallas_call x3 -> x4, Pallas kernels: 16.1 us -> 19.7 us  [the longest x1 8.12 us: per_device(): pl.pallas_call(functools.partial(middle_kernel, 1), out_shape=[*solved_sh...]
    ppermute x12 -> x9, waiting for transfers between devices: 26.9 us -> 24 us  [the longest x2 19.1 us: first_exchange(): lax.ppermute(x, AXES, circles((lat,), k))]
  transfers between devices with their start and end apart: 13 -> 12, of which waited for: 3 -> 4; matrix products, arithmetic and copies ran while one was open for 1% -> 2% of each run, Pallas kernels for 23% -> 25%
where the time goes in v1:
time: 140 us
  Pallas kernels  63.8 us (46%)
  starting transfers between devices  45.6 us (33%)
  waiting for transfers between devices  24.9 us (18%)
  between operations  2.31 us (2%)
  local copies, waits for them, and re-layouts  2.2 us (2%)
    pallas_call x2, Pallas kernels, forcing(): pl.pallas_call(functools.partial(forcing_kernel, step), out_shape=pltpu.H...  22.4 us
    ppermute x2, waiting for transfers between devices, first_exchange(): lax.ppermute(x, AXES, circles((lat,), k))  19.1 us
    ppermute x4, starting transfers between devices, boundary_rows(): return (lax.ppermute(first, 'lat', down), lax.ppermute(last, 'lat', up))  9.52 us
    all_to_all x1, starting transfers between devices, per_device(): got = lax.all_to_all(sent, AXES, 0, 0, tiled=True)  8.52 us
    pallas_call x1, Pallas kernels, per_device(): pl.pallas_call(functools.partial(middle_kernel, 1), out_shape=[*solved_sh...  8.12 us
    ppermute x2, starting transfers between devices, westward(): lax.ppermute(edge, 'lon', [(i, (i - 1) % count) for i in range(count)])  8.07 us
    pallas_call x1, Pallas kernels, per_device(): pl.pallas_call(functools.partial(first_kernel, 1), out_shape=solved_shape...  7.92 us
    pallas_call x1, Pallas kernels, per_device(): pl.pallas_call(functools.partial(last_kernel, 0), out_shape=[pltpu.HBM(co...  7.41 us
  transfers between devices with their start and end apart: 12, of which 4 were waited for; matrix products, arithmetic and copies ran while one was open for 2% of the time, Pallas kernels for 25%

profile of v1, /device:TPU:0, one launch (start us, length us, event | category | flops | bytes accessed | tf_op | source)
XLA Modules:
  0.0 140.2 jit_solution(9303770095896487858)
XLA Ops:
  0.7 7.9 %first.1 = (f32[72,8,8,256]{3,2,1,0:T(8,128)}, f32[72,8,256]{2,1,0:T(8,128)}, f32[72,8,256]{2,1,0:T(8,128)}, f32[73,8,256]{2,1,0:T(8,128)}, f32[9,8,128]{2,1,0:T(8,128)S(1)}) custom-call(f32[72,8,8,256]{3,2,1,0:T(8,128)} %costate.1, f32[2,71,8,256]{3,2,1,0:T(8,128)} %diffusion.1, f32[2,8,256]{2,1,0:T(8,128)} %north.7, f32[2,8,256]{2,1,0:T(8,128)} %south.7, ...), custom_call_target="tpu_custom_call" | custom-call | tf_op jit(solution)/shard_map/first/pallas_call | solution.py:885
  8.6 7.2 %collective-permute-start.18 = (f32[73,8,256]{2,1,0:T(8,128)}, f32[73,8,256]{2,1,0:T(8,128)S(1)}, u32[]{:S(2)}, u32[]{:S(2)}) collective-permute-start(f32[73,8,256]{2,1,0:T(8,128)} %get-tuple-element.66.polar_in), channel_id=1, source_target_pairs={{16,0},{32,16},{48,32},{64,48},{80,64},{96,80},{112,96},{0,112},{3... | collective-permute-start | bytes 1794056 | tf_op jit(solution)/shard_map/ppermute | solution.py:909
  15.8 1.3 collective-permute-start.16
  17.1 3.1 %collective-permute-start.17 = (f32[72,8,256]{2,1,0:T(8,128)}, f32[72,8,256]{2,1,0:T(8,128)S(1)}, u32[]{:S(2)}, u32[]{:S(2)}) collective-permute-start(f32[72,8,256]{2,1,0:T(8,128)} %get-tuple-element.65), channel_id=1, source_target_pairs={{0,1},{1,2},{2,3},{3,4},{4,5},{5,6},{6,7},{7,8},{8,9},{9,10},{10,1... | collective-permute-start | bytes 1769480 | tf_op jit(solution)/shard_map/ppermute | solution.py:761
  20.2 0.1 copy.13.counts
  20.3 6.4 %pack.1 = f32[128,32,128]{2,1,0:T(8,128)} custom-call(s32[2,1]{1,0:T(2,128)S(1)} %copy.13.counts, s32[2,1,1280]{2,1,0:T(1,128)S(1)} %bitcast.5, s32[2,1280]{1,0:T(2,128)S(1)} %copy-done.7, f32[2,72,1280]{2,1,0:T(8,128)S(1)} %copy-done.1, f32[2,8,1280]{2,1,0:T(8,128)S(1)} %copy-done.5), custom_call_target="tpu_custom_call" | custom-call | tf_op jit(solution)/shard_map/pack/pallas_call | solution.py:150
  26.7 3.2 %collective-permute-done.18.nearby_in = f32[73,8,256]{2,1,0:T(8,128)S(1)} collective-permute-done((f32[73,8,256]{2,1,0:T(8,128)}, f32[73,8,256]{2,1,0:T(8,128)S(1)}, u32[]{:S(2)}, u32[]{:S(2)}) %collective-permute-start.18) | collective-permute-done | bytes 598048 | tf_op jit(solution)/shard_map/ppermute | solution.py:909
  29.9 0.8 copy-done.11
  30.8 8.5 %all-to-all-start = ((f32[128,32,128]{2,1,0:T(8,128)}), f32[128,32,128]{2,1,0:T(8,128)S(1)}, u32[]{:S(2)}, u32[]{:S(2)}) async-start(f32[128,32,128]{2,1,0:T(8,128)} %pack.1), calls=%async_computation | async-start | bytes 4194304 | tf_op jit(solution)/shard_map/all_to_all | solution.py:914
  39.3 0.6 fusion.1
  40.0 1.4 fusion
  41.4 4.3 %borders.1 = (f32[9,8,128]{2,1,0:T(8,128)S(1)}, f32[72,8,256]{2,1,0:T(8,128)}) custom-call(s32[2,128]{1,0:T(2,128)S(1)} %copy-done.8, f32[9,8,128]{2,1,0:T(8,128)S(1)} %get-tuple-element.70.column, f32[2,8,256]{2,1,0:T(8,128)S(1)} %copy-done.2, f32[2,8,256]{2,1,0:T(8,128)S(1)} %copy-done.3, f32[72,8,256]{2,1,0:T(8,128)} %copy-done.9, ...), custom_call_target="tpu_custom_call" | custom-call | tf_op jit(solution)/shard_map/borders/pallas_call | solution.py:782
  45.7 3.9 %collective-permute-start.19 = (f32[9,8,128]{2,1,0:T(8,128)S(1)}, f32[9,8,128]{2,1,0:T(8,128)S(1)}, u32[]{:S(2)}, u32[]{:S(2)}) collective-permute-start(f32[9,8,128]{2,1,0:T(8,128)S(1)} %get-tuple-element.73), channel_id=1, source_target_pairs={{0,112},{16,0},{32,16},{48,32},{64,48},{80,64},{96,80},{112,96},{1... | collective-permute-start | bytes 110600 | tf_op jit(solution)/shard_map/ppermute | solution.py:776
  49.5 0.6 fusion.2
  51.3 1.5 %conditional.3 = (f32[72,8,256]{2,1,0:T(8,128)}) conditional(s32[]{:T(128)} %bitcast.4, f32[72,8,256]{2,1,0:T(8,128)} %get-tuple-element.72, f32[72,8,256]{2,1,0:T(8,128)} %get-tuple-element.72, f32[72,8,256]{2,1,0:T(8,128)} %get-tuple-element.72, f32[72,8,256]{2,1,0:T(8,128)} %get-tuple-element.72, ...), branch_computations={%region_8.0_spmd, %region_9.0_spmd, %region_10.0_spmd, %region_11.... | conditional | bytes 2359344 | solution.py:802
  51.3 1.5 %collective-permute-start.12 = (f32[72,8,256]{2,1,0:T(8,128)}, f32[72,8,256]{2,1,0:T(8,128)}, u32[]{:S(2)}, u32[]{:S(2)}) collective-permute-start(f32[72,8,256]{2,1,0:T(8,128)} %param.12), channel_id=1, source_target_pairs={{79,15},{95,31},{111,47},{127,63},{15,79},{31,95},{47,111},{63,127}} | collective-permute-start | bytes 1769480 | tf_op jit(solution)/shard_map/cond/branch_4_fun/ppermute | solution.py:806
  52.8 21.0 %conditional.2 = (f32[72,8,256]{2,1,0:T(8,128)}) conditional(s32[]{:T(128)} %bitcast.3, f32[72,8,256]{2,1,0:T(8,128)} %get-tuple-element.72, f32[72,8,256]{2,1,0:T(8,128)} %get-tuple-element.72, f32[72,8,256]{2,1,0:T(8,128)} %get-tuple-element.72, f32[72,8,256]{2,1,0:T(8,128)} %get-tuple-element.72, ...), branch_computations={%region_0.0_spmd, %region_1.0_spmd, %region_2.0_spmd, %region_3.0_... | conditional | bytes 2359344 | solution.py:802
  52.8 1.9 %collective-permute-start.6 = (f32[72,8,256]{2,1,0:T(8,128)}, f32[72,8,256]{2,1,0:T(8,128)}, u32[]{:S(2)}, u32[]{:S(2)}) collective-permute-start(f32[72,8,256]{2,1,0:T(8,128)} %param.6), channel_id=1, source_target_pairs={{96,0},{112,16},{0,32},{16,48},{32,64},{48,80},{64,96},{80,112}} | collective-permute-start | bytes 1769480 | tf_op jit(solution)/shard_map/cond/branch_6_fun/ppermute | solution.py:806
  54.8 19.1 %collective-permute-done.6 = f32[72,8,256]{2,1,0:T(8,128)} collective-permute-done((f32[72,8,256]{2,1,0:T(8,128)}, f32[72,8,256]{2,1,0:T(8,128)}, u32[]{:S(2)}, u32[]{:S(2)}) %collective-permute-start.6) | collective-permute-done | bytes 589856 | tf_op jit(solution)/shard_map/cond/branch_6_fun/ppermute | solution.py:806
  73.9 11.1 %forcing.2.forcing_in = f32[72,8,8,256]{3,2,1,0:T(8,128)} custom-call(f32[128,32,128]{2,1,0:T(8,128)S(1)} %all-to-all-done.received), custom_call_target="tpu_custom_call" | custom-call | tf_op jit(solution)/shard_map/forcing/pallas_call | solution.py:233
  85.0 8.1 %middle.1 = (f32[72,8,8,256]{3,2,1,0:T(8,128)}, f32[72,8,256]{2,1,0:T(8,128)}, f32[72,8,256]{2,1,0:T(8,128)}, f32[8,10,8,256]{3,2,1,0:T(8,128)}, f32[9,8,128]{2,1,0:T(8,128)S(1)}, /*index=5*/f32[8,8,256]{2,1,0:T(8,128)S(1)}) custom-call(f32[72,8,8,256]{3,2,1,0:T(8,128)} %get-tuple-element.61.before_step, f32[72,8,8,256]{3,2,1,0:T(8,128)} %forcing.2.forcing_in, ...), custom_call_target="tpu_custom_call" | custom-call | tf_op jit(solution)/shard_map/middle/pallas_call | solution.py:919
  93.1 1.3 collective-permute-start.20
  94.4 3.9 %collective-permute-start.21 = (f32[72,8,256]{2,1,0:T(8,128)}, f32[72,8,256]{2,1,0:T(8,128)}, u32[]{:S(2)}, u32[]{:S(2)}) collective-permute-start(f32[72,8,256]{2,1,0:T(8,128)} %get-tuple-element.78), channel_id=1, source_target_pairs={{0,1},{1,2},{2,3},{3,4},{4,5},{5,6},{6,7},{7,8},{8,9},{9,10},{10,1... | collective-permute-start | bytes 1769480 | tf_op jit(solution)/shard_map/ppermute | solution.py:761
  98.3 3.5 %all-to-all-start.1 = ((f32[8,10,8,256]{3,2,1,0:T(8,128)}), f32[8,10,8,256]{3,2,1,0:T(8,128)S(1)}, u32[]{:S(2)}, u32[]{:S(2)}) async-start(f32[8,10,8,256]{3,2,1,0:T(8,128)} %get-tuple-element.79), calls=%async_computation.1 | async-start | bytes 1310720 | tf_op jit(solution)/shard_map/all_to_all | solution.py:942
  101.9 11.3 %forcing.3.forcing_in = f32[72,8,8,256]{3,2,1,0:T(8,128)} custom-call(f32[128,32,128]{2,1,0:T(8,128)S(1)} %all-to-all-done.received), custom_call_target="tpu_custom_call" | custom-call | tf_op jit(solution)/shard_map/forcing/pallas_call | solution.py:233
  113.2 5.5 %rotate.1 = f32[8,9,8,256]{3,2,1,0:T(8,128)} custom-call(s32[2,128]{1,0:T(2,128)S(1)} %copy-done.8, f32[8,10,8,256]{3,2,1,0:T(8,128)S(1)} %all-to-all-done.1.circle_in), custom_call_target="tpu_custom_call" | custom-call | tf_op jit(solution)/shard_map/rotate/pallas_call | solution.py:820
  118.7 5.4 %all-to-all-start.2 = ((f32[8,9,8,256]{3,2,1,0:T(8,128)}), f32[8,9,8,256]{3,2,1,0:T(8,128)S(1)}, u32[]{:S(2)}, u32[]{:S(2)}) async-start(f32[8,9,8,256]{3,2,1,0:T(8,128)} %rotate.1), calls=%async_computation.2 | async-start | bytes 1179648 | tf_op jit(solution)/shard_map/all_to_all | solution.py:834
  124.1 1.8 %edge.1 = f32[9,8,128]{2,1,0:T(8,128)S(1)} custom-call(f32[9,8,128]{2,1,0:T(8,128)S(1)} %get-tuple-element.84.column, f32[2,8,256]{2,1,0:T(8,128)S(1)} %copy-done.2, f32[2,8,256]{2,1,0:T(8,128)S(1)} %copy-done.3, f32[72,8,256]{2,1,0:T(8,128)S(1)} %collective-permute-done.20.after_in, f32[72,8,256]{2,1,0:T(8,128)} %collective-permute-done.21.before_in), custom_call_target="tpu_custom_call" | custom-call | tf_op jit(solution)/shard_map/edge/pallas_call | solution.py:835
  125.9 4.2 %collective-permute-start.22 = (f32[9,8,128]{2,1,0:T(8,128)S(1)}, f32[9,8,128]{2,1,0:T(8,128)S(1)}, u32[]{:S(2)}, u32[]{:S(2)}) collective-permute-start(f32[9,8,128]{2,1,0:T(8,128)S(1)} %edge.1), channel_id=1, source_target_pairs={{0,112},{16,0},{32,16},{48,32},{64,48},{80,64},{96,80},{112,96},{1... | collective-permute-start | bytes 110600 | tf_op jit(solution)/shard_map/ppermute | solution.py:776
  130.1 1.6 %collective-permute-done.22.edge = f32[9,8,128]{2,1,0:T(8,128)S(1)} collective-permute-done((f32[9,8,128]{2,1,0:T(8,128)S(1)}, f32[9,8,128]{2,1,0:T(8,128)S(1)}, u32[]{:S(2)}, u32[]{:S(2)}) %collective-permute-start.22) | collective-permute-done | bytes 36896 | tf_op jit(solution)/shard_map/ppermute | solution.py:776
  131.7 0.9 all-to-all-done.2.pole_in
  132.6 7.4 %last.1 = (f32[72,8,8,256]{3,2,1,0:T(8,128)}, f32[8,8,256]{2,1,0:T(8,128)}) custom-call(f32[72,8,8,256]{3,2,1,0:T(8,128)} %get-tuple-element.74.before_step, f32[72,8,8,256]{3,2,1,0:T(8,128)} %forcing.3.forcing_in, f32[72,8,256]{2,1,0:T(8,128)S(1)} %collective-permute-done.20.after_in, f32[72,8,256]{2,1,0:T(8,128)} %collective-permute-done.21.before_in, ...), custom_call_target="tpu_custom_call" | custom-call | tf_op jit(solution)/shard_map/last/pallas_call | solution.py:948
  (33 shorter events, 0.1 us)
Async XLA Ops:
  0.6 19.6 %copy-start.12 = (s32[2,1]{0,1:T(1,128)S(1)}, s32[2,1]{0,1:T(1,128)}, u32[]{:S(2)}) copy-start(s32[2,1]{0,1:T(1,128)} %param.35) | copy-start | bytes 28
  0.6 19.7 %copy-start.5 = (f32[2,8,1280]{2,1,0:T(8,128)S(1)}, f32[2,8,1280]{2,1,0:T(8,128)}, u32[]{:S(2)}) copy-start(f32[2,8,1280]{2,1,0:T(8,128)} %misfits.1) | copy-start | bytes 245764
  0.7 19.7 %copy-start.1 = (f32[2,72,1280]{2,1,0:T(8,128)S(1)}, f32[2,72,1280]{2,1,0:T(8,128)}, u32[]{:S(2)}) copy-start(f32[2,72,1280]{2,1,0:T(8,128)} %kernels.1) | copy-start | bytes 2211844
  0.7 19.6 %copy-start.7 = (s32[2,1280]{1,0:T(2,128)S(1)}, s32[2,1280]{1,0:T(2,128)}, u32[]{:S(2)}) copy-start(s32[2,1280]{1,0:T(2,128)} %columns.1) | copy-start | bytes 30724
  0.7 19.6 %copy-start.6 = (s32[2,1280,1]{1,2,0:T(1,128)S(1)}, s32[2,1280,1]{1,2,0:T(1,128)}, u32[]{:S(2)}) copy-start(s32[2,1280,1]{1,2,0:T(1,128)} %param.33) | copy-start | bytes 30724
  8.6 30.7 %copy-start.8 = (s32[2,128]{1,0:T(2,128)S(1)}, s32[2,128]{1,0:T(2,128)}, u32[]{:S(2)}) copy-start(s32[2,128]{1,0:T(2,128)} %shift.3) | copy-start | bytes 3076
  8.6 32.7 %copy-start.2 = (f32[2,8,256]{2,1,0:T(8,128)S(1)}, f32[2,8,256]{2,1,0:T(8,128)}, u32[]{:S(2)}) copy-start(f32[2,8,256]{2,1,0:T(8,128)} %north.7) | copy-start | bytes 49156
  8.6 32.7 %copy-start.3 = (f32[2,8,256]{2,1,0:T(8,128)S(1)}, f32[2,8,256]{2,1,0:T(8,128)}, u32[]{:S(2)}) copy-start(f32[2,8,256]{2,1,0:T(8,128)} %south.7) | copy-start | bytes 49156
  8.6 21.3 %collective-permute-start.18 = (f32[73,8,256]{2,1,0:T(8,128)}, f32[73,8,256]{2,1,0:T(8,128)S(1)}, u32[]{:S(2)}, u32[]{:S(2)}) collective-permute-start(f32[73,8,256]{2,1,0:T(8,128)} %get-tuple-element.66.polar_in), channel_id=1, source_target_pairs={{16,0},{32,16},{48,32},{64,48},{80,64},{96,80},{112,96},{0,112},{3... | collective-permute-start | bytes 1794056 | tf_op jit(solution)/shard_map/ppermute | solution.py:909
  15.8 10.9 %collective-permute-start.16 = (f32[72,8,256]{2,1,0:T(8,128)}, f32[72,8,256]{2,1,0:T(8,128)S(1)}, u32[]{:S(2)}, u32[]{:S(2)}) collective-permute-start(f32[72,8,256]{2,1,0:T(8,128)} %get-tuple-element.64), channel_id=1, source_target_pairs={{1,0},{2,1},{3,2},{4,3},{5,4},{6,5},{7,6},{8,7},{9,8},{10,9},{11,1... | collective-permute-start | bytes 1769480 | tf_op jit(solution)/shard_map/ppermute | solution.py:761
  17.1 9.6 %collective-permute-start.17 = (f32[72,8,256]{2,1,0:T(8,128)}, f32[72,8,256]{2,1,0:T(8,128)S(1)}, u32[]{:S(2)}, u32[]{:S(2)}) collective-permute-start(f32[72,8,256]{2,1,0:T(8,128)} %get-tuple-element.65), channel_id=1, source_target_pairs={{0,1},{1,2},{2,3},{3,4},{4,5},{5,6},{6,7},{7,8},{8,9},{9,10},{10,1... | collective-permute-start | bytes 1769480 | tf_op jit(solution)/shard_map/ppermute | solution.py:761
  26.7 3.2 %copy-start.9 = (f32[72,8,256]{2,1,0:T(8,128)}, f32[72,8,256]{2,1,0:T(8,128)S(1)}, u32[]{:S(2)}) copy-start(f32[72,8,256]{2,1,0:T(8,128)S(1)} %collective-permute-done.16.after_in) | copy-start | bytes 1769476
  26.7 3.2 %copy-start.10 = (f32[72,8,256]{2,1,0:T(8,128)}, f32[72,8,256]{2,1,0:T(8,128)S(1)}, u32[]{:S(2)}) copy-start(f32[72,8,256]{2,1,0:T(8,128)S(1)} %collective-permute-done.17.before_in) | copy-start | bytes 1769476
  29.9 0.8 copy-start.11
  30.8 43.1 %all-to-all-start = ((f32[128,32,128]{2,1,0:T(8,128)}), f32[128,32,128]{2,1,0:T(8,128)S(1)}, u32[]{:S(2)}, u32[]{:S(2)}) async-start(f32[128,32,128]{2,1,0:T(8,128)} %pack.1), calls=%async_computation | async-start | bytes 4194304 | tf_op jit(solution)/shard_map/all_to_all | solution.py:914
  39.3 45.7 %copy-start = (f32[2,71,8,256]{3,2,1,0:T(8,128)S(1)}, f32[2,71,8,256]{3,2,1,0:T(8,128)}, u32[]{:S(2)}) copy-start(f32[2,71,8,256]{3,2,1,0:T(8,128)} %diffusion.1) | copy-start | bytes 3489796
  39.3 45.7 %copy-start.4 = (f32[2,8,256]{2,1,0:T(8,128)S(1)}, f32[2,8,256]{2,1,0:T(8,128)}, u32[]{:S(2)}) copy-start(f32[2,8,256]{2,1,0:T(8,128)} %east.3) | copy-start | bytes 49156
  45.7 39.3 %collective-permute-start.19 = (f32[9,8,128]{2,1,0:T(8,128)S(1)}, f32[9,8,128]{2,1,0:T(8,128)S(1)}, u32[]{:S(2)}, u32[]{:S(2)}) collective-permute-start(f32[9,8,128]{2,1,0:T(8,128)S(1)} %get-tuple-element.73), channel_id=1, source_target_pairs={{0,112},{16,0},{32,16},{48,32},{64,48},{80,64},{96,80},{112,96},{1... | collective-permute-start | bytes 110600 | tf_op jit(solution)/shard_map/ppermute | solution.py:776
  51.3 1.5 %collective-permute-start.12 = (f32[72,8,256]{2,1,0:T(8,128)}, f32[72,8,256]{2,1,0:T(8,128)}, u32[]{:S(2)}, u32[]{:S(2)}) collective-permute-start(f32[72,8,256]{2,1,0:T(8,128)} %param.12), channel_id=1, source_target_pairs={{79,15},{95,31},{111,47},{127,63},{15,79},{31,95},{47,111},{63,127}} | collective-permute-start | bytes 1769480 | tf_op jit(solution)/shard_map/cond/branch_4_fun/ppermute | solution.py:806
  52.8 21.0 %collective-permute-start.6 = (f32[72,8,256]{2,1,0:T(8,128)}, f32[72,8,256]{2,1,0:T(8,128)}, u32[]{:S(2)}, u32[]{:S(2)}) collective-permute-start(f32[72,8,256]{2,1,0:T(8,128)} %param.6), channel_id=1, source_target_pairs={{96,0},{112,16},{0,32},{16,48},{32,64},{48,80},{64,96},{80,112}} | collective-permute-start | bytes 1769480 | tf_op jit(solution)/shard_map/cond/branch_6_fun/ppermute | solution.py:806
  93.1 20.0 %collective-permute-start.20 = (f32[72,8,256]{2,1,0:T(8,128)}, f32[72,8,256]{2,1,0:T(8,128)S(1)}, u32[]{:S(2)}, u32[]{:S(2)}) collective-permute-start(f32[72,8,256]{2,1,0:T(8,128)} %get-tuple-element.77), channel_id=1, source_target_pairs={{1,0},{2,1},{3,2},{4,3},{5,4},{6,5},{7,6},{8,7},{9,8},{10,9},{11,1... | collective-permute-start | bytes 1769480 | tf_op jit(solution)/shard_map/ppermute | solution.py:761
  94.4 18.7 %collective-permute-start.21 = (f32[72,8,256]{2,1,0:T(8,128)}, f32[72,8,256]{2,1,0:T(8,128)}, u32[]{:S(2)}, u32[]{:S(2)}) collective-permute-start(f32[72,8,256]{2,1,0:T(8,128)} %get-tuple-element.78), channel_id=1, source_target_pairs={{0,1},{1,2},{2,3},{3,4},{4,5},{5,6},{6,7},{7,8},{8,9},{9,10},{10,1... | collective-permute-start | bytes 1769480 | tf_op jit(solution)/shard_map/ppermute | solution.py:761
  98.3 14.8 %all-to-all-start.1 = ((f32[8,10,8,256]{3,2,1,0:T(8,128)}), f32[8,10,8,256]{3,2,1,0:T(8,128)S(1)}, u32[]{:S(2)}, u32[]{:S(2)}) async-start(f32[8,10,8,256]{3,2,1,0:T(8,128)} %get-tuple-element.79), calls=%async_computation.1 | async-start | bytes 1310720 | tf_op jit(solution)/shard_map/all_to_all | solution.py:942
  118.7 13.9 %all-to-all-start.2 = ((f32[8,9,8,256]{3,2,1,0:T(8,128)}), f32[8,9,8,256]{3,2,1,0:T(8,128)S(1)}, u32[]{:S(2)}, u32[]{:S(2)}) async-start(f32[8,9,8,256]{3,2,1,0:T(8,128)} %rotate.1), calls=%async_computation.2 | async-start | bytes 1179648 | tf_op jit(solution)/shard_map/all_to_all | solution.py:834
  125.9 5.8 %collective-permute-start.22 = (f32[9,8,128]{2,1,0:T(8,128)S(1)}, f32[9,8,128]{2,1,0:T(8,128)S(1)}, u32[]{:S(2)}, u32[]{:S(2)}) collective-permute-start(f32[9,8,128]{2,1,0:T(8,128)S(1)} %edge.1), channel_id=1, source_target_pairs={{0,112},{16,0},{32,16},{48,32},{64,48},{80,64},{96,80},{112,96},{1... | collective-permute-start | bytes 110600 | tf_op jit(solution)/shard_map/ppermute | solution.py:776

commit v2 on v1

--- a/solution.py
+++ b/solution.py
@@ -163,21 +163,36 @@
     )(counts, held(owners), held(columns), held(kernels), held(misfits))
 
 
-def forcing_kernel(step, received, result, out, fields, hots, place, ordered, done):
+def streamed_forcing_kernel(step, received, result, out, *scratch):
+    done = scratch[-1]
+
+    def copy(r):
+        return pltpu.make_async_copy(out.at[:, r], result.at[:, r], done.at[r])
+
+    forcing_kernel(step, received, out, *scratch[:-1], finished=lambda r: copy(r).start())
+    for r in range(out.shape[1]):
+        copy(r).wait()
+
+
+def forcing_kernel(
+    step, received, out, fields, hots, place, ordered, finished=lambda r: None
+):
     levels, rows, tracers, cells = out.shape
-    slots = received.shape[0] * CAP
+    sources = received.shape[0]
+    slots = sources * CAP
     blocks = slots // LANES
-    sources = LANES // CAP
+    at_column = levels + tracers
+    data = received[:, step * CAP : (step + 1) * CAP, :].reshape(slots, LANES)
+    high, low = halves(data)
+    fields[:, :LANES] = high
+    fields[:, LANES:] = low
+    shape = (8, 2 * LANES)
+    pick = (lax.broadcasted_iota(jnp.int32, shape, 1) & (LANES - 1)) == at_column
+    column = dot(jnp.where(pick, 1.0, 0.0).astype(BF16), fields[...], ((1,), (1,)))
+    cell_row = (column.astype(jnp.int32) - 1) >> (cells.bit_length() - 1)
     sub = lax.broadcasted_iota(jnp.int32, (rows, LANES), 0)
-    at_column = levels + tracers
     for b in range(blocks):
-        span = slice(b * LANES, (b + 1) * LANES)
-        block = received[b * sources : (b + 1) * sources, step * CAP : (step + 1) * CAP, :]
-        turned = block.reshape(LANES, LANES).T
-        high, low = halves(turned)
-        fields[:LANES, span] = high
-        fields[LANES:, span] = low
-        row = (turned[at_column : at_column + 1].astype(jnp.int32) - 1) >> 8
+        row = cell_row[:, b * LANES : (b + 1) * LANES]
         hots[b * rows : (b + 1) * rows, :] = jnp.where(sub == row, 1.0, 0.0)
     counted = dot(hots[...].astype(BF16), counting_table())
     run = jnp.zeros((rows, LANES), F32)
@@ -201,51 +216,69 @@
 
     def sort(i, carry):
         hot = one_hot(place[...] - (i * wide).astype(F32), wide)
-        both = dot(fields[...], hot, ((1,), (1,)))
-        ordered[:, pl.ds(pl.multiple_of(i * wide, wide), wide)] = both[:LANES] + both[LANES:]
+        both = dot(hot, fields[...])
+        ordered[pl.ds(pl.multiple_of(i * wide, wide), wide), :] = both[:, :LANES] + both[:, LANES:]
         return carry
 
     lax.fori_loop(0, (used + 1) // 2, sort, 0)
     out[...] = jnp.zeros_like(out)
-    cell = lax.broadcasted_iota(jnp.int32, (cells, LANES), 0)
+    name = lax.broadcasted_iota(jnp.int32, (LANES, cells), 1).astype(F32)
     first = jnp.int32(0)
     for r in range(rows):
-        names = (cell + (r * cells + 1)).astype(F32)
 
         def add(p, carry):
-            block = ordered[:, pl.ds(pl.multiple_of(p * LANES, LANES), LANES)]
-            hot = jnp.where(names == block[at_column : at_column + 1], 1.0, 0.0).astype(BF16)
-            product = block[:levels][:, None, :] * block[levels:at_column][None]
-            high, low = halves(product.reshape(levels * tracers, LANES))
-            total = dot(high, hot, ((1,), (1,))) + dot(low, hot, ((1,), (1,)))
+            block = ordered[pl.ds(pl.multiple_of(p * LANES, LANES), LANES), :]
+            own = jnp.broadcast_to(
+                block[:, at_column : at_column + 1] - (r * cells + 1.0), (LANES, cells)
+            )
+            hot = jnp.where(name == own, 1.0, 0.0).astype(BF16)
+            turned = block.T
+            product = turned[:levels][:, None, :] * turned[levels:at_column][None]
+            first_half, second_half = halves(product.reshape(levels * tracers, LANES))
+            total = dot(first_half, hot) + dot(second_half, hot)
             out[:, r, :, :] += total.reshape(levels, tracers, cells)
             return carry
 
         lax.fori_loop(first, first + counts[r], add, 0)
         first = first + counts[r]
-        pltpu.make_async_copy(out.at[:, r], result.at[:, r], done.at[r]).start()
-    for r in range(rows):
-        pltpu.make_async_copy(out.at[:, r], result.at[:, r], done.at[r]).wait()
-
-
-def forcing(step, received, levels, tracers, rows, cells):
+        finished(r)
+
+
+def forcing(step, received, shape, streamed):
     slots = received.shape[0] * CAP
+    scratch = [
+        pltpu.VMEM((slots, 2 * LANES), BF16),
+        pltpu.VMEM((slots // LANES * shape[1], LANES), F32),
+        pltpu.VMEM((1, slots), F32),
+        pltpu.VMEM((slots + shape[1] * LANES, LANES), F32),
+    ]
+    if streamed:
+        scratch = [resident(*shape), *scratch, pltpu.SemaphoreType.DMA((shape[1],))]
     return pl.pallas_call(
-        functools.partial(forcing_kernel, step),
-        out_shape=pltpu.HBM((levels, rows, tracers, cells), F32),
+        functools.partial(streamed_forcing_kernel if streamed else forcing_kernel, step),
+        out_shape=pltpu.HBM(shape, F32) if streamed else resident(*shape),
         in_specs=[vmem()],
-        out_specs=hbm(),
-        scratch_shapes=[
-            pltpu.VMEM((levels, rows, tracers, cells), F32),
-            pltpu.VMEM((2 * LANES, slots), BF16),
-            pltpu.VMEM((slots // LANES * rows, LANES), F32),
-            pltpu.VMEM((1, slots), F32),
-            pltpu.VMEM((LANES, slots + rows * LANES), F32),
-            pltpu.SemaphoreType.DMA((rows,)),
-        ],
-        compiler_params=params(14),
+        out_specs=hbm() if streamed else vmem(),
+        scratch_shapes=scratch,
+        compiler_params=params(16 if streamed else 12),
         name="forcing",
     )(held(received))
+
+
+def shift_matrix(inner, cells):
+    shape = (2 * cells, cells)
+    source = lax.broadcasted_iota(jnp.int32, shape, 0)
+    target = lax.broadcasted_iota(jnp.int32, shape, 1) + inner
+    picks = [jnp.where(source == target + k, 1.0, 0.0).astype(BF16) for k in range(2)]
+    return jnp.concatenate(picks, axis=1)
+
+
+def shifted(low, high, matrix):
+    row = jnp.concatenate([low, high], axis=1)
+    first, rest = row.astype(BF16), None
+    rest = row - first.astype(F32)
+    second, third = halves(rest)
+    return dot(first, matrix) + dot(second, matrix) + dot(third, matrix)
 
 
 def spread(x, row, tracers):
@@ -464,18 +497,16 @@
         levels = turned.shape[0]
         circle = cells * lax.axis_size("lon")
         amount = jnp.where(lat == 0, shift[step, 0], shift[step, rows * last_lat + rows - 1])
-        back = 2 * cells - (lax.rem(amount + 2 * circle, circle) & (cells - 1))
-        weight = jnp.concatenate([polar[levels], nearby[levels]], axis=1)
-
-        def one(i, carry):
-            for j in range(GROUP):
-                level = i * GROUP + j
-                row = jnp.concatenate([polar[level], nearby[level]], axis=1)
-                moved = row + weight * (pltpu.roll(row, 2 * cells - 1, 1) - row)
-                turned[level] = pltpu.roll(moved, back, 1)[:, :cells]
-            return carry
-
-        lax.fori_loop(0, levels // GROUP, one, 0)
+        matrix = shift_matrix(lax.rem(amount + 2 * circle, circle) & (cells - 1), cells)
+        tracers = turned.shape[1]
+        weight = shifted(polar[levels], nearby[levels], matrix)[:1, :cells]
+        size = 3 * GROUP
+        for i in range(levels // size):
+            at = slice(i * size, (i + 1) * size)
+            low, high = [x[at].reshape(size * tracers, cells) for x in (polar, nearby)]
+            row = shifted(low, high, matrix)
+            row = row[:, :cells] + weight * (row[:, cells:] - row[:, :cells])
+            turned[at] = row.reshape(size, tracers, cells)
         sending.start()
 
     finish()
@@ -535,7 +566,7 @@
     return finish
 
 
-def rotate_kernel(step, shift, circle_in, out, circle, moved, turned, ready):
+def rotate_kernel(step, shift, circle_in, out, circle, turned, ready):
     parts, groups, group, cells = turned.shape
     lat = lax.axis_index("lat")
     last_lat = lax.axis_size("lat") - 1
@@ -548,26 +579,20 @@
         amount = jnp.where(lat == 0, shift[step, 0], shift[step, rows * last_lat + rows - 1])
         amount = lax.rem(amount + 2 * parts * cells, parts * cells)
         hops = amount // cells
-        inner = amount - hops * cells
-        shape = (group, cells)
-        lane = lax.broadcasted_iota(jnp.int32, shape, 1)
-        back = lax.rem(cells - inner, cells)
+        matrix = shift_matrix(amount - hops * cells, cells)
         fetch.wait()
         for part in range(parts):
-            weight = jnp.broadcast_to(circle[part, groups, 0:1, :], shape)
-            for g in range(groups):
-                here = circle[part, g]
-                following = jnp.where(
-                    lane == cells - 1,
-                    pltpu.roll(circle[(part + 1) % parts, g], cells - 1, 1),
-                    pltpu.roll(here, cells - 1, 1),
-                )
-                moved[part, g] = pltpu.roll(here + weight * (following - here), back, 1)
-        for part in range(parts):
-            low = lax.rem(part + hops, parts)
-            high = lax.rem(part + hops + 1, parts)
-            for g in range(groups):
-                turned[part, g] = jnp.where(lane < cells - inner, moved[low, g], moved[high, g])
+            near = lax.rem(part + hops, parts)
+            far = lax.rem(part + hops + 1, parts)
+            low, high = [
+                circle[x].reshape((groups + 1) * group, cells) for x in (near, far)
+            ]
+            row = shifted(low, high, matrix)
+            size = groups * group
+            weight = row[size : size + 1, :cells]
+            row = row[:size]
+            row = row[:, :cells] + weight * (row[:, cells:] - row[:, :cells])
+            turned[part] = row.reshape(groups, group, cells)
         send = pltpu.make_async_copy(turned, out, ready.at[1])
         send.start()
         send.wait()
@@ -639,7 +664,7 @@
 def middle_kernel(
     step,
     before_step,
-    forcing_in,
+    forced,
     after_in,
     before_in,
     south_pole,
@@ -658,7 +683,6 @@
     coefs,
     ratios,
     diffused,
-    forced,
     after,
     before,
     pole,
@@ -671,8 +695,8 @@
 ):
     levels, rows, tracers, cells = diffused.shape
     wait = streams(
-        (before_step, forcing_in, after_in, before_in),
-        (diffused, forced, after, before),
+        (before_step, after_in, before_in),
+        (diffused, after, before),
         (south_pole, north_pole),
         pole,
         arrived,
@@ -792,7 +816,7 @@
             pltpu.VMEM((levels, tracers, cells), F32),
             pltpu.SemaphoreType.DMA((5,)),
         ],
-        compiler_params=params(6),
+        compiler_params=params(8),
         name="borders",
     )(shift, column, north, south, after, before, pinned(polar), nearby)
     edge = westward(edge)
@@ -825,10 +849,9 @@
         scratch_shapes=[
             pltpu.VMEM(circle.shape, F32),
             pltpu.VMEM(shape, F32),
-            pltpu.VMEM(shape, F32),
             pltpu.SemaphoreType.DMA((2,)),
         ],
-        compiler_params=params(6),
+        compiler_params=params(8),
         name="rotate",
     )(shift, circle)
     pole = lax.all_to_all(turned, "lon", 0, 0, tiled=True)
@@ -912,10 +935,11 @@
     sent, *around = lax.optimization_barrier((sent, *around))
     around = [pinned(x) for x in around]
     got = lax.all_to_all(sent, AXES, 0, 0, tiled=True)
-    forced = pinned(forcing(1, got, levels, tracers, rows, cells))
+    shape = (levels, rows, tracers, cells)
+    forced = forcing(1, got, shape, False)
     around = first_exchange(1, *around, polar, column, *couplings[:2], polar_shift, hops)
-    scratch = [field, field, line, line]
-    transfers = pltpu.SemaphoreType.DMA((5, groups))
+    scratch = [field, line, line]
+    transfers = pltpu.SemaphoreType.DMA((4, groups))
     solved, first, last, polar, column, surface = pl.pallas_call(
         functools.partial(middle_kernel, 1),
         out_shape=[
@@ -924,7 +948,7 @@
             solved_shapes[4],
             resident(rows, tracers, cells),
         ],
-        in_specs=[hbm()] * 2 + [anywhere()] * 2 + [hbm()] * 2 + [vmem()] * 5,
+        in_specs=[hbm(), vmem()] + [anywhere()] * 2 + [hbm()] * 2 + [vmem()] * 5,
         out_specs=solved_specs + [vmem()],
         scratch_shapes=[
             coefs,
@@ -936,12 +960,12 @@
             transfers,
             leaving,
         ],
-        compiler_params=params(26),
+        compiler_params=params(20),
         name="middle",
     )(pinned(diffused), forced, *around, diffusion, *couplings)
     around = (*boundary_rows(first, last), lax.all_to_all(polar, "lon", 0, 0, tiled=True))
     got, column = lax.optimization_barrier((got, column))
-    forced = pinned(forcing(0, got, levels, tracers, rows, cells))
+    forced = forcing(0, got, shape, True)
     forced, *around = lax.optimization_barrier((forced, *around))
     around = last_exchange(0, *around, column, *couplings[:2], polar_shift)
     return tuple(
@@ -955,10 +979,11 @@
             out_specs=[hbm(), vmem()],
             scratch_shapes=[
                 coefs,
+                field,
                 *scratch,
                 pltpu.VMEM((tracers, groups, GROUP, cells), F32),
                 output,
-                transfers,
+                pltpu.SemaphoreType.DMA((5, groups)),
                 semaphores,
             ],
             compiler_params=params(22),

time: 140 us -> 137 us (0.979)
  Pallas kernels: 63.8 us -> 54.7 us
  starting transfers between devices: 45.6 us -> 49.2 us
  waiting for transfers between devices: 24.9 us -> 26.4 us
    pallas_call x2, Pallas kernels: 22.4 us -> 15.8 us  [forcing(): pl.pallas_call(functools.partial(streamed_forcing_kernel if streamed else...]
    all_to_all x1, waiting for transfers between devices: 0.01 us -> 5.2 us  [per_device(): lax.all_to_all(polar, 'lon', 0, 0, tiled=True)]
    ppermute x2, waiting for transfers between devices: 19.1 us -> 15.5 us  [first_exchange(): lax.ppermute(x, AXES, circles((lat,), k))]
    all_to_all x1, starting transfers between devices: 3.54 us -> 5.65 us  [per_device(): lax.all_to_all(polar, 'lon', 0, 0, tiled=True)]
    ppermute x4, starting transfers between devices: 9.52 us -> 11.6 us  [boundary_rows(): return (lax.ppermute(first, 'lat', down), lax.ppermute(last, 'lat', up))]
    pallas_call x1, Pallas kernels: 5.54 us -> 4.09 us  [last_exchange(): pl.pallas_call(functools.partial(rotate_kernel, step), out_shape=pltpu.HB...]
  transfers between devices with their start and end apart: 12 -> 12, of which waited for: 4 -> 5; matrix products, arithmetic and copies ran while one was open for 2% -> 2% of each run, Pallas kernels for 25% -> 20%
where the time goes in v2:
time: 137 us; the launch traced here: 136 us
  Pallas kernels  54.7 us (40%)
  starting transfers between devices  49.2 us (36%)
  waiting for transfers between devices  26.4 us (19%)
  between operations  2.27 us (2%)
  local copies, waits for them, and re-layouts  2.2 us (2%)
  other arithmetic  1.39 us (1%)
    pallas_call x2, Pallas kernels, forcing(): pl.pallas_call(functools.partial(streamed_forcing_kernel if streamed else...  15.8 us
    ppermute x2, waiting for transfers between devices, first_exchange(): lax.ppermute(x, AXES, circles((lat,), k))  15.5 us
    ppermute x4, starting transfers between devices, boundary_rows(): return (lax.ppermute(first, 'lat', down), lax.ppermute(last, 'lat', up))  11.6 us
    all_to_all x1, starting transfers between devices, per_device(): got = lax.all_to_all(sent, AXES, 0, 0, tiled=True)  8.52 us
    ppermute x2, starting transfers between devices, westward(): lax.ppermute(edge, 'lon', [(i, (i - 1) % count) for i in range(count)])  8.07 us
    pallas_call x1, Pallas kernels, per_device(): pl.pallas_call(functools.partial(first_kernel, 1), out_shape=solved_shape...  7.92 us
    pallas_call x1, Pallas kernels, per_device(): pl.pallas_call(functools.partial(middle_kernel, 1), out_shape=[*solved_sh...  7.42 us
    pallas_call x1, Pallas kernels, per_device(): pl.pallas_call(functools.partial(last_kernel, 0), out_shape=[pltpu.HBM(co...  7.41 us
  transfers between devices with their start and end apart: 12, of which 5 were waited for; matrix products, arithmetic and copies ran while one was open for 2% of the time, Pallas kernels for 20%

profile of v2, /device:TPU:0, one launch (start us, length us, event | category | flops | bytes accessed | tf_op | source)
XLA Modules:
  0.0 136.2 jit_solution(1122936617970538956)
XLA Ops:
  0.7 7.9 %first.1 = (f32[72,8,8,256]{3,2,1,0:T(8,128)}, f32[72,8,256]{2,1,0:T(8,128)}, f32[72,8,256]{2,1,0:T(8,128)}, f32[73,8,256]{2,1,0:T(8,128)}, f32[9,8,128]{2,1,0:T(8,128)S(1)}) custom-call(f32[72,8,8,256]{3,2,1,0:T(8,128)} %costate.1, f32[2,71,8,256]{3,2,1,0:T(8,128)} %diffusion.1, f32[2,8,256]{2,1,0:T(8,128)} %north.7, f32[2,8,256]{2,1,0:T(8,128)} %south.7, ...), custom_call_target="tpu_custom_call" | custom-call | tf_op jit(solution)/shard_map/first/pallas_call | solution.py:908
  8.6 7.2 %collective-permute-start.18 = (f32[73,8,256]{2,1,0:T(8,128)}, f32[73,8,256]{2,1,0:T(8,128)S(1)}, u32[]{:S(2)}, u32[]{:S(2)}) collective-permute-start(f32[73,8,256]{2,1,0:T(8,128)} %get-tuple-element.66.polar_in), channel_id=1, source_target_pairs={{16,0},{32,16},{48,32},{64,48},{80,64},{96,80},{112,96},{0,112},{3... | collective-permute-start | bytes 1794056 | tf_op jit(solution)/shard_map/ppermute | solution.py:932
  15.8 1.3 collective-permute-start.16
  17.1 3.1 %collective-permute-start.17 = (f32[72,8,256]{2,1,0:T(8,128)}, f32[72,8,256]{2,1,0:T(8,128)S(1)}, u32[]{:S(2)}, u32[]{:S(2)}) collective-permute-start(f32[72,8,256]{2,1,0:T(8,128)} %get-tuple-element.65), channel_id=1, source_target_pairs={{0,1},{1,2},{2,3},{3,4},{4,5},{5,6},{6,7},{7,8},{8,9},{9,10},{10,1... | collective-permute-start | bytes 1769480 | tf_op jit(solution)/shard_map/ppermute | solution.py:785
  20.3 6.4 %pack.1 = f32[128,32,128]{2,1,0:T(8,128)} custom-call(s32[2,1]{1,0:T(2,128)S(1)} %copy.13.counts, s32[2,1,1280]{2,1,0:T(1,128)S(1)} %bitcast.5, s32[2,1280]{1,0:T(2,128)S(1)} %copy-done.7, f32[2,72,1280]{2,1,0:T(8,128)S(1)} %copy-done.1, f32[2,8,1280]{2,1,0:T(8,128)S(1)} %copy-done.5), custom_call_target="tpu_custom_call" | custom-call | tf_op jit(solution)/shard_map/pack/pallas_call | solution.py:150
  26.7 3.2 %collective-permute-done.18.nearby_in = f32[73,8,256]{2,1,0:T(8,128)S(1)} collective-permute-done((f32[73,8,256]{2,1,0:T(8,128)}, f32[73,8,256]{2,1,0:T(8,128)S(1)}, u32[]{:S(2)}, u32[]{:S(2)}) %collective-permute-start.18) | collective-permute-done | bytes 598048 | tf_op jit(solution)/shard_map/ppermute | solution.py:932
  29.9 0.8 copy-done.11
  30.8 8.5 %all-to-all-start = ((f32[128,32,128]{2,1,0:T(8,128)}), f32[128,32,128]{2,1,0:T(8,128)S(1)}, u32[]{:S(2)}, u32[]{:S(2)}) async-start(f32[128,32,128]{2,1,0:T(8,128)} %pack.1), calls=%async_computation | async-start | bytes 4194304 | tf_op jit(solution)/shard_map/all_to_all | solution.py:937
  39.3 0.6 fusion.1
  40.0 1.4 %fusion = s32[2]{0:T(128)S(1)} fusion(s32[1]{0:T(128)} %bitcast.2, s32[1]{0:T(128)} %bitcast.1), kind=kLoop, calls=%fused_computation.1 | loop fusion | flops 6 | bytes 16 | tf_op jit(solution)/shard_map/shift_right_arithmetic | solution.py:931
  41.4 3.9 %borders.1 = (f32[9,8,128]{2,1,0:T(8,128)S(1)}, f32[72,8,256]{2,1,0:T(8,128)}) custom-call(s32[2,128]{1,0:T(2,128)S(1)} %copy-done.8, f32[9,8,128]{2,1,0:T(8,128)S(1)} %get-tuple-element.70.column, f32[2,8,256]{2,1,0:T(8,128)S(1)} %copy-done.2, f32[2,8,256]{2,1,0:T(8,128)S(1)} %copy-done.3, f32[72,8,256]{2,1,0:T(8,128)} %copy-done.9, ...), custom_call_target="tpu_custom_call" | custom-call | tf_op jit(solution)/shard_map/borders/pallas_call | solution.py:806
  45.2 3.9 %collective-permute-start.19 = (f32[9,8,128]{2,1,0:T(8,128)S(1)}, f32[9,8,128]{2,1,0:T(8,128)S(1)}, u32[]{:S(2)}, u32[]{:S(2)}) collective-permute-start(f32[9,8,128]{2,1,0:T(8,128)S(1)} %get-tuple-element.73), channel_id=1, source_target_pairs={{0,112},{16,0},{32,16},{48,32},{64,48},{80,64},{96,80},{112,96},{1... | collective-permute-start | bytes 110600 | tf_op jit(solution)/shard_map/ppermute | solution.py:800
  49.1 0.6 fusion.2
  50.9 1.5 %conditional.3 = (f32[72,8,256]{2,1,0:T(8,128)}) conditional(s32[]{:T(128)} %bitcast.4, f32[72,8,256]{2,1,0:T(8,128)} %get-tuple-element.72, f32[72,8,256]{2,1,0:T(8,128)} %get-tuple-element.72, f32[72,8,256]{2,1,0:T(8,128)} %get-tuple-element.72, f32[72,8,256]{2,1,0:T(8,128)} %get-tuple-element.72, ...), branch_computations={%region_8.0_spmd, %region_9.0_spmd, %region_10.0_spmd, %region_11.... | conditional | bytes 2359344 | solution.py:826
  50.9 1.5 %collective-permute-start.12 = (f32[72,8,256]{2,1,0:T(8,128)}, f32[72,8,256]{2,1,0:T(8,128)}, u32[]{:S(2)}, u32[]{:S(2)}) collective-permute-start(f32[72,8,256]{2,1,0:T(8,128)} %param.12), channel_id=1, source_target_pairs={{79,15},{95,31},{111,47},{127,63},{15,79},{31,95},{47,111},{63,127}} | collective-permute-start | bytes 1769480 | tf_op jit(solution)/shard_map/cond/branch_4_fun/ppermute | solution.py:830
  52.4 17.9 %conditional.2 = (f32[72,8,256]{2,1,0:T(8,128)}) conditional(s32[]{:T(128)} %bitcast.3, f32[72,8,256]{2,1,0:T(8,128)} %get-tuple-element.72, f32[72,8,256]{2,1,0:T(8,128)} %get-tuple-element.72, f32[72,8,256]{2,1,0:T(8,128)} %get-tuple-element.72, f32[72,8,256]{2,1,0:T(8,128)} %get-tuple-element.72, ...), branch_computations={%region_0.0_spmd, %region_1.0_spmd, %region_2.0_spmd, %region_3.0_... | conditional | bytes 2359344 | solution.py:826
  52.4 2.4 %collective-permute-start.4 = (f32[72,8,256]{2,1,0:T(8,128)}, f32[72,8,256]{2,1,0:T(8,128)}, u32[]{:S(2)}, u32[]{:S(2)}) collective-permute-start(f32[72,8,256]{2,1,0:T(8,128)} %param.4), channel_id=1, source_target_pairs={{64,0},{80,16},{96,32},{112,48},{0,64},{16,80},{32,96},{48,112}} | collective-permute-start | bytes 1769480 | tf_op jit(solution)/shard_map/cond/branch_4_fun/ppermute | solution.py:830
  54.8 15.5 %collective-permute-done.4 = f32[72,8,256]{2,1,0:T(8,128)} collective-permute-done((f32[72,8,256]{2,1,0:T(8,128)}, f32[72,8,256]{2,1,0:T(8,128)}, u32[]{:S(2)}, u32[]{:S(2)}) %collective-permute-start.4) | collective-permute-done | bytes 589856 | tf_op jit(solution)/shard_map/cond/branch_4_fun/ppermute | solution.py:830
  70.3 7.3 %forcing.2.forced = f32[72,8,8,256]{3,2,1,0:T(8,128)S(1)} custom-call(f32[128,32,128]{2,1,0:T(8,128)S(1)} %all-to-all-done.received), custom_call_target="tpu_custom_call" | custom-call | tf_op jit(solution)/shard_map/forcing/pallas_call | solution.py:257
  77.6 7.4 %middle.1 = (f32[72,8,8,256]{3,2,1,0:T(8,128)}, f32[72,8,256]{2,1,0:T(8,128)}, f32[72,8,256]{2,1,0:T(8,128)}, f32[8,10,8,256]{3,2,1,0:T(8,128)}, f32[9,8,128]{2,1,0:T(8,128)S(1)}, /*index=5*/f32[8,8,256]{2,1,0:T(8,128)S(1)}) custom-call(f32[72,8,8,256]{3,2,1,0:T(8,128)} %get-tuple-element.61.before_step, f32[72,8,8,256]{3,2,1,0:T(8,128)S(1)} %forcing.2.forced, ...), custom_call_target="tpu_custom_call" | custom-call | tf_op jit(solution)/shard_map/middle/pallas_call | solution.py:943
  85.1 1.3 collective-permute-start.20
  86.4 5.9 %collective-permute-start.21 = (f32[72,8,256]{2,1,0:T(8,128)}, f32[72,8,256]{2,1,0:T(8,128)}, u32[]{:S(2)}, u32[]{:S(2)}) collective-permute-start(f32[72,8,256]{2,1,0:T(8,128)} %get-tuple-element.78), channel_id=1, source_target_pairs={{0,1},{1,2},{2,3},{3,4},{4,5},{5,6},{6,7},{7,8},{8,9},{9,10},{10,1... | collective-permute-start | bytes 1769480 | tf_op jit(solution)/shard_map/ppermute | solution.py:785
  92.3 5.7 %all-to-all-start.1 = ((f32[8,10,8,256]{3,2,1,0:T(8,128)}), f32[8,10,8,256]{3,2,1,0:T(8,128)S(1)}, u32[]{:S(2)}, u32[]{:S(2)}) async-start(f32[8,10,8,256]{3,2,1,0:T(8,128)} %get-tuple-element.79), calls=%async_computation.1 | async-start | bytes 1310720 | tf_op jit(solution)/shard_map/all_to_all | solution.py:966
  97.9 8.5 %forcing.3.forcing_in = f32[72,8,8,256]{3,2,1,0:T(8,128)} custom-call(f32[128,32,128]{2,1,0:T(8,128)S(1)} %all-to-all-done.received), custom_call_target="tpu_custom_call" | custom-call | tf_op jit(solution)/shard_map/forcing/pallas_call | solution.py:257
  106.4 5.2 %all-to-all-done.1.circle_in = f32[8,10,8,256]{3,2,1,0:T(8,128)S(1)} async-done(((f32[8,10,8,256]{3,2,1,0:T(8,128)}), f32[8,10,8,256]{3,2,1,0:T(8,128)S(1)}, u32[]{:S(2)}, u32[]{:S(2)}) %all-to-all-start.1) | async-done | bytes 655392 | tf_op jit(solution)/shard_map/all_to_all | solution.py:966
  111.6 4.1 %rotate.1 = f32[8,9,8,256]{3,2,1,0:T(8,128)} custom-call(s32[2,128]{1,0:T(2,128)S(1)} %copy-done.8, f32[8,10,8,256]{3,2,1,0:T(8,128)S(1)} %all-to-all-done.1.circle_in), custom_call_target="tpu_custom_call" | custom-call | tf_op jit(solution)/shard_map/rotate/pallas_call | solution.py:844
  115.7 4.4 %all-to-all-start.2 = ((f32[8,9,8,256]{3,2,1,0:T(8,128)}), f32[8,9,8,256]{3,2,1,0:T(8,128)S(1)}, u32[]{:S(2)}, u32[]{:S(2)}) async-start(f32[8,9,8,256]{3,2,1,0:T(8,128)} %rotate.1), calls=%async_computation.2 | async-start | bytes 1179648 | tf_op jit(solution)/shard_map/all_to_all | solution.py:857
  120.1 1.8 %edge.1 = f32[9,8,128]{2,1,0:T(8,128)S(1)} custom-call(f32[9,8,128]{2,1,0:T(8,128)S(1)} %get-tuple-element.84.column, f32[2,8,256]{2,1,0:T(8,128)S(1)} %copy-done.2, f32[2,8,256]{2,1,0:T(8,128)S(1)} %copy-done.3, f32[72,8,256]{2,1,0:T(8,128)S(1)} %collective-permute-done.20.after_in, f32[72,8,256]{2,1,0:T(8,128)} %collective-permute-done.21.before_in), custom_call_target="tpu_custom_call" | custom-call | tf_op jit(solution)/shard_map/edge/pallas_call | solution.py:858
  121.9 4.2 %collective-permute-start.22 = (f32[9,8,128]{2,1,0:T(8,128)S(1)}, f32[9,8,128]{2,1,0:T(8,128)S(1)}, u32[]{:S(2)}, u32[]{:S(2)}) collective-permute-start(f32[9,8,128]{2,1,0:T(8,128)S(1)} %edge.1), channel_id=1, source_target_pairs={{0,112},{16,0},{32,16},{48,32},{64,48},{80,64},{96,80},{112,96},{1... | collective-permute-start | bytes 110600 | tf_op jit(solution)/shard_map/ppermute | solution.py:800
  126.1 1.6 %collective-permute-done.22.edge = f32[9,8,128]{2,1,0:T(8,128)S(1)} collective-permute-done((f32[9,8,128]{2,1,0:T(8,128)S(1)}, f32[9,8,128]{2,1,0:T(8,128)S(1)}, u32[]{:S(2)}, u32[]{:S(2)}) %collective-permute-start.22) | collective-permute-done | bytes 36896 | tf_op jit(solution)/shard_map/ppermute | solution.py:800
  127.7 0.9 all-to-all-done.2.pole_in
  128.6 7.4 %last.1 = (f32[72,8,8,256]{3,2,1,0:T(8,128)}, f32[8,8,256]{2,1,0:T(8,128)}) custom-call(f32[72,8,8,256]{3,2,1,0:T(8,128)} %get-tuple-element.74.before_step, f32[72,8,8,256]{3,2,1,0:T(8,128)} %forcing.3.forcing_in, f32[72,8,256]{2,1,0:T(8,128)S(1)} %collective-permute-done.20.after_in, f32[72,8,256]{2,1,0:T(8,128)} %collective-permute-done.21.before_in, ...), custom_call_target="tpu_custom_call" | custom-call | tf_op jit(solution)/shard_map/last/pallas_call | solution.py:972
  (33 shorter events, 0.2 us)
Async XLA Ops:
  0.6 19.6 %copy-start.12 = (s32[2,1]{0,1:T(1,128)S(1)}, s32[2,1]{0,1:T(1,128)}, u32[]{:S(2)}) copy-start(s32[2,1]{0,1:T(1,128)} %param.35) | copy-start | bytes 28
  0.6 19.7 %copy-start.5 = (f32[2,8,1280]{2,1,0:T(8,128)S(1)}, f32[2,8,1280]{2,1,0:T(8,128)}, u32[]{:S(2)}) copy-start(f32[2,8,1280]{2,1,0:T(8,128)} %misfits.1) | copy-start | bytes 245764
  0.7 19.7 %copy-start.1 = (f32[2,72,1280]{2,1,0:T(8,128)S(1)}, f32[2,72,1280]{2,1,0:T(8,128)}, u32[]{:S(2)}) copy-start(f32[2,72,1280]{2,1,0:T(8,128)} %kernels.1) | copy-start | bytes 2211844
  0.7 19.6 %copy-start.7 = (s32[2,1280]{1,0:T(2,128)S(1)}, s32[2,1280]{1,0:T(2,128)}, u32[]{:S(2)}) copy-start(s32[2,1280]{1,0:T(2,128)} %columns.1) | copy-start | bytes 30724
  0.7 19.6 %copy-start.6 = (s32[2,1280,1]{1,2,0:T(1,128)S(1)}, s32[2,1280,1]{1,2,0:T(1,128)}, u32[]{:S(2)}) copy-start(s32[2,1280,1]{1,2,0:T(1,128)} %param.33) | copy-start | bytes 30724
  8.6 30.7 %copy-start.8 = (s32[2,128]{1,0:T(2,128)S(1)}, s32[2,128]{1,0:T(2,128)}, u32[]{:S(2)}) copy-start(s32[2,128]{1,0:T(2,128)} %shift.3) | copy-start | bytes 3076
  8.6 32.7 %copy-start.2 = (f32[2,8,256]{2,1,0:T(8,128)S(1)}, f32[2,8,256]{2,1,0:T(8,128)}, u32[]{:S(2)}) copy-start(f32[2,8,256]{2,1,0:T(8,128)} %north.7) | copy-start | bytes 49156
  8.6 32.7 %copy-start.3 = (f32[2,8,256]{2,1,0:T(8,128)S(1)}, f32[2,8,256]{2,1,0:T(8,128)}, u32[]{:S(2)}) copy-start(f32[2,8,256]{2,1,0:T(8,128)} %south.7) | copy-start | bytes 49156
  8.6 21.3 %collective-permute-start.18 = (f32[73,8,256]{2,1,0:T(8,128)}, f32[73,8,256]{2,1,0:T(8,128)S(1)}, u32[]{:S(2)}, u32[]{:S(2)}) collective-permute-start(f32[73,8,256]{2,1,0:T(8,128)} %get-tuple-element.66.polar_in), channel_id=1, source_target_pairs={{16,0},{32,16},{48,32},{64,48},{80,64},{96,80},{112,96},{0,112},{3... | collective-permute-start | bytes 1794056 | tf_op jit(solution)/shard_map/ppermute | solution.py:932
  15.8 10.9 %collective-permute-start.16 = (f32[72,8,256]{2,1,0:T(8,128)}, f32[72,8,256]{2,1,0:T(8,128)S(1)}, u32[]{:S(2)}, u32[]{:S(2)}) collective-permute-start(f32[72,8,256]{2,1,0:T(8,128)} %get-tuple-element.64), channel_id=1, source_target_pairs={{1,0},{2,1},{3,2},{4,3},{5,4},{6,5},{7,6},{8,7},{9,8},{10,9},{11,1... | collective-permute-start | bytes 1769480 | tf_op jit(solution)/shard_map/ppermute | solution.py:785
  17.1 9.6 %collective-permute-start.17 = (f32[72,8,256]{2,1,0:T(8,128)}, f32[72,8,256]{2,1,0:T(8,128)S(1)}, u32[]{:S(2)}, u32[]{:S(2)}) collective-permute-start(f32[72,8,256]{2,1,0:T(8,128)} %get-tuple-element.65), channel_id=1, source_target_pairs={{0,1},{1,2},{2,3},{3,4},{4,5},{5,6},{6,7},{7,8},{8,9},{9,10},{10,1... | collective-permute-start | bytes 1769480 | tf_op jit(solution)/shard_map/ppermute | solution.py:785
  26.7 3.2 %copy-start.9 = (f32[72,8,256]{2,1,0:T(8,128)}, f32[72,8,256]{2,1,0:T(8,128)S(1)}, u32[]{:S(2)}) copy-start(f32[72,8,256]{2,1,0:T(8,128)S(1)} %collective-permute-done.16.after_in) | copy-start | bytes 1769476
  26.7 3.2 %copy-start.10 = (f32[72,8,256]{2,1,0:T(8,128)}, f32[72,8,256]{2,1,0:T(8,128)S(1)}, u32[]{:S(2)}) copy-start(f32[72,8,256]{2,1,0:T(8,128)S(1)} %collective-permute-done.17.before_in) | copy-start | bytes 1769476
  29.9 0.8 copy-start.11
  30.8 39.5 %all-to-all-start = ((f32[128,32,128]{2,1,0:T(8,128)}), f32[128,32,128]{2,1,0:T(8,128)S(1)}, u32[]{:S(2)}, u32[]{:S(2)}) async-start(f32[128,32,128]{2,1,0:T(8,128)} %pack.1), calls=%async_computation | async-start | bytes 4194304 | tf_op jit(solution)/shard_map/all_to_all | solution.py:937
  39.3 38.3 %copy-start = (f32[2,71,8,256]{3,2,1,0:T(8,128)S(1)}, f32[2,71,8,256]{3,2,1,0:T(8,128)}, u32[]{:S(2)}) copy-start(f32[2,71,8,256]{3,2,1,0:T(8,128)} %diffusion.1) | copy-start | bytes 3489796
  39.3 38.3 %copy-start.4 = (f32[2,8,256]{2,1,0:T(8,128)S(1)}, f32[2,8,256]{2,1,0:T(8,128)}, u32[]{:S(2)}) copy-start(f32[2,8,256]{2,1,0:T(8,128)} %east.3) | copy-start | bytes 49156
  45.2 32.4 %collective-permute-start.19 = (f32[9,8,128]{2,1,0:T(8,128)S(1)}, f32[9,8,128]{2,1,0:T(8,128)S(1)}, u32[]{:S(2)}, u32[]{:S(2)}) collective-permute-start(f32[9,8,128]{2,1,0:T(8,128)S(1)} %get-tuple-element.73), channel_id=1, source_target_pairs={{0,112},{16,0},{32,16},{48,32},{64,48},{80,64},{96,80},{112,96},{1... | collective-permute-start | bytes 110600 | tf_op jit(solution)/shard_map/ppermute | solution.py:800
  50.9 1.5 %collective-permute-start.12 = (f32[72,8,256]{2,1,0:T(8,128)}, f32[72,8,256]{2,1,0:T(8,128)}, u32[]{:S(2)}, u32[]{:S(2)}) collective-permute-start(f32[72,8,256]{2,1,0:T(8,128)} %param.12), channel_id=1, source_target_pairs={{79,15},{95,31},{111,47},{127,63},{15,79},{31,95},{47,111},{63,127}} | collective-permute-start | bytes 1769480 | tf_op jit(solution)/shard_map/cond/branch_4_fun/ppermute | solution.py:830
  52.4 17.9 %collective-permute-start.4 = (f32[72,8,256]{2,1,0:T(8,128)}, f32[72,8,256]{2,1,0:T(8,128)}, u32[]{:S(2)}, u32[]{:S(2)}) collective-permute-start(f32[72,8,256]{2,1,0:T(8,128)} %param.4), channel_id=1, source_target_pairs={{64,0},{80,16},{96,32},{112,48},{0,64},{16,80},{32,96},{48,112}} | collective-permute-start | bytes 1769480 | tf_op jit(solution)/shard_map/cond/branch_4_fun/ppermute | solution.py:830
  85.1 26.5 %collective-permute-start.20 = (f32[72,8,256]{2,1,0:T(8,128)}, f32[72,8,256]{2,1,0:T(8,128)S(1)}, u32[]{:S(2)}, u32[]{:S(2)}) collective-permute-start(f32[72,8,256]{2,1,0:T(8,128)} %get-tuple-element.77), channel_id=1, source_target_pairs={{1,0},{2,1},{3,2},{4,3},{5,4},{6,5},{7,6},{8,7},{9,8},{10,9},{11,1... | collective-permute-start | bytes 1769480 | tf_op jit(solution)/shard_map/ppermute | solution.py:785
  86.4 25.2 %collective-permute-start.21 = (f32[72,8,256]{2,1,0:T(8,128)}, f32[72,8,256]{2,1,0:T(8,128)}, u32[]{:S(2)}, u32[]{:S(2)}) collective-permute-start(f32[72,8,256]{2,1,0:T(8,128)} %get-tuple-element.78), channel_id=1, source_target_pairs={{0,1},{1,2},{2,3},{3,4},{4,5},{5,6},{6,7},{7,8},{8,9},{9,10},{10,1... | collective-permute-start | bytes 1769480 | tf_op jit(solution)/shard_map/ppermute | solution.py:785
  92.3 19.3 %all-to-all-start.1 = ((f32[8,10,8,256]{3,2,1,0:T(8,128)}), f32[8,10,8,256]{3,2,1,0:T(8,128)S(1)}, u32[]{:S(2)}, u32[]{:S(2)}) async-start(f32[8,10,8,256]{3,2,1,0:T(8,128)} %get-tuple-element.79), calls=%async_computation.1 | async-start | bytes 1310720 | tf_op jit(solution)/shard_map/all_to_all | solution.py:966
  115.7 12.9 %all-to-all-start.2 = ((f32[8,9,8,256]{3,2,1,0:T(8,128)}), f32[8,9,8,256]{3,2,1,0:T(8,128)S(1)}, u32[]{:S(2)}, u32[]{:S(2)}) async-start(f32[8,9,8,256]{3,2,1,0:T(8,128)} %rotate.1), calls=%async_computation.2 | async-start | bytes 1179648 | tf_op jit(solution)/shard_map/all_to_all | solution.py:857
  121.9 5.8 %collective-permute-start.22 = (f32[9,8,128]{2,1,0:T(8,128)S(1)}, f32[9,8,128]{2,1,0:T(8,128)S(1)}, u32[]{:S(2)}, u32[]{:S(2)}) collective-permute-start(f32[9,8,128]{2,1,0:T(8,128)S(1)} %edge.1), channel_id=1, source_target_pairs={{0,112},{16,0},{32,16},{48,32},{64,48},{80,64},{96,80},{112,96},{1... | collective-permute-start | bytes 110600 | tf_op jit(solution)/shard_map/ppermute | solution.py:800

commit v3 on v2

--- a/solution.py
+++ b/solution.py
@@ -11,6 +11,7 @@
 LANES = 128
 CAP = 16
 GROUP = 8
+SPAN = 3
 F32 = jnp.float32
 BF16 = jnp.bfloat16
 MIB = 1024 * 1024
@@ -48,19 +49,17 @@
     return pltpu.VMEM(shape, F32)
 
 
-def chunk(source, target, done, g):
-    at = pl.ds(g * GROUP, GROUP)
-    return pltpu.make_async_copy(source.at[at], target.at[at], done.at[g])
-
-
-def start_all(source, target, done):
-    for g in range(source.shape[0] // GROUP):
-        chunk(source, target, done, g).start()
-
-
-def wait_all(source, target, done):
-    for g in range(source.shape[0] // GROUP):
-        chunk(source, target, done, g).wait()
+def chunk(source, target, done, c):
+    at = pl.ds(c * GROUP * SPAN, GROUP * SPAN)
+    return pltpu.make_async_copy(source.at[at], target.at[at], done.at[c])
+
+
+def at_span(g, place, act):
+    if isinstance(g, int):
+        if g % SPAN == place:
+            act(g // SPAN)
+    else:
+        pl.when(lax.rem(g, SPAN) == place)(lambda: act(lax.div(g, SPAN)))
 
 
 def dot(a, b, contract=((1,), (0,))):
@@ -70,6 +69,10 @@
 def halves(x):
     high = x.astype(BF16)
     return high, (x - high.astype(F32)).astype(BF16)
+
+
+def spare_lane(levels, tracers):
+    return levels + tracers + 8
 
 
 def pack_kernel(
@@ -78,6 +81,7 @@
     steps, levels, held = kernels.shape
     tracers = misfits.shape[1]
     shape = (LANES, LANES)
+    half = CAP // 2
     device = lax.broadcasted_iota(jnp.int32, shape, 0)
     table = counting_table()
     for step in range(steps):
@@ -96,14 +100,31 @@
             target[step : step + 1, start : start + LANES] = jnp.where(
                 here >= 0, here * CAP + rank.astype(jnp.int32), -1
             )
-        column = columns[step : step + 1, :].astype(F32) + 1.0
-        column = jnp.where(lax.broadcasted_iota(jnp.int32, (8, held), 0) == 0, column, 0.0)
-        unused = jnp.zeros((LANES - levels - tracers - 8, held), F32)
-        high, low = halves(
-            jnp.concatenate([kernels[step], misfits[step], column, unused], axis=0)
+    spare = spare_lane(levels, tracers)
+    main = LANES - spare
+
+    def fill(k, part, pieces):
+        rows = jnp.concatenate(
+            [jnp.zeros((x, held), F32) if isinstance(x, int) else x for x in pieces], axis=0
         )
-        payload[step, :LANES, :] = high
-        payload[step, LANES:, :] = low
+        high, low = halves(rows)
+        payload[k, :LANES, part * held : (part + 1) * held] = high
+        payload[k, LANES:, part * held : (part + 1) * held] = low
+
+    def column(step):
+        x = columns[step : step + 1, :].astype(F32) + 1.0
+        return jnp.where(lax.broadcasted_iota(jnp.int32, (8, held), 0) == 0, x, 0.0)
+
+    rest = [kernels[0, main:, :], misfits[0], column(0)]
+    used = levels - main + tracers + 8
+    fill(0, 0, [kernels[1], misfits[1], column(1), main])
+    fill(0, 1, [spare, kernels[0, :main, :]])
+    fill(1, 0, [*rest, LANES - used])
+    fill(1, 1, [LANES // 2, *rest, LANES // 2 - used])
+    slot = target[0:1, :] & (CAP - 1)
+    owner = target[0:1, :] >> (CAP.bit_length() - 1)
+    lower = jnp.where((target[0:1, :] >= 0) & (slot < half), owner * half + slot, -1)
+    upper = jnp.where((target[0:1, :] >= 0) & (slot >= half), owner * half + slot - half, -1)
     owned = 256 // CAP
     tiles = out.shape[0] // owned
 
@@ -112,13 +133,14 @@
         return pltpu.make_async_copy(staged.at[at], out.at[at], done.at[i])
 
     def place(i, carry):
-        for step in range(steps):
-            hot = one_hot(target[step : step + 1, :] - i * owned * CAP, owned * CAP)
-            both = dot(hot, payload[step], ((1,), (1,)))
+        for k, ats, size, rows in (
+            (0, (target[1:2, :], target[0:1, :]), owned * CAP, slice(0, CAP)),
+            (1, (lower, upper), owned * half, slice(CAP, CAP + half)),
+        ):
+            hot = jnp.concatenate([one_hot(at - i * size, size) for at in ats], axis=1)
+            both = dot(hot, payload[k], ((1,), (1,)))
             both = both[:, :LANES] + both[:, LANES:]
-            staged[pl.ds(i * owned, owned), step * CAP : (step + 1) * CAP, :] = both.reshape(
-                owned, CAP, LANES
-            )
+            staged[pl.ds(i * owned, owned), rows, :] = both.reshape(owned, -1, LANES)
         copy(i).start()
         return carry
 
@@ -149,16 +171,16 @@
     devices = lax.axis_size("lon") * lax.axis_size("lat")
     return pl.pallas_call(
         pack_kernel,
-        out_shape=pltpu.HBM((devices, steps * CAP, LANES), F32),
+        out_shape=pltpu.HBM((devices, CAP + CAP // 2, LANES), F32),
         in_specs=[smem()] + [vmem()] * 4,
         out_specs=hbm(),
         scratch_shapes=[
-            pltpu.VMEM((steps, 2 * LANES, slots), BF16),
+            pltpu.VMEM((2, 2 * LANES, 2 * slots), BF16),
             pltpu.VMEM((steps, slots), jnp.int32),
-            pltpu.VMEM((devices, steps * CAP, LANES), F32),
+            pltpu.VMEM((devices, CAP + CAP // 2, LANES), F32),
             pltpu.SemaphoreType.DMA((devices * CAP // 256,)),
         ],
-        compiler_params=params(8),
+        compiler_params=params(12),
         name="pack",
     )(counts, held(owners), held(columns), held(kernels), held(misfits))
 
@@ -181,8 +203,25 @@
     sources = received.shape[0]
     slots = sources * CAP
     blocks = slots // LANES
-    at_column = levels + tracers
-    data = received[:, step * CAP : (step + 1) * CAP, :].reshape(slots, LANES)
+    spare = spare_lane(levels, tracers)
+    data = received[:, :CAP, :].reshape(slots, LANES)
+    if step == 1:
+        at_column = levels + tracers
+
+        def profile(turned):
+            return turned[:levels]
+
+    else:
+        at_column = levels - (LANES - spare) + tracers
+        extra = received[:, CAP:, :]
+        other = pltpu.roll(extra.reshape(slots // 2, LANES), LANES // 2, 1)
+        extra = jnp.concatenate([extra, other.reshape(extra.shape)], axis=1)
+        lane = lax.broadcasted_iota(jnp.int32, (slots, LANES), 1)
+        data = jnp.where(lane < LANES // 2, extra.reshape(slots, LANES), data)
+
+        def profile(turned):
+            return jnp.concatenate([turned[spare:], turned[: at_column - tracers]], axis=0)
+
     high, low = halves(data)
     fields[:, :LANES] = high
     fields[:, LANES:] = low
@@ -233,9 +272,11 @@
             )
             hot = jnp.where(name == own, 1.0, 0.0).astype(BF16)
             turned = block.T
-            product = turned[:levels][:, None, :] * turned[levels:at_column][None]
-            first_half, second_half = halves(product.reshape(levels * tracers, LANES))
-            total = dot(first_half, hot) + dot(second_half, hot)
+            product = profile(turned)[:, None, :] * turned[at_column - tracers : at_column][None]
+            product = product.reshape(levels * tracers, LANES)
+            total = dot(
+                jnp.concatenate(halves(product), axis=1), jnp.concatenate([hot, hot], axis=0)
+            )
             out[:, r, :, :] += total.reshape(levels, tracers, cells)
             return carry
 
@@ -320,15 +361,26 @@
     else:
         polar[levels] = jnp.broadcast_to(east, (tracers, cells))
 
-    def polar_copy(g):
+    chunks = groups // SPAN
+
+    def polar_copy(at, c):
         if by_tracer:
-            source, target = [x.at[:, g] for x in (polar, results[3])]
+            source, target = [x.at[:, at] for x in (polar, results[3])]
         else:
-            at = pl.ds(g * GROUP, GROUP if not isinstance(g, int) else 1)
             source, target = [x.at[at] for x in (polar, results[3])]
-        return pltpu.make_async_copy(source, target, done.at[3, g])
-
-    polar_copy(groups).start()
+        return pltpu.make_async_copy(source, target, done.at[3, c])
+
+    def copies(c):
+        size = SPAN if by_tracer else SPAN * GROUP
+        moves = [chunk(fields[k], results[k], done.at[k], c) for k in range(3)]
+        return [*moves, polar_copy(pl.ds(c * size, size), c)]
+
+    def send(c):
+        for copy in copies(c):
+            copy.start()
+
+    weight = polar_copy(pl.ds(groups if by_tracer else levels, 1), chunks)
+    weight.start()
     lane = lax.broadcasted_iota(jnp.int32, (tracers, LANES), 1)
 
     def group(i, solved):
@@ -356,17 +408,14 @@
             else:
                 polar[level] = row
         column[at] = west
-        for k in range(3):
-            chunk(fields[k], results[k], done.at[k], at).start()
-        polar_copy(at).start()
+        at_span(at, 0, send)
         return solved
 
     lax.fori_loop(0, groups, group, [jnp.zeros((tracers, cells), F32)] * rows)
-    polar_copy(groups).wait()
-    for g in range(groups):
-        for k in range(3):
-            chunk(fields[k], results[k], done.at[k], g).wait()
-        polar_copy(jnp.int32(g)).wait()
+    weight.wait()
+    for c in range(chunks):
+        for copy in copies(c):
+            copy.wait()
 
 
 def forward_sweep(levels, rows, tracers, cells, diffusion, right_of):
@@ -422,14 +471,14 @@
     chunk(costate, staged, arrived, 0).start()
     for copy in small:
         copy.start()
-    for g in range(1, levels // GROUP):
-        chunk(costate, staged, arrived, g).start()
+    for c in range(1, levels // (GROUP * SPAN)):
+        chunk(costate, staged, arrived, c).start()
     for copy in small:
         copy.wait()
 
     def right_of(g, j, final):
         if j == 0:
-            chunk(costate, staged, arrived, g).wait()
+            at_span(g, 0, lambda c: chunk(costate, staged, arrived, c).wait())
         level = g * GROUP + j
         rights = [staged[level, :, r, :] for r in range(rows)]
 
@@ -633,12 +682,13 @@
     last_lat = lax.axis_size("lat") - 1
     last = len(sources)
 
-    def polar_copy(source, g):
+    def polar_copy(source, c):
         if len(pole.shape) == 4:
-            return pltpu.make_async_copy(source.at[:, g], pole.at[:, g], done.at[last, g])
-        return chunk(source, pole, done.at[last], g)
-
-    for g in range(targets[0].shape[0] // GROUP):
+            at = pl.ds(c * SPAN, SPAN)
+            return pltpu.make_async_copy(source.at[:, at], pole.at[:, at], done.at[last, c])
+        return chunk(source, pole, done.at[last], c)
+
+    for g in range(targets[0].shape[0] // (GROUP * SPAN)):
         for k, (source, target) in enumerate(zip(sources, targets)):
             chunk(source, target, done.at[k], g).start()
 
@@ -705,7 +755,7 @@
 
     def right_of(g, j, final):
         if j == 0:
-            wait(g)
+            at_span(g, 0, wait)
         level = g * GROUP + j
         rights = transported(g, j, diffused, after, before, edge[g], coefs, pole)
         rights = [rights[r] + forced[level, r] for r in range(rows)]
@@ -763,20 +813,21 @@
     prepare_stencil(step, north, south, east, coefs)
 
     def group(g, carry):
-        wait(g)
+        at_span(g, 0, wait)
         edge_row = edge[g]
         for j in range(GROUP):
             level = g * GROUP + j
             values = transported(g, j, diffused, after, before, edge_row, coefs, pole)
             for r in range(rows):
                 staged[level, :, r, :] = values[r] + forced[level, r]
-        chunk(staged, state, sent, g).start()
+        at_span(g, SPAN - 1, lambda c: chunk(staged, state, sent, c).start())
         return carry
 
     lax.fori_loop(0, levels // GROUP, group, 0)
     for r in range(rows):
         gradient[:, r, :] = surface[r] + staged[levels - 1, :, r, :]
-    wait_all(staged, state, sent)
+    for c in range(levels // (GROUP * SPAN)):
+        chunk(staged, state, sent, c).wait()
 
 
 def boundary_rows(first, last):
@@ -902,9 +953,9 @@
     line = pltpu.VMEM((levels, tracers, cells), F32)
     solved_scratch = [field, line, line, pltpu.VMEM((levels + 1, tracers, cells), F32)]
     solved_specs = [hbm()] * 4 + [vmem()]
-    leaving = pltpu.SemaphoreType.DMA((4, groups + 1))
+    leaving = pltpu.SemaphoreType.DMA((4, groups // SPAN + 1))
     output = pltpu.VMEM(costate.shape, F32)
-    semaphores = pltpu.SemaphoreType.DMA((groups,))
+    semaphores = pltpu.SemaphoreType.DMA((groups // SPAN,))
     diffused, first, last, polar, column = pl.pallas_call(
         functools.partial(first_kernel, 1),
         out_shape=solved_shapes,
@@ -939,7 +990,7 @@
     forced = forcing(1, got, shape, False)
     around = first_exchange(1, *around, polar, column, *couplings[:2], polar_shift, hops)
     scratch = [field, line, line]
-    transfers = pltpu.SemaphoreType.DMA((4, groups))
+    transfers = pltpu.SemaphoreType.DMA((4, groups // SPAN))
     solved, first, last, polar, column, surface = pl.pallas_call(
         functools.partial(middle_kernel, 1),
         out_shape=[
@@ -983,7 +1034,7 @@
                 *scratch,
                 pltpu.VMEM((tracers, groups, GROUP, cells), F32),
                 output,
-                pltpu.SemaphoreType.DMA((5, groups)),
+                pltpu.SemaphoreType.DMA((5, groups // SPAN)),
                 semaphores,
             ],
             compiler_params=params(22),

time: 137 us -> 131 us (0.956)
  starting transfers between devices: 49.2 us -> 43.7 us
  local copies, waits for them, and re-layouts: 2.2 us -> 3.75 us
  Pallas kernels: 54.7 us -> 53.3 us
    pallas_call x2, Pallas kernels: 15.8 us -> 12.2 us  [forcing(): pl.pallas_call(functools.partial(streamed_forcing_kernel if streamed else...]
    all_to_all x1, waiting for transfers between devices: 5.2 us -> 8.59 us  [per_device(): lax.all_to_all(polar, 'lon', 0, 0, tiled=True)]
    pallas_call x1, Pallas kernels: 6.37 us -> 9.31 us  [packed(): pl.pallas_call(pack_kernel, out_shape=pltpu.HBM((devices, CAP + CAP // 2,...]
    ppermute x1, waiting for transfers between devices: 3.19 us -> 0.25 us  [per_device(): nearby = lax.ppermute(polar, AXES, circles((0, lat_count - 1), 1))]
    ppermute x4, starting transfers between devices: 11.6 us -> 8.7 us  [boundary_rows(): return (lax.ppermute(first, 'lat', down), lax.ppermute(last, 'lat', up))]
    unnamed x26 -> x30, local copies, waits for them, and re-layouts: 0.88 us -> 2.43 us
    ppermute x2, waiting for transfers between devices: 15.5 us -> 14 us  [first_exchange(): lax.ppermute(x, AXES, circles((lat,), k))]
where the time goes in v3:
time: 131 us; the launch traced here: 130 us
  Pallas kernels  53.3 us (41%)
  starting transfers between devices  43.7 us (33%)
  waiting for transfers between devices  25.5 us (19%)
  local copies, waits for them, and re-layouts  3.75 us (3%)
  between operations  2.43 us (2%)
  other arithmetic  1.34 us (1%)
    ppermute x2, waiting for transfers between devices, first_exchange(): lax.ppermute(x, AXES, circles((lat,), k))  14 us
    pallas_call x2, Pallas kernels, forcing(): pl.pallas_call(functools.partial(streamed_forcing_kernel if streamed else...  12.2 us
    pallas_call x1, Pallas kernels, packed(): pl.pallas_call(pack_kernel, out_shape=pltpu.HBM((devices, CAP + CAP // 2,...  9.31 us
    ppermute x4, starting transfers between devices, boundary_rows(): return (lax.ppermute(first, 'lat', down), lax.ppermute(last, 'lat', up))  8.7 us
    all_to_all x1, waiting for transfers between devices, per_device(): lax.all_to_all(polar, 'lon', 0, 0, tiled=True)  8.59 us
    all_to_all x1, starting transfers between devices, per_device(): got = lax.all_to_all(sent, AXES, 0, 0, tiled=True)  8.34 us
    ppermute x2, starting transfers between devices, westward(): lax.ppermute(edge, 'lon', [(i, (i - 1) % count) for i in range(count)])  8.02 us
    pallas_call x1, Pallas kernels, per_device(): pl.pallas_call(functools.partial(first_kernel, 1), out_shape=solved_shape...  7.82 us
  transfers between devices with their start and end apart: 12, of which 5 were waited for; matrix products, arithmetic and copies ran while one was open for 2% of the time, Pallas kernels for 20%

profile of v3, /device:TPU:0, one launch (start us, length us, event | category | flops | bytes accessed | tf_op | source)
XLA Modules:
  0.0 130.0 jit_solution(1823760353151819467)
XLA Ops:
  0.7 7.8 %first.1 = (f32[72,8,8,256]{3,2,1,0:T(8,128)}, f32[72,8,256]{2,1,0:T(8,128)}, f32[72,8,256]{2,1,0:T(8,128)}, f32[73,8,256]{2,1,0:T(8,128)}, f32[9,8,128]{2,1,0:T(8,128)S(1)}) custom-call(f32[72,8,8,256]{3,2,1,0:T(8,128)} %costate.1, f32[2,71,8,256]{3,2,1,0:T(8,128)} %diffusion.1, f32[2,8,256]{2,1,0:T(8,128)} %north.7, f32[2,8,256]{2,1,0:T(8,128)} %south.7, ...), custom_call_target="tpu_custom_call" | custom-call | tf_op jit(solution)/shard_map/first/pallas_call | solution.py:959
  8.5 7.0 %collective-permute-start.18 = (f32[73,8,256]{2,1,0:T(8,128)}, f32[73,8,256]{2,1,0:T(8,128)S(1)}, u32[]{:S(2)}, u32[]{:S(2)}) collective-permute-start(f32[73,8,256]{2,1,0:T(8,128)} %get-tuple-element.66.polar_in), channel_id=1, source_target_pairs={{16,0},{32,16},{48,32},{64,48},{80,64},{96,80},{112,96},{0,112},{3... | collective-permute-start | bytes 1794056 | tf_op jit(solution)/shard_map/ppermute | solution.py:983
  15.6 1.3 collective-permute-start.16
  16.9 3.1 %collective-permute-start.17 = (f32[72,8,256]{2,1,0:T(8,128)}, f32[72,8,256]{2,1,0:T(8,128)S(1)}, u32[]{:S(2)}, u32[]{:S(2)}) collective-permute-start(f32[72,8,256]{2,1,0:T(8,128)} %get-tuple-element.65), channel_id=1, source_target_pairs={{0,1},{1,2},{2,3},{3,4},{4,5},{5,6},{6,7},{7,8},{8,9},{9,10},{10,1... | collective-permute-start | bytes 1769480 | tf_op jit(solution)/shard_map/ppermute | solution.py:836
  20.1 9.3 %pack.1 = f32[128,24,128]{2,1,0:T(8,128)} custom-call(s32[2,1]{1,0:T(2,128)S(1)} %copy.13.counts, s32[2,1,1280]{2,1,0:T(1,128)S(1)} %bitcast.5, s32[2,1280]{1,0:T(2,128)S(1)} %copy-done.9, f32[2,72,1280]{2,1,0:T(8,128)S(1)} %copy-done.1, f32[2,8,1280]{2,1,0:T(8,128)S(1)} %copy-done.5), custom_call_target="tpu_custom_call" | custom-call | tf_op jit(solution)/shard_map/pack/pallas_call | solution.py:172
  29.7 0.6 copy-done.12
  30.7 8.3 %all-to-all-start = ((f32[128,24,128]{2,1,0:T(8,128)}), f32[128,24,128]{2,1,0:T(8,128)S(1)}, u32[]{:S(2)}, u32[]{:S(2)}) async-start(f32[128,24,128]{2,1,0:T(8,128)} %pack.1), calls=%async_computation | async-start | bytes 3145728 | tf_op jit(solution)/shard_map/all_to_all | solution.py:988
  39.1 0.6 fusion.1
  39.7 1.3 %fusion = s32[2]{0:T(128)S(1)} fusion(s32[1]{0:T(128)} %bitcast.2, s32[1]{0:T(128)} %bitcast.1), kind=kLoop, calls=%fused_computation.1 | loop fusion | flops 6 | bytes 16 | tf_op jit(solution)/shard_map/shift_right_arithmetic | solution.py:982
  41.1 3.9 %borders.1 = (f32[9,8,128]{2,1,0:T(8,128)S(1)}, f32[72,8,256]{2,1,0:T(8,128)}) custom-call(s32[2,128]{1,0:T(2,128)S(1)} %copy-done.10, f32[9,8,128]{2,1,0:T(8,128)S(1)} %get-tuple-element.70.column, f32[2,8,256]{2,1,0:T(8,128)S(1)} %copy-done.2, f32[2,8,256]{2,1,0:T(8,128)S(1)} %copy-done.3, f32[72,8,256]{2,1,0:T(8,128)} %copy-done.11, ...), custom_call_target="tpu_custom_call" | custom-call | tf_op jit(solution)/shard_map/borders/pallas_call | solution.py:857
  45.0 3.9 %collective-permute-start.19 = (f32[9,8,128]{2,1,0:T(8,128)S(1)}, f32[9,8,128]{2,1,0:T(8,128)S(1)}, u32[]{:S(2)}, u32[]{:S(2)}) collective-permute-start(f32[9,8,128]{2,1,0:T(8,128)S(1)} %get-tuple-element.73), channel_id=1, source_target_pairs={{0,112},{16,0},{32,16},{48,32},{64,48},{80,64},{96,80},{112,96},{1... | collective-permute-start | bytes 110600 | tf_op jit(solution)/shard_map/ppermute | solution.py:851
  50.8 1.5 %conditional.3 = (f32[72,8,256]{2,1,0:T(8,128)}) conditional(s32[]{:T(128)} %bitcast.4, f32[72,8,256]{2,1,0:T(8,128)} %get-tuple-element.72, f32[72,8,256]{2,1,0:T(8,128)} %get-tuple-element.72, f32[72,8,256]{2,1,0:T(8,128)} %get-tuple-element.72, f32[72,8,256]{2,1,0:T(8,128)} %get-tuple-element.72, ...), branch_computations={%region_8.0_spmd, %region_9.0_spmd, %region_10.0_spmd, %region_11.... | conditional | bytes 2359344 | solution.py:877
  50.8 1.5 %collective-permute-start.12 = (f32[72,8,256]{2,1,0:T(8,128)}, f32[72,8,256]{2,1,0:T(8,128)}, u32[]{:S(2)}, u32[]{:S(2)}) collective-permute-start(f32[72,8,256]{2,1,0:T(8,128)} %param.12), channel_id=1, source_target_pairs={{79,15},{95,31},{111,47},{127,63},{15,79},{31,95},{47,111},{63,127}} | collective-permute-start | bytes 1769480 | tf_op jit(solution)/shard_map/cond/branch_4_fun/ppermute | solution.py:881
  52.3 15.9 %conditional.2 = (f32[72,8,256]{2,1,0:T(8,128)}) conditional(s32[]{:T(128)} %bitcast.3, f32[72,8,256]{2,1,0:T(8,128)} %get-tuple-element.72, f32[72,8,256]{2,1,0:T(8,128)} %get-tuple-element.72, f32[72,8,256]{2,1,0:T(8,128)} %get-tuple-element.72, f32[72,8,256]{2,1,0:T(8,128)} %get-tuple-element.72, ...), branch_computations={%region_0.0_spmd, %region_1.0_spmd, %region_2.0_spmd, %region_3.0_... | conditional | bytes 2359344 | solution.py:877
  52.3 1.9 %collective-permute-start.3 = (f32[72,8,256]{2,1,0:T(8,128)}, f32[72,8,256]{2,1,0:T(8,128)}, u32[]{:S(2)}, u32[]{:S(2)}) collective-permute-start(f32[72,8,256]{2,1,0:T(8,128)} %param.3), channel_id=1, source_target_pairs={{48,0},{64,16},{80,32},{96,48},{112,64},{0,80},{16,96},{32,112}} | collective-permute-start | bytes 1769480 | tf_op jit(solution)/shard_map/cond/branch_3_fun/ppermute | solution.py:881
  54.2 14.0 %collective-permute-done.3 = f32[72,8,256]{2,1,0:T(8,128)} collective-permute-done((f32[72,8,256]{2,1,0:T(8,128)}, f32[72,8,256]{2,1,0:T(8,128)}, u32[]{:S(2)}, u32[]{:S(2)}) %collective-permute-start.3) | collective-permute-done | bytes 589856 | tf_op jit(solution)/shard_map/cond/branch_3_fun/ppermute | solution.py:881
  68.2 5.5 %forcing.2.forced = f32[72,8,8,256]{3,2,1,0:T(8,128)S(1)} custom-call(f32[128,24,128]{2,1,0:T(8,128)S(1)} %all-to-all-done.received), custom_call_target="tpu_custom_call" | custom-call | tf_op jit(solution)/shard_map/forcing/pallas_call | solution.py:298
  73.7 7.8 %middle.1 = (f32[72,8,8,256]{3,2,1,0:T(8,128)}, f32[72,8,256]{2,1,0:T(8,128)}, f32[72,8,256]{2,1,0:T(8,128)}, f32[8,10,8,256]{3,2,1,0:T(8,128)}, f32[9,8,128]{2,1,0:T(8,128)S(1)}, /*index=5*/f32[8,8,256]{2,1,0:T(8,128)S(1)}) custom-call(f32[72,8,8,256]{3,2,1,0:T(8,128)} %get-tuple-element.61.before_step, f32[72,8,8,256]{3,2,1,0:T(8,128)S(1)} %forcing.2.forced, ...), custom_call_target="tpu_custom_call" | custom-call | tf_op jit(solution)/shard_map/middle/pallas_call | solution.py:994
  81.5 0.6 copy-done.6
  82.1 1.3 collective-permute-start.20
  83.4 3.1 %collective-permute-start.21 = (f32[72,8,256]{2,1,0:T(8,128)}, f32[72,8,256]{2,1,0:T(8,128)S(1)}, u32[]{:S(2)}, u32[]{:S(2)}) collective-permute-start(f32[72,8,256]{2,1,0:T(8,128)} %get-tuple-element.78), channel_id=1, source_target_pairs={{0,1},{1,2},{2,3},{3,4},{4,5},{5,6},{6,7},{7,8},{8,9},{9,10},{10,1... | collective-permute-start | bytes 1769480 | tf_op jit(solution)/shard_map/ppermute | solution.py:836
  86.5 4.6 %all-to-all-start.1 = ((f32[8,10,8,256]{3,2,1,0:T(8,128)}), f32[8,10,8,256]{3,2,1,0:T(8,128)S(1)}, u32[]{:S(2)}, u32[]{:S(2)}) async-start(f32[8,10,8,256]{3,2,1,0:T(8,128)} %get-tuple-element.79), calls=%async_computation.1 | async-start | bytes 1310720 | tf_op jit(solution)/shard_map/all_to_all | solution.py:1017
  91.1 6.7 %forcing.3.forcing_in = f32[72,8,8,256]{3,2,1,0:T(8,128)} custom-call(f32[128,24,128]{2,1,0:T(8,128)S(1)} %all-to-all-done.received), custom_call_target="tpu_custom_call" | custom-call | tf_op jit(solution)/shard_map/forcing/pallas_call | solution.py:298
  97.8 8.6 %all-to-all-done.1.circle_in = f32[8,10,8,256]{3,2,1,0:T(8,128)S(1)} async-done(((f32[8,10,8,256]{3,2,1,0:T(8,128)}), f32[8,10,8,256]{3,2,1,0:T(8,128)S(1)}, u32[]{:S(2)}, u32[]{:S(2)}) %all-to-all-start.1) | async-done | bytes 655392 | tf_op jit(solution)/shard_map/all_to_all | solution.py:1017
  106.4 4.1 %rotate.1 = f32[8,9,8,256]{3,2,1,0:T(8,128)} custom-call(s32[2,128]{1,0:T(2,128)S(1)} %copy-done.10, f32[8,10,8,256]{3,2,1,0:T(8,128)S(1)} %all-to-all-done.1.circle_in), custom_call_target="tpu_custom_call" | custom-call | tf_op jit(solution)/shard_map/rotate/pallas_call | solution.py:895
  110.5 3.6 %all-to-all-start.2 = ((f32[8,9,8,256]{3,2,1,0:T(8,128)}), f32[8,9,8,256]{3,2,1,0:T(8,128)S(1)}, u32[]{:S(2)}, u32[]{:S(2)}) async-start(f32[8,9,8,256]{3,2,1,0:T(8,128)} %rotate.1), calls=%async_computation.2 | async-start | bytes 1179648 | tf_op jit(solution)/shard_map/all_to_all | solution.py:908
  114.1 0.8 copy-done.7
  114.8 0.9 edge.1
  115.8 4.2 %collective-permute-start.22 = (f32[9,8,128]{2,1,0:T(8,128)S(1)}, f32[9,8,128]{2,1,0:T(8,128)S(1)}, u32[]{:S(2)}, u32[]{:S(2)}) collective-permute-start(f32[9,8,128]{2,1,0:T(8,128)S(1)} %edge.1), channel_id=1, source_target_pairs={{0,112},{16,0},{32,16},{48,32},{64,48},{80,64},{96,80},{112,96},{1... | collective-permute-start | bytes 110600 | tf_op jit(solution)/shard_map/ppermute | solution.py:851
  119.9 1.6 %collective-permute-done.22.edge = f32[9,8,128]{2,1,0:T(8,128)S(1)} collective-permute-done((f32[9,8,128]{2,1,0:T(8,128)S(1)}, f32[9,8,128]{2,1,0:T(8,128)S(1)}, u32[]{:S(2)}, u32[]{:S(2)}) %collective-permute-start.22) | collective-permute-done | bytes 36896 | tf_op jit(solution)/shard_map/ppermute | solution.py:851
  121.6 1.0 all-to-all-done.2.pole_in
  122.6 7.3 %last.1 = (f32[72,8,8,256]{3,2,1,0:T(8,128)}, f32[8,8,256]{2,1,0:T(8,128)}) custom-call(f32[72,8,8,256]{3,2,1,0:T(8,128)} %get-tuple-element.74.before_step, f32[72,8,8,256]{3,2,1,0:T(8,128)} %forcing.3.forcing_in, f32[72,8,256]{2,1,0:T(8,128)S(1)} %collective-permute-done.20.after_in, f32[72,8,256]{2,1,0:T(8,128)S(1)} %collective-permute-done.21.before_in, ...), custom_call_target="tpu_custom_call" | custom-call | tf_op jit(solution)/shard_map/last/pallas_call | solution.py:1023
  (37 shorter events, 1.4 us)
Async XLA Ops:
  0.6 40.4 %copy-start.3 = (f32[2,8,256]{2,1,0:T(8,128)S(1)}, f32[2,8,256]{2,1,0:T(8,128)}, u32[]{:S(2)}) copy-start(f32[2,8,256]{2,1,0:T(8,128)} %south.7) | copy-start | bytes 49156
  0.6 40.4 %copy-start.2 = (f32[2,8,256]{2,1,0:T(8,128)S(1)}, f32[2,8,256]{2,1,0:T(8,128)}, u32[]{:S(2)}) copy-start(f32[2,8,256]{2,1,0:T(8,128)} %north.7) | copy-start | bytes 49156
  0.7 19.3 %copy-start.14 = (s32[2,1]{0,1:T(1,128)S(1)}, s32[2,1]{0,1:T(1,128)}, u32[]{:S(2)}) copy-start(s32[2,1]{0,1:T(1,128)} %param.35) | copy-start | bytes 28
  0.7 19.4 %copy-start.5 = (f32[2,8,1280]{2,1,0:T(8,128)S(1)}, f32[2,8,1280]{2,1,0:T(8,128)}, u32[]{:S(2)}) copy-start(f32[2,8,1280]{2,1,0:T(8,128)} %misfits.1) | copy-start | bytes 245764
  0.7 19.4 %copy-start.1 = (f32[2,72,1280]{2,1,0:T(8,128)S(1)}, f32[2,72,1280]{2,1,0:T(8,128)}, u32[]{:S(2)}) copy-start(f32[2,72,1280]{2,1,0:T(8,128)} %kernels.1) | copy-start | bytes 2211844
  0.7 19.4 %copy-start.9 = (s32[2,1280]{1,0:T(2,128)S(1)}, s32[2,1280]{1,0:T(2,128)}, u32[]{:S(2)}) copy-start(s32[2,1280]{1,0:T(2,128)} %columns.1) | copy-start | bytes 30724
  0.7 19.4 %copy-start.8 = (s32[2,1280,1]{1,2,0:T(1,128)S(1)}, s32[2,1280,1]{1,2,0:T(1,128)}, u32[]{:S(2)}) copy-start(s32[2,1280,1]{1,2,0:T(1,128)} %param.33) | copy-start | bytes 30724
  0.7 38.4 %copy-start.10 = (s32[2,128]{1,0:T(2,128)S(1)}, s32[2,128]{1,0:T(2,128)}, u32[]{:S(2)}) copy-start(s32[2,128]{1,0:T(2,128)} %shift.3) | copy-start | bytes 3076
  8.5 21.2 %collective-permute-start.18 = (f32[73,8,256]{2,1,0:T(8,128)}, f32[73,8,256]{2,1,0:T(8,128)S(1)}, u32[]{:S(2)}, u32[]{:S(2)}) collective-permute-start(f32[73,8,256]{2,1,0:T(8,128)} %get-tuple-element.66.polar_in), channel_id=1, source_target_pairs={{16,0},{32,16},{48,32},{64,48},{80,64},{96,80},{112,96},{0,112},{3... | collective-permute-start | bytes 1794056 | tf_op jit(solution)/shard_map/ppermute | solution.py:983
  15.6 13.8 %collective-permute-start.16 = (f32[72,8,256]{2,1,0:T(8,128)}, f32[72,8,256]{2,1,0:T(8,128)S(1)}, u32[]{:S(2)}, u32[]{:S(2)}) collective-permute-start(f32[72,8,256]{2,1,0:T(8,128)} %get-tuple-element.64), channel_id=1, source_target_pairs={{1,0},{2,1},{3,2},{4,3},{5,4},{6,5},{7,6},{8,7},{9,8},{10,9},{11,1... | collective-permute-start | bytes 1769480 | tf_op jit(solution)/shard_map/ppermute | solution.py:836
  16.9 12.5 %collective-permute-start.17 = (f32[72,8,256]{2,1,0:T(8,128)}, f32[72,8,256]{2,1,0:T(8,128)S(1)}, u32[]{:S(2)}, u32[]{:S(2)}) collective-permute-start(f32[72,8,256]{2,1,0:T(8,128)} %get-tuple-element.65), channel_id=1, source_target_pairs={{0,1},{1,2},{2,3},{3,4},{4,5},{5,6},{6,7},{7,8},{8,9},{9,10},{10,1... | collective-permute-start | bytes 1769480 | tf_op jit(solution)/shard_map/ppermute | solution.py:836
  29.4 11.7 %copy-start.11 = (f32[72,8,256]{2,1,0:T(8,128)}, f32[72,8,256]{2,1,0:T(8,128)S(1)}, u32[]{:S(2)}) copy-start(f32[72,8,256]{2,1,0:T(8,128)S(1)} %collective-permute-done.16.after_in) | copy-start | bytes 1769476
  29.4 0.9 copy-start.12
  29.7 1.0 copy-start.13
  30.7 37.5 %all-to-all-start = ((f32[128,24,128]{2,1,0:T(8,128)}), f32[128,24,128]{2,1,0:T(8,128)S(1)}, u32[]{:S(2)}, u32[]{:S(2)}) async-start(f32[128,24,128]{2,1,0:T(8,128)} %pack.1), calls=%async_computation | async-start | bytes 3145728 | tf_op jit(solution)/shard_map/all_to_all | solution.py:988
  39.1 34.6 %copy-start = (f32[2,71,8,256]{3,2,1,0:T(8,128)S(1)}, f32[2,71,8,256]{3,2,1,0:T(8,128)}, u32[]{:S(2)}) copy-start(f32[2,71,8,256]{3,2,1,0:T(8,128)} %diffusion.1) | copy-start | bytes 3489796
  39.1 34.6 %copy-start.4 = (f32[2,8,256]{2,1,0:T(8,128)S(1)}, f32[2,8,256]{2,1,0:T(8,128)}, u32[]{:S(2)}) copy-start(f32[2,8,256]{2,1,0:T(8,128)} %east.3) | copy-start | bytes 49156
  45.0 28.7 %collective-permute-start.19 = (f32[9,8,128]{2,1,0:T(8,128)S(1)}, f32[9,8,128]{2,1,0:T(8,128)S(1)}, u32[]{:S(2)}, u32[]{:S(2)}) collective-permute-start(f32[9,8,128]{2,1,0:T(8,128)S(1)} %get-tuple-element.73), channel_id=1, source_target_pairs={{0,112},{16,0},{32,16},{48,32},{64,48},{80,64},{96,80},{112,96},{1... | collective-permute-start | bytes 110600 | tf_op jit(solution)/shard_map/ppermute | solution.py:851
  50.8 1.5 %collective-permute-start.12 = (f32[72,8,256]{2,1,0:T(8,128)}, f32[72,8,256]{2,1,0:T(8,128)}, u32[]{:S(2)}, u32[]{:S(2)}) collective-permute-start(f32[72,8,256]{2,1,0:T(8,128)} %param.12), channel_id=1, source_target_pairs={{79,15},{95,31},{111,47},{127,63},{15,79},{31,95},{47,111},{63,127}} | collective-permute-start | bytes 1769480 | tf_op jit(solution)/shard_map/cond/branch_4_fun/ppermute | solution.py:881
  52.3 15.9 %collective-permute-start.3 = (f32[72,8,256]{2,1,0:T(8,128)}, f32[72,8,256]{2,1,0:T(8,128)}, u32[]{:S(2)}, u32[]{:S(2)}) collective-permute-start(f32[72,8,256]{2,1,0:T(8,128)} %param.3), channel_id=1, source_target_pairs={{48,0},{64,16},{80,32},{96,48},{112,64},{0,80},{16,96},{32,112}} | collective-permute-start | bytes 1769480 | tf_op jit(solution)/shard_map/cond/branch_3_fun/ppermute | solution.py:881
  81.5 0.6 copy-start.6
  82.1 24.3 %collective-permute-start.20 = (f32[72,8,256]{2,1,0:T(8,128)}, f32[72,8,256]{2,1,0:T(8,128)S(1)}, u32[]{:S(2)}, u32[]{:S(2)}) collective-permute-start(f32[72,8,256]{2,1,0:T(8,128)} %get-tuple-element.77), channel_id=1, source_target_pairs={{1,0},{2,1},{3,2},{4,3},{5,4},{6,5},{7,6},{8,7},{9,8},{10,9},{11,1... | collective-permute-start | bytes 1769480 | tf_op jit(solution)/shard_map/ppermute | solution.py:836
  83.4 23.0 %collective-permute-start.21 = (f32[72,8,256]{2,1,0:T(8,128)}, f32[72,8,256]{2,1,0:T(8,128)S(1)}, u32[]{:S(2)}, u32[]{:S(2)}) collective-permute-start(f32[72,8,256]{2,1,0:T(8,128)} %get-tuple-element.78), channel_id=1, source_target_pairs={{0,1},{1,2},{2,3},{3,4},{4,5},{5,6},{6,7},{7,8},{8,9},{9,10},{10,1... | collective-permute-start | bytes 1769480 | tf_op jit(solution)/shard_map/ppermute | solution.py:836
  86.5 19.9 %all-to-all-start.1 = ((f32[8,10,8,256]{3,2,1,0:T(8,128)}), f32[8,10,8,256]{3,2,1,0:T(8,128)S(1)}, u32[]{:S(2)}, u32[]{:S(2)}) async-start(f32[8,10,8,256]{3,2,1,0:T(8,128)} %get-tuple-element.79), calls=%async_computation.1 | async-start | bytes 1310720 | tf_op jit(solution)/shard_map/all_to_all | solution.py:1017
  110.5 12.1 %all-to-all-start.2 = ((f32[8,9,8,256]{3,2,1,0:T(8,128)}), f32[8,9,8,256]{3,2,1,0:T(8,128)S(1)}, u32[]{:S(2)}, u32[]{:S(2)}) async-start(f32[8,9,8,256]{3,2,1,0:T(8,128)} %rotate.1), calls=%async_computation.2 | async-start | bytes 1179648 | tf_op jit(solution)/shard_map/all_to_all | solution.py:908
  114.1 0.8 copy-start.7
  115.8 5.8 %collective-permute-start.22 = (f32[9,8,128]{2,1,0:T(8,128)S(1)}, f32[9,8,128]{2,1,0:T(8,128)S(1)}, u32[]{:S(2)}, u32[]{:S(2)}) collective-permute-start(f32[9,8,128]{2,1,0:T(8,128)S(1)} %edge.1), channel_id=1, source_target_pairs={{0,112},{16,0},{32,16},{48,32},{64,48},{80,64},{96,80},{112,96},{1... | collective-permute-start | bytes 110600 | tf_op jit(solution)/shard_map/ppermute | solution.py:851

commit v4 on v3

--- a/solution.py
+++ b/solution.py
@@ -125,7 +125,7 @@
     owner = target[0:1, :] >> (CAP.bit_length() - 1)
     lower = jnp.where((target[0:1, :] >= 0) & (slot < half), owner * half + slot, -1)
     upper = jnp.where((target[0:1, :] >= 0) & (slot >= half), owner * half + slot - half, -1)
-    owned = 256 // CAP
+    owned = 512 // CAP
     tiles = out.shape[0] // owned
 
     def copy(i):
@@ -137,7 +137,7 @@
             (0, (target[1:2, :], target[0:1, :]), owned * CAP, slice(0, CAP)),
             (1, (lower, upper), owned * half, slice(CAP, CAP + half)),
         ):
-            hot = jnp.concatenate([one_hot(at - i * size, size) for at in ats], axis=1)
+            hot = jnp.concatenate([tall_one_hot(at - i * size, size) for at in ats], axis=1)
             both = dot(hot, payload[k], ((1,), (1,)))
             both = both[:, :LANES] + both[:, LANES:]
             staged[pl.ds(i * owned, owned), rows, :] = both.reshape(owned, -1, LANES)
@@ -154,6 +154,11 @@
     shape = (size, at.shape[1])
     row = lax.broadcasted_iota(jnp.int32, shape, 0).astype(F32).astype(BF16)
     return jnp.where(row == at, jnp.ones(shape, BF16), jnp.zeros(shape, BF16))
+
+
+def tall_one_hot(at, size):
+    parts = [one_hot(at - start, 256) for start in range(0, size, 256)]
+    return parts[0] if len(parts) == 1 else jnp.concatenate(parts, axis=0)
 
 
 def counting_table():
@@ -178,9 +183,9 @@
             pltpu.VMEM((2, 2 * LANES, 2 * slots), BF16),
             pltpu.VMEM((steps, slots), jnp.int32),
             pltpu.VMEM((devices, CAP + CAP // 2, LANES), F32),
-            pltpu.SemaphoreType.DMA((devices * CAP // 256,)),
+            pltpu.SemaphoreType.DMA((devices * CAP // 512,)),
         ],
-        compiler_params=params(12),
+        compiler_params=params(20),
         name="pack",
     )(counts, held(owners), held(columns), held(kernels), held(misfits))
 
@@ -515,6 +520,8 @@
     nearby_in,
     edge,
     turned_out,
+    south_hops,
+    north_hops,
     after,
     before,
     polar,
@@ -523,6 +530,12 @@
     ready,
 ):
     rows, cells = north.shape[1:]
+    circle = cells * lax.axis_size("lon")
+    amounts = [
+        lax.rem(shift[step, x] + 2 * circle, circle) for x in (0, shift.shape[1] - 1)
+    ]
+    south_hops[0, 0] = amounts[0] // cells
+    north_hops[0, 0] = amounts[1] // cells
     fetches = [
         pltpu.make_async_copy(source, target, ready.at[2 + k])
         for k, (source, target) in enumerate(((polar_in, polar), (nearby_in, nearby)))
@@ -544,9 +557,8 @@
         for fetch in fetches:
             fetch.wait()
         levels = turned.shape[0]
-        circle = cells * lax.axis_size("lon")
-        amount = jnp.where(lat == 0, shift[step, 0], shift[step, rows * last_lat + rows - 1])
-        matrix = shift_matrix(lax.rem(amount + 2 * circle, circle) & (cells - 1), cells)
+        amount = jnp.where(lat == 0, amounts[0], amounts[1])
+        matrix = shift_matrix(lax.rem(amount, cells), cells)
         tracers = turned.shape[1]
         weight = shifted(polar[levels], nearby[levels], matrix)[:1, :cells]
         size = 3 * GROUP
@@ -615,7 +627,7 @@
     return finish
 
 
-def rotate_kernel(step, shift, circle_in, out, circle, turned, ready):
+def rotate_kernel(step, shift, circle_in, out, circle, pairs, turned, ready):
     parts, groups, group, cells = turned.shape
     lat = lax.axis_index("lat")
     last_lat = lax.axis_size("lat") - 1
@@ -630,18 +642,22 @@
         hops = amount // cells
         matrix = shift_matrix(amount - hops * cells, cells)
         fetch.wait()
+        height = (groups + 1) * group
         for part in range(parts):
+            at = slice(part * height, (part + 1) * height)
             near = lax.rem(part + hops, parts)
             far = lax.rem(part + hops + 1, parts)
-            low, high = [
-                circle[x].reshape((groups + 1) * group, cells) for x in (near, far)
-            ]
-            row = shifted(low, high, matrix)
-            size = groups * group
-            weight = row[size : size + 1, :cells]
-            row = row[:size]
-            row = row[:, :cells] + weight * (row[:, cells:] - row[:, :cells])
-            turned[part] = row.reshape(groups, group, cells)
+            pairs[at, :cells] = circle[near].reshape(height, cells)
+            pairs[at, cells:] = circle[far].reshape(height, cells)
+        batch = parts // 2
+        for i in range(2):
+            rows_at = slice(i * batch * height, (i + 1) * batch * height)
+            row = shifted(pairs[rows_at, :cells], pairs[rows_at, cells:], matrix)
+            row = row.reshape(batch, groups + 1, group, 2 * cells)
+            weight = row[:, groups:, :1, :cells]
+            row = row[:, :groups]
+            row = row[..., :cells] + weight * (row[..., cells:] - row[..., :cells])
+            turned[i * batch : (i + 1) * batch] = row
         send = pltpu.make_async_copy(turned, out, ready.at[1])
         send.start()
         send.wait()
@@ -851,14 +867,19 @@
     return held(lax.ppermute(edge, "lon", [(i, (i - 1) % count) for i in range(count)]))
 
 
-def first_exchange(step, after, before, nearby, polar, column, north, south, shift, hops):
+def first_exchange(step, after, before, nearby, polar, column, north, south, shift):
     poles = (0, lax.axis_size("lat") - 1)
     levels, tracers, cells = after.shape
-    edge, turned = pl.pallas_call(
+    edge, turned, *hops = pl.pallas_call(
         functools.partial(borders_kernel, step),
-        out_shape=[resident(*column.shape), pltpu.HBM((levels, tracers, cells), F32)],
+        out_shape=[
+            resident(*column.shape),
+            pltpu.HBM((levels, tracers, cells), F32),
+            jax.ShapeDtypeStruct((1, 1), jnp.int32),
+            jax.ShapeDtypeStruct((1, 1), jnp.int32),
+        ],
         in_specs=[smem()] + [vmem()] * 3 + [anywhere()] * 4,
-        out_specs=[vmem(), hbm()],
+        out_specs=[vmem(), hbm(), smem(), smem()],
         scratch_shapes=[
             pltpu.VMEM((levels, tracers, LANES), F32),
             pltpu.VMEM((levels, tracers, LANES), F32),
@@ -875,7 +896,7 @@
     for lat, hop in zip(poles, hops):
         moved.append(
             lax.switch(
-                hop,
+                hop.reshape(()),
                 [
                     functools.partial(
                         lambda k, lat, x: lax.ppermute(x, AXES, circles((lat,), k)), k, lat
@@ -899,10 +920,11 @@
         out_specs=hbm(),
         scratch_shapes=[
             pltpu.VMEM(circle.shape, F32),
+            pltpu.VMEM((parts * groups * group, 2 * cells), F32),
             pltpu.VMEM(shape, F32),
             pltpu.SemaphoreType.DMA((2,)),
         ],
-        compiler_params=params(8),
+        compiler_params=params(14),
         name="rotate",
     )(shift, circle)
     pole = lax.all_to_all(turned, "lon", 0, 0, tiled=True)
@@ -977,10 +999,7 @@
     couplings = [held(x) for x in couplings]
     diffusion = held(diffusion)
     counts, column = lax.optimization_barrier((sounding_counts, column))
-    lat_count, lon_count = lax.axis_size("lat"), lax.axis_size("lon")
-    ends = jnp.stack([polar_shift[1, 0], polar_shift[1, -1]])
-    hops = (ends & (cells * lon_count - 1)) >> (cells.bit_length() - 1)
-    nearby = lax.ppermute(polar, AXES, circles((0, lat_count - 1), 1))
+    nearby = lax.ppermute(polar, AXES, circles((0, lax.axis_size("lat") - 1), 1))
     around = (*boundary_rows(first, last), nearby)
     sent = packed(counts, owner_rows, columns, kernels, misfits)
     sent, *around = lax.optimization_barrier((sent, *around))
@@ -988,7 +1007,7 @@
     got = lax.all_to_all(sent, AXES, 0, 0, tiled=True)
     shape = (levels, rows, tracers, cells)
     forced = forcing(1, got, shape, False)
-    around = first_exchange(1, *around, polar, column, *couplings[:2], polar_shift, hops)
+    around = first_exchange(1, *around, polar, column, *couplings[:2], polar_shift)
     scratch = [field, line, line]
     transfers = pltpu.SemaphoreType.DMA((4, groups // SPAN))
     solved, first, last, polar, column, surface = pl.pallas_call(

time: 131 us -> 130 us (level)
  Pallas kernels: 53.3 us -> 59.7 us
  waiting for transfers between devices: 25.5 us -> 21 us
  local copies, waits for them, and re-layouts: 3.75 us -> 2.34 us
  other arithmetic: 1.34 us -> 0 us
    pallas_call x2, Pallas kernels: 12.2 us -> 21.4 us  [forcing(): pl.pallas_call(functools.partial(streamed_forcing_kernel if streamed else...]
    all_to_all x1, waiting for transfers between devices: 8.59 us -> 0.01 us  [per_device(): lax.all_to_all(polar, 'lon', 0, 0, tiled=True)]
    ppermute x1, waiting for transfers between devices: 0.25 us -> 2.5 us  [per_device(): lax.ppermute(polar, AXES, circles((0, lax.axis_size('lat') - 1), 1))]
    pallas_call x1, Pallas kernels: 9.31 us -> 7.06 us  [packed(): pl.pallas_call(pack_kernel, out_shape=pltpu.HBM((devices, CAP + CAP // 2,...]
    ppermute x2, waiting for transfers between devices: 14 us -> 15.4 us  [first_exchange(): lax.ppermute(x, AXES, circles((lat,), k))]
    shift_right_arithmetic x1 -> x0, other arithmetic: 1.34 us -> none  [per_device(): hops = (ends & cells * lon_count - 1) >> cells.bit_length() - 1]
  transfers between devices with their start and end apart: 12 -> 12, of which waited for: 5 -> 4; matrix products, arithmetic and copies ran while one was open for 2% -> 0% of each run, Pallas kernels for 20% -> 26%
where the time goes in v4:
time: 130 us; the launch traced here: 129 us
  Pallas kernels  59.7 us (46%)
  starting transfers between devices  44.1 us (34%)
  waiting for transfers between devices  21 us (16%)
  between operations  2.35 us (2%)
  local copies, waits for them, and re-layouts  2.34 us (2%)
    pallas_call x2, Pallas kernels, forcing(): pl.pallas_call(functools.partial(streamed_forcing_kernel if streamed else...  21.4 us
    ppermute x2, waiting for transfers between devices, first_exchange(): lax.ppermute(x, AXES, circles((lat,), k))  15.4 us
    ppermute x4, starting transfers between devices, boundary_rows(): return (lax.ppermute(first, 'lat', down), lax.ppermute(last, 'lat', up))  8.7 us
    all_to_all x1, starting transfers between devices, per_device(): got = lax.all_to_all(sent, AXES, 0, 0, tiled=True)  8.52 us
    ppermute x2, starting transfers between devices, westward(): lax.ppermute(edge, 'lon', [(i, (i - 1) % count) for i in range(count)])  8.06 us
    pallas_call x1, Pallas kernels, per_device(): pl.pallas_call(functools.partial(first_kernel, 1), out_shape=solved_shape...  7.81 us
    pallas_call x1, Pallas kernels, per_device(): pl.pallas_call(functools.partial(middle_kernel, 1), out_shape=[*solved_sh...  7.8 us
    pallas_call x1, Pallas kernels, per_device(): pl.pallas_call(functools.partial(last_kernel, 0), out_shape=[pltpu.HBM(co...  7.29 us
  transfers between devices with their start and end apart: 12, of which 4 were waited for; matrix products, arithmetic and copies ran while one was open for 0% of the time, Pallas kernels for 26%

profile of v4, /device:TPU:0, one launch (start us, length us, event | category | flops | bytes accessed | tf_op | source)
XLA Modules:
  0.0 129.5 jit_solution(12256805361707609651)
XLA Ops:
  0.7 7.8 %first.1 = (f32[72,8,8,256]{3,2,1,0:T(8,128)}, f32[72,8,256]{2,1,0:T(8,128)}, f32[72,8,256]{2,1,0:T(8,128)}, f32[73,8,256]{2,1,0:T(8,128)}, f32[9,8,128]{2,1,0:T(8,128)S(1)}) custom-call(f32[72,8,8,256]{3,2,1,0:T(8,128)} %costate.1, f32[2,71,8,256]{3,2,1,0:T(8,128)} %diffusion.1, f32[2,8,256]{2,1,0:T(8,128)} %north.7, f32[2,8,256]{2,1,0:T(8,128)} %south.7, ...), custom_call_target="tpu_custom_call" | custom-call | tf_op jit(solution)/shard_map/first/pallas_call | solution.py:981
  8.5 7.0 %collective-permute-start.18 = (f32[73,8,256]{2,1,0:T(8,128)}, f32[73,8,256]{2,1,0:T(8,128)S(1)}, u32[]{:S(2)}, u32[]{:S(2)}) collective-permute-start(f32[73,8,256]{2,1,0:T(8,128)} %get-tuple-element.68.polar_in), channel_id=1, source_target_pairs={{16,0},{32,16},{48,32},{64,48},{80,64},{96,80},{112,96},{0,112},{3... | collective-permute-start | bytes 1794056 | tf_op jit(solution)/shard_map/ppermute | solution.py:1002
  15.6 1.3 collective-permute-start.16
  16.9 3.1 %collective-permute-start.17 = (f32[72,8,256]{2,1,0:T(8,128)}, f32[72,8,256]{2,1,0:T(8,128)S(1)}, u32[]{:S(2)}, u32[]{:S(2)}) collective-permute-start(f32[72,8,256]{2,1,0:T(8,128)} %get-tuple-element.67), channel_id=1, source_target_pairs={{0,1},{1,2},{2,3},{3,4},{4,5},{5,6},{6,7},{7,8},{8,9},{9,10},{10,1... | collective-permute-start | bytes 1769480 | tf_op jit(solution)/shard_map/ppermute | solution.py:852
  20.0 0.1 copy.13.counts
  20.1 7.1 %pack.1 = f32[128,24,128]{2,1,0:T(8,128)} custom-call(s32[2,1]{1,0:T(2,128)S(1)} %copy.13.counts, s32[2,1,1280]{2,1,0:T(1,128)S(1)} %bitcast.3, s32[2,1280]{1,0:T(2,128)S(1)} %copy-done.9, f32[2,72,1280]{2,1,0:T(8,128)S(1)} %copy-done.1, f32[2,8,1280]{2,1,0:T(8,128)S(1)} %copy-done.5), custom_call_target="tpu_custom_call" | custom-call | tf_op jit(solution)/shard_map/pack/pallas_call | solution.py:177
  27.2 2.5 %collective-permute-done.18.nearby_in = f32[73,8,256]{2,1,0:T(8,128)S(1)} collective-permute-done((f32[73,8,256]{2,1,0:T(8,128)}, f32[73,8,256]{2,1,0:T(8,128)S(1)}, u32[]{:S(2)}, u32[]{:S(2)}) %collective-permute-start.18) | collective-permute-done | bytes 598048 | tf_op jit(solution)/shard_map/ppermute | solution.py:1002
  29.7 0.8 copy-done.13
  30.5 8.5 %all-to-all-start = ((f32[128,24,128]{2,1,0:T(8,128)}), f32[128,24,128]{2,1,0:T(8,128)S(1)}, u32[]{:S(2)}, u32[]{:S(2)}) async-start(f32[128,24,128]{2,1,0:T(8,128)} %pack.1), calls=%async_computation | async-start | bytes 3145728 | tf_op jit(solution)/shard_map/all_to_all | solution.py:1007
  39.1 0.0 copy-start
  39.1 4.4 %borders.1 = (f32[9,8,128]{2,1,0:T(8,128)S(1)}, f32[72,8,256]{2,1,0:T(8,128)}, s32[1,1]{1,0:T(1,128)}, s32[1,1]{1,0:T(1,128)}) custom-call(s32[2,128]{1,0:T(2,128)S(1)} %copy-done.10, f32[9,8,128]{2,1,0:T(8,128)S(1)} %get-tuple-element.72.column, f32[2,8,256]{2,1,0:T(8,128)S(1)} %copy-done.2, f32[2,8,256]{2,1,0:T(8,128)S(1)} %copy-done.3, ...), custom_call_target="tpu_custom_call" | custom-call | tf_op jit(solution)/shard_map/borders/pallas_call | solution.py:873
  43.5 3.9 %collective-permute-start.19 = (f32[9,8,128]{2,1,0:T(8,128)S(1)}, f32[9,8,128]{2,1,0:T(8,128)S(1)}, u32[]{:S(2)}, u32[]{:S(2)}) collective-permute-start(f32[9,8,128]{2,1,0:T(8,128)S(1)} %get-tuple-element.77), channel_id=1, source_target_pairs={{0,112},{16,0},{32,16},{48,32},{64,48},{80,64},{96,80},{112,96},{1... | collective-permute-start | bytes 110600 | tf_op jit(solution)/shard_map/ppermute | solution.py:867
  48.6 1.5 %conditional.3 = (f32[72,8,256]{2,1,0:T(8,128)}) conditional(s32[]{:T(128)} %bitcast.2, f32[72,8,256]{2,1,0:T(8,128)} %get-tuple-element.75, f32[72,8,256]{2,1,0:T(8,128)} %get-tuple-element.75, f32[72,8,256]{2,1,0:T(8,128)} %get-tuple-element.75, f32[72,8,256]{2,1,0:T(8,128)} %get-tuple-element.75, ...), branch_computations={%region_8.0_spmd, %region_9.0_spmd, %region_10.0_spmd, %region_11.... | conditional | bytes 2359344 | solution.py:898
  48.6 1.5 %collective-permute-start.12 = (f32[72,8,256]{2,1,0:T(8,128)}, f32[72,8,256]{2,1,0:T(8,128)}, u32[]{:S(2)}, u32[]{:S(2)}) collective-permute-start(f32[72,8,256]{2,1,0:T(8,128)} %param.12), channel_id=1, source_target_pairs={{79,15},{95,31},{111,47},{127,63},{15,79},{31,95},{47,111},{63,127}} | collective-permute-start | bytes 1769480 | tf_op jit(solution)/shard_map/cond/branch_4_fun/ppermute | solution.py:902
  50.1 17.7 %conditional.2 = (f32[72,8,256]{2,1,0:T(8,128)}) conditional(s32[]{:T(128)} %bitcast.1, f32[72,8,256]{2,1,0:T(8,128)} %get-tuple-element.75, f32[72,8,256]{2,1,0:T(8,128)} %get-tuple-element.75, f32[72,8,256]{2,1,0:T(8,128)} %get-tuple-element.75, f32[72,8,256]{2,1,0:T(8,128)} %get-tuple-element.75, ...), branch_computations={%region_0.0_spmd, %region_1.0_spmd, %region_2.0_spmd, %region_3.0_... | conditional | bytes 2359344 | solution.py:898
  50.1 2.2 %collective-permute-start.2 = (f32[72,8,256]{2,1,0:T(8,128)}, f32[72,8,256]{2,1,0:T(8,128)}, u32[]{:S(2)}, u32[]{:S(2)}) collective-permute-start(f32[72,8,256]{2,1,0:T(8,128)} %param.2), channel_id=1, source_target_pairs={{32,0},{48,16},{64,32},{80,48},{96,64},{112,80},{0,96},{16,112}} | collective-permute-start | bytes 1769480 | tf_op jit(solution)/shard_map/cond/branch_2_fun/ppermute | solution.py:902
  52.4 15.4 %collective-permute-done.2 = f32[72,8,256]{2,1,0:T(8,128)} collective-permute-done((f32[72,8,256]{2,1,0:T(8,128)}, f32[72,8,256]{2,1,0:T(8,128)}, u32[]{:S(2)}, u32[]{:S(2)}) %collective-permute-start.2) | collective-permute-done | bytes 589856 | tf_op jit(solution)/shard_map/cond/branch_2_fun/ppermute | solution.py:902
  67.8 10.0 %forcing.2.forced = f32[72,8,8,256]{3,2,1,0:T(8,128)S(1)} custom-call(f32[128,24,128]{2,1,0:T(8,128)S(1)} %all-to-all-done.received), custom_call_target="tpu_custom_call" | custom-call | tf_op jit(solution)/shard_map/forcing/pallas_call | solution.py:303
  77.8 7.8 %middle.1 = (f32[72,8,8,256]{3,2,1,0:T(8,128)}, f32[72,8,256]{2,1,0:T(8,128)}, f32[72,8,256]{2,1,0:T(8,128)}, f32[8,10,8,256]{3,2,1,0:T(8,128)}, f32[9,8,128]{2,1,0:T(8,128)S(1)}, /*index=5*/f32[8,8,256]{2,1,0:T(8,128)S(1)}) custom-call(f32[72,8,8,256]{3,2,1,0:T(8,128)} %get-tuple-element.63.before_step, f32[72,8,8,256]{3,2,1,0:T(8,128)S(1)} %forcing.2.forced, ...), custom_call_target="tpu_custom_call" | custom-call | tf_op jit(solution)/shard_map/middle/pallas_call | solution.py:1013
  85.7 0.6 copy-done.6
  86.3 1.3 collective-permute-start.20
  87.6 3.1 %collective-permute-start.21 = (f32[72,8,256]{2,1,0:T(8,128)}, f32[72,8,256]{2,1,0:T(8,128)S(1)}, u32[]{:S(2)}, u32[]{:S(2)}) collective-permute-start(f32[72,8,256]{2,1,0:T(8,128)} %get-tuple-element.82), channel_id=1, source_target_pairs={{0,1},{1,2},{2,3},{3,4},{4,5},{5,6},{6,7},{7,8},{8,9},{9,10},{10,1... | collective-permute-start | bytes 1769480 | tf_op jit(solution)/shard_map/ppermute | solution.py:852
  90.6 3.6 %all-to-all-start.1 = ((f32[8,10,8,256]{3,2,1,0:T(8,128)}), f32[8,10,8,256]{3,2,1,0:T(8,128)S(1)}, u32[]{:S(2)}, u32[]{:S(2)}) async-start(f32[8,10,8,256]{3,2,1,0:T(8,128)} %get-tuple-element.83), calls=%async_computation.1 | async-start | bytes 1310720 | tf_op jit(solution)/shard_map/all_to_all | solution.py:1036
  94.2 11.4 %forcing.3.forcing_in = f32[72,8,8,256]{3,2,1,0:T(8,128)} custom-call(f32[128,24,128]{2,1,0:T(8,128)S(1)} %all-to-all-done.received), custom_call_target="tpu_custom_call" | custom-call | tf_op jit(solution)/shard_map/forcing/pallas_call | solution.py:303
  105.6 3.0 %rotate.1 = f32[8,9,8,256]{3,2,1,0:T(8,128)} custom-call(s32[2,128]{1,0:T(2,128)S(1)} %copy-done.10, f32[8,10,8,256]{3,2,1,0:T(8,128)S(1)} %all-to-all-done.1.circle_in), custom_call_target="tpu_custom_call" | custom-call | tf_op jit(solution)/shard_map/rotate/pallas_call | solution.py:916
  108.6 4.5 %all-to-all-start.2 = ((f32[8,9,8,256]{3,2,1,0:T(8,128)}), f32[8,9,8,256]{3,2,1,0:T(8,128)S(1)}, u32[]{:S(2)}, u32[]{:S(2)}) async-start(f32[8,9,8,256]{3,2,1,0:T(8,128)} %rotate.1), calls=%async_computation.2 | async-start | bytes 1179648 | tf_op jit(solution)/shard_map/all_to_all | solution.py:930
  113.1 0.8 copy-done.7
  113.8 0.9 edge.1
  114.8 4.2 %collective-permute-start.22 = (f32[9,8,128]{2,1,0:T(8,128)S(1)}, f32[9,8,128]{2,1,0:T(8,128)S(1)}, u32[]{:S(2)}, u32[]{:S(2)}) collective-permute-start(f32[9,8,128]{2,1,0:T(8,128)S(1)} %edge.1), channel_id=1, source_target_pairs={{0,112},{16,0},{32,16},{48,32},{64,48},{80,64},{96,80},{112,96},{1... | collective-permute-start | bytes 110600 | tf_op jit(solution)/shard_map/ppermute | solution.py:867
  119.0 2.2 %collective-permute-done.22.edge = f32[9,8,128]{2,1,0:T(8,128)S(1)} collective-permute-done((f32[9,8,128]{2,1,0:T(8,128)S(1)}, f32[9,8,128]{2,1,0:T(8,128)S(1)}, u32[]{:S(2)}, u32[]{:S(2)}) %collective-permute-start.22) | collective-permute-done | bytes 36896 | tf_op jit(solution)/shard_map/ppermute | solution.py:867
  121.2 0.8 all-to-all-done.2.pole_in
  122.0 7.3 %last.1 = (f32[72,8,8,256]{3,2,1,0:T(8,128)}, f32[8,8,256]{2,1,0:T(8,128)}) custom-call(f32[72,8,8,256]{3,2,1,0:T(8,128)} %get-tuple-element.78.before_step, f32[72,8,8,256]{3,2,1,0:T(8,128)} %forcing.3.forcing_in, f32[72,8,256]{2,1,0:T(8,128)S(1)} %collective-permute-done.20.after_in, f32[72,8,256]{2,1,0:T(8,128)S(1)} %collective-permute-done.21.before_in, ...), custom_call_target="tpu_custom_call" | custom-call | tf_op jit(solution)/shard_map/last/pallas_call | solution.py:1042
  (34 shorter events, 0.1 us)
Async XLA Ops:
  0.6 38.4 %copy-start.3 = (f32[2,8,256]{2,1,0:T(8,128)S(1)}, f32[2,8,256]{2,1,0:T(8,128)}, u32[]{:S(2)}) copy-start(f32[2,8,256]{2,1,0:T(8,128)} %south.7) | copy-start | bytes 49156
  0.6 38.4 %copy-start.2 = (f32[2,8,256]{2,1,0:T(8,128)S(1)}, f32[2,8,256]{2,1,0:T(8,128)}, u32[]{:S(2)}) copy-start(f32[2,8,256]{2,1,0:T(8,128)} %north.7) | copy-start | bytes 49156
  0.7 19.3 %copy-start.14 = (s32[2,1]{0,1:T(1,128)S(1)}, s32[2,1]{0,1:T(1,128)}, u32[]{:S(2)}) copy-start(s32[2,1]{0,1:T(1,128)} %param.35) | copy-start | bytes 28
  0.7 19.4 %copy-start.5 = (f32[2,8,1280]{2,1,0:T(8,128)S(1)}, f32[2,8,1280]{2,1,0:T(8,128)}, u32[]{:S(2)}) copy-start(f32[2,8,1280]{2,1,0:T(8,128)} %misfits.1) | copy-start | bytes 245764
  0.7 19.4 %copy-start.1 = (f32[2,72,1280]{2,1,0:T(8,128)S(1)}, f32[2,72,1280]{2,1,0:T(8,128)}, u32[]{:S(2)}) copy-start(f32[2,72,1280]{2,1,0:T(8,128)} %kernels.1) | copy-start | bytes 2211844
  0.7 19.4 %copy-start.9 = (s32[2,1280]{1,0:T(2,128)S(1)}, s32[2,1280]{1,0:T(2,128)}, u32[]{:S(2)}) copy-start(s32[2,1280]{1,0:T(2,128)} %columns.1) | copy-start | bytes 30724
  0.7 19.4 %copy-start.8 = (s32[2,1280,1]{1,2,0:T(1,128)S(1)}, s32[2,1280,1]{1,2,0:T(1,128)}, u32[]{:S(2)}) copy-start(s32[2,1280,1]{1,2,0:T(1,128)} %param.33) | copy-start | bytes 30724
  0.7 38.4 %copy-start.10 = (s32[2,128]{1,0:T(2,128)S(1)}, s32[2,128]{1,0:T(2,128)}, u32[]{:S(2)}) copy-start(s32[2,128]{1,0:T(2,128)} %shift.3) | copy-start | bytes 3076
  8.5 21.2 %collective-permute-start.18 = (f32[73,8,256]{2,1,0:T(8,128)}, f32[73,8,256]{2,1,0:T(8,128)S(1)}, u32[]{:S(2)}, u32[]{:S(2)}) collective-permute-start(f32[73,8,256]{2,1,0:T(8,128)} %get-tuple-element.68.polar_in), channel_id=1, source_target_pairs={{16,0},{32,16},{48,32},{64,48},{80,64},{96,80},{112,96},{0,112},{3... | collective-permute-start | bytes 1794056 | tf_op jit(solution)/shard_map/ppermute | solution.py:1002
  15.6 11.6 %collective-permute-start.16 = (f32[72,8,256]{2,1,0:T(8,128)}, f32[72,8,256]{2,1,0:T(8,128)S(1)}, u32[]{:S(2)}, u32[]{:S(2)}) collective-permute-start(f32[72,8,256]{2,1,0:T(8,128)} %get-tuple-element.66), channel_id=1, source_target_pairs={{1,0},{2,1},{3,2},{4,3},{5,4},{6,5},{7,6},{8,7},{9,8},{10,9},{11,1... | collective-permute-start | bytes 1769480 | tf_op jit(solution)/shard_map/ppermute | solution.py:852
  16.9 10.3 %collective-permute-start.17 = (f32[72,8,256]{2,1,0:T(8,128)}, f32[72,8,256]{2,1,0:T(8,128)S(1)}, u32[]{:S(2)}, u32[]{:S(2)}) collective-permute-start(f32[72,8,256]{2,1,0:T(8,128)} %get-tuple-element.67), channel_id=1, source_target_pairs={{0,1},{1,2},{2,3},{3,4},{4,5},{5,6},{6,7},{7,8},{8,9},{9,10},{10,1... | collective-permute-start | bytes 1769480 | tf_op jit(solution)/shard_map/ppermute | solution.py:852
  27.2 11.9 %copy-start.11 = (f32[72,8,256]{2,1,0:T(8,128)}, f32[72,8,256]{2,1,0:T(8,128)S(1)}, u32[]{:S(2)}) copy-start(f32[72,8,256]{2,1,0:T(8,128)S(1)} %collective-permute-done.16.after_in) | copy-start | bytes 1769476
  27.2 2.5 %copy-start.12 = (f32[72,8,256]{2,1,0:T(8,128)}, f32[72,8,256]{2,1,0:T(8,128)S(1)}, u32[]{:S(2)}) copy-start(f32[72,8,256]{2,1,0:T(8,128)S(1)} %collective-permute-done.17.before_in) | copy-start | bytes 1769476
  29.7 0.8 copy-start.13
  30.5 37.3 %all-to-all-start = ((f32[128,24,128]{2,1,0:T(8,128)}), f32[128,24,128]{2,1,0:T(8,128)S(1)}, u32[]{:S(2)}, u32[]{:S(2)}) async-start(f32[128,24,128]{2,1,0:T(8,128)} %pack.1), calls=%async_computation | async-start | bytes 3145728 | tf_op jit(solution)/shard_map/all_to_all | solution.py:1007
  39.1 38.8 %copy-start = (f32[2,71,8,256]{3,2,1,0:T(8,128)S(1)}, f32[2,71,8,256]{3,2,1,0:T(8,128)}, u32[]{:S(2)}) copy-start(f32[2,71,8,256]{3,2,1,0:T(8,128)} %diffusion.1) | copy-start | bytes 3489796
  39.1 38.8 %copy-start.4 = (f32[2,8,256]{2,1,0:T(8,128)S(1)}, f32[2,8,256]{2,1,0:T(8,128)}, u32[]{:S(2)}) copy-start(f32[2,8,256]{2,1,0:T(8,128)} %east.3) | copy-start | bytes 49156
  43.5 34.3 %collective-permute-start.19 = (f32[9,8,128]{2,1,0:T(8,128)S(1)}, f32[9,8,128]{2,1,0:T(8,128)S(1)}, u32[]{:S(2)}, u32[]{:S(2)}) collective-permute-start(f32[9,8,128]{2,1,0:T(8,128)S(1)} %get-tuple-element.77), channel_id=1, source_target_pairs={{0,112},{16,0},{32,16},{48,32},{64,48},{80,64},{96,80},{112,96},{1... | collective-permute-start | bytes 110600 | tf_op jit(solution)/shard_map/ppermute | solution.py:867
  48.6 1.5 %collective-permute-start.12 = (f32[72,8,256]{2,1,0:T(8,128)}, f32[72,8,256]{2,1,0:T(8,128)}, u32[]{:S(2)}, u32[]{:S(2)}) collective-permute-start(f32[72,8,256]{2,1,0:T(8,128)} %param.12), channel_id=1, source_target_pairs={{79,15},{95,31},{111,47},{127,63},{15,79},{31,95},{47,111},{63,127}} | collective-permute-start | bytes 1769480 | tf_op jit(solution)/shard_map/cond/branch_4_fun/ppermute | solution.py:902
  50.1 17.7 %collective-permute-start.2 = (f32[72,8,256]{2,1,0:T(8,128)}, f32[72,8,256]{2,1,0:T(8,128)}, u32[]{:S(2)}, u32[]{:S(2)}) collective-permute-start(f32[72,8,256]{2,1,0:T(8,128)} %param.2), channel_id=1, source_target_pairs={{32,0},{48,16},{64,32},{80,48},{96,64},{112,80},{0,96},{16,112}} | collective-permute-start | bytes 1769480 | tf_op jit(solution)/shard_map/cond/branch_2_fun/ppermute | solution.py:902
  85.7 0.6 copy-start.6
  86.3 19.3 %collective-permute-start.20 = (f32[72,8,256]{2,1,0:T(8,128)}, f32[72,8,256]{2,1,0:T(8,128)S(1)}, u32[]{:S(2)}, u32[]{:S(2)}) collective-permute-start(f32[72,8,256]{2,1,0:T(8,128)} %get-tuple-element.81), channel_id=1, source_target_pairs={{1,0},{2,1},{3,2},{4,3},{5,4},{6,5},{7,6},{8,7},{9,8},{10,9},{11,1... | collective-permute-start | bytes 1769480 | tf_op jit(solution)/shard_map/ppermute | solution.py:852
  87.6 18.1 %collective-permute-start.21 = (f32[72,8,256]{2,1,0:T(8,128)}, f32[72,8,256]{2,1,0:T(8,128)S(1)}, u32[]{:S(2)}, u32[]{:S(2)}) collective-permute-start(f32[72,8,256]{2,1,0:T(8,128)} %get-tuple-element.82), channel_id=1, source_target_pairs={{0,1},{1,2},{2,3},{3,4},{4,5},{5,6},{6,7},{7,8},{8,9},{9,10},{10,1... | collective-permute-start | bytes 1769480 | tf_op jit(solution)/shard_map/ppermute | solution.py:852
  90.6 15.0 %all-to-all-start.1 = ((f32[8,10,8,256]{3,2,1,0:T(8,128)}), f32[8,10,8,256]{3,2,1,0:T(8,128)S(1)}, u32[]{:S(2)}, u32[]{:S(2)}) async-start(f32[8,10,8,256]{3,2,1,0:T(8,128)} %get-tuple-element.83), calls=%async_computation.1 | async-start | bytes 1310720 | tf_op jit(solution)/shard_map/all_to_all | solution.py:1036
  108.6 13.4 %all-to-all-start.2 = ((f32[8,9,8,256]{3,2,1,0:T(8,128)}), f32[8,9,8,256]{3,2,1,0:T(8,128)S(1)}, u32[]{:S(2)}, u32[]{:S(2)}) async-start(f32[8,9,8,256]{3,2,1,0:T(8,128)} %rotate.1), calls=%async_computation.2 | async-start | bytes 1179648 | tf_op jit(solution)/shard_map/all_to_all | solution.py:930
  113.1 0.8 copy-start.7
  114.8 6.4 %collective-permute-start.22 = (f32[9,8,128]{2,1,0:T(8,128)S(1)}, f32[9,8,128]{2,1,0:T(8,128)S(1)}, u32[]{:S(2)}, u32[]{:S(2)}) collective-permute-start(f32[9,8,128]{2,1,0:T(8,128)S(1)} %edge.1), channel_id=1, source_target_pairs={{0,112},{16,0},{32,16},{48,32},{64,48},{80,64},{96,80},{112,96},{1... | collective-permute-start | bytes 110600 | tf_op jit(solution)/shard_map/ppermute | solution.py:867

commit v5 on v4

--- a/solution.py
+++ b/solution.py
@@ -508,58 +508,40 @@
     return own * diffused[level, row] + north * up + south * down
 
 
-def borders_kernel(
+def turn_kernel(
     step,
     shift,
-    column,
-    north,
-    south,
-    after_in,
-    before_in,
     polar_in,
     nearby_in,
-    edge,
     turned_out,
     south_hops,
     north_hops,
-    after,
-    before,
     polar,
     nearby,
     turned,
     ready,
 ):
-    rows, cells = north.shape[1:]
+    levels, tracers, cells = turned.shape
     circle = cells * lax.axis_size("lon")
     amounts = [
         lax.rem(shift[step, x] + 2 * circle, circle) for x in (0, shift.shape[1] - 1)
     ]
     south_hops[0, 0] = amounts[0] // cells
     north_hops[0, 0] = amounts[1] // cells
-    fetches = [
-        pltpu.make_async_copy(source, target, ready.at[2 + k])
-        for k, (source, target) in enumerate(((polar_in, polar), (nearby_in, nearby)))
-    ]
-    sending = pltpu.make_async_copy(turned, turned_out, ready.at[4])
     lat = lax.axis_index("lat")
-    last_lat = lax.axis_size("lat") - 1
-    at_pole = (lat == 0) | (lat == last_lat)
-
-    @pl.when(at_pole)
+
+    @pl.when((lat == 0) | (lat == lax.axis_size("lat") - 1))
     def _():
+        fetches = [
+            pltpu.make_async_copy(polar_in, polar, ready.at[0]),
+            pltpu.make_async_copy(nearby_in, nearby, ready.at[1]),
+        ]
         for fetch in fetches:
             fetch.start()
-
-    finish = west_column(step, column, north, south, after_in, before_in, edge, after, before, ready)
-
-    @pl.when(at_pole)
-    def _():
+        amount = jnp.where(lat == 0, amounts[0], amounts[1])
+        matrix = shift_matrix(lax.rem(amount, cells), cells)
         for fetch in fetches:
             fetch.wait()
-        levels = turned.shape[0]
-        amount = jnp.where(lat == 0, amounts[0], amounts[1])
-        matrix = shift_matrix(lax.rem(amount, cells), cells)
-        tracers = turned.shape[1]
         weight = shifted(polar[levels], nearby[levels], matrix)[:1, :cells]
         size = 3 * GROUP
         for i in range(levels // size):
@@ -568,13 +550,9 @@
             row = shifted(low, high, matrix)
             row = row[:, :cells] + weight * (row[:, cells:] - row[:, :cells])
             turned[at] = row.reshape(size, tracers, cells)
-        sending.start()
-
-    finish()
-
-    @pl.when(at_pole)
-    def _():
-        sending.wait()
+        send = pltpu.make_async_copy(turned, turned_out, ready.at[2])
+        send.start()
+        send.wait()
 
 
 def edge_kernel(
@@ -862,36 +840,47 @@
     ]
 
 
-def westward(edge):
+def west_edge(step, column, north, south, after, before):
+    levels, tracers, cells = after.shape
+    edge = pl.pallas_call(
+        functools.partial(edge_kernel, step),
+        out_shape=resident(*column.shape),
+        in_specs=[vmem()] * 3 + [anywhere()] * 2,
+        out_specs=vmem(),
+        scratch_shapes=[
+            pltpu.VMEM((levels, tracers, LANES), F32),
+            pltpu.VMEM((levels, tracers, LANES), F32),
+            pltpu.SemaphoreType.DMA((2,)),
+        ],
+        compiler_params=params(4),
+        name="edge",
+    )(column, north, south, after, before)
     count = lax.axis_size("lon")
     return held(lax.ppermute(edge, "lon", [(i, (i - 1) % count) for i in range(count)]))
 
 
-def first_exchange(step, after, before, nearby, polar, column, north, south, shift):
+def first_exchange(step, first, last, nearby, polar, column, north, south, shift):
     poles = (0, lax.axis_size("lat") - 1)
-    levels, tracers, cells = after.shape
-    edge, turned, *hops = pl.pallas_call(
-        functools.partial(borders_kernel, step),
+    levels, tracers, cells = first.shape
+    after, before = boundary_rows(first, last)
+    turned, *hops = pl.pallas_call(
+        functools.partial(turn_kernel, step),
         out_shape=[
-            resident(*column.shape),
             pltpu.HBM((levels, tracers, cells), F32),
             jax.ShapeDtypeStruct((1, 1), jnp.int32),
             jax.ShapeDtypeStruct((1, 1), jnp.int32),
         ],
-        in_specs=[smem()] + [vmem()] * 3 + [anywhere()] * 4,
-        out_specs=[vmem(), hbm(), smem(), smem()],
+        in_specs=[smem()] + [anywhere()] * 2,
+        out_specs=[hbm(), smem(), smem()],
         scratch_shapes=[
-            pltpu.VMEM((levels, tracers, LANES), F32),
-            pltpu.VMEM((levels, tracers, LANES), F32),
             pltpu.VMEM(polar.shape, F32),
             pltpu.VMEM(polar.shape, F32),
             pltpu.VMEM((levels, tracers, cells), F32),
-            pltpu.SemaphoreType.DMA((5,)),
+            pltpu.SemaphoreType.DMA((3,)),
         ],
         compiler_params=params(8),
-        name="borders",
-    )(shift, column, north, south, after, before, pinned(polar), nearby)
-    edge = westward(edge)
+        name="turn",
+    )(shift, pinned(polar), nearby)
     moved = []
     for lat, hop in zip(poles, hops):
         moved.append(
@@ -906,6 +895,8 @@
                 turned,
             )
         )
+    after, before, *moved = lax.optimization_barrier((after, before, *moved))
+    edge = west_edge(step, column, north, south, after, before)
     return after, before, pinned(moved[0]), pinned(moved[1]), edge
 
 
@@ -928,20 +919,7 @@
         name="rotate",
     )(shift, circle)
     pole = lax.all_to_all(turned, "lon", 0, 0, tiled=True)
-    edge = pl.pallas_call(
-        functools.partial(edge_kernel, step),
-        out_shape=resident(*column.shape),
-        in_specs=[vmem()] * 3 + [anywhere()] * 2,
-        out_specs=vmem(),
-        scratch_shapes=[
-            pltpu.VMEM((levels, tracers, LANES), F32),
-            pltpu.VMEM((levels, tracers, LANES), F32),
-            pltpu.SemaphoreType.DMA((2,)),
-        ],
-        compiler_params=params(4),
-        name="edge",
-    )(column, north, south, after, before)
-    return after, before, pole, westward(edge)
+    return after, before, pole, west_edge(step, column, north, south, after, before)
 
 
 def per_device(
@@ -1000,14 +978,15 @@
     diffusion = held(diffusion)
     counts, column = lax.optimization_barrier((sounding_counts, column))
     nearby = lax.ppermute(polar, AXES, circles((0, lax.axis_size("lat") - 1), 1))
-    around = (*boundary_rows(first, last), nearby)
     sent = packed(counts, owner_rows, columns, kernels, misfits)
-    sent, *around = lax.optimization_barrier((sent, *around))
-    around = [pinned(x) for x in around]
+    sent, nearby = lax.optimization_barrier((sent, nearby))
+    nearby = pinned(nearby)
     got = lax.all_to_all(sent, AXES, 0, 0, tiled=True)
     shape = (levels, rows, tracers, cells)
     forced = forcing(1, got, shape, False)
-    around = first_exchange(1, *around, polar, column, *couplings[:2], polar_shift)
+    around = first_exchange(
+        1, first, last, nearby, polar, column, *couplings[:2], polar_shift
+    )
     scratch = [field, line, line]
     transfers = pltpu.SemaphoreType.DMA((4, groups // SPAN))
     solved, first, last, polar, column, surface = pl.pallas_call(
@@ -1033,11 +1012,13 @@
         compiler_params=params(20),
         name="middle",
     )(pinned(diffused), forced, *around, diffusion, *couplings)
-    around = (*boundary_rows(first, last), lax.all_to_all(polar, "lon", 0, 0, tiled=True))
+    circle = lax.all_to_all(polar, "lon", 0, 0, tiled=True)
     got, column = lax.optimization_barrier((got, column))
     forced = forcing(0, got, shape, True)
-    forced, *around = lax.optimization_barrier((forced, *around))
-    around = last_exchange(0, *around, column, *couplings[:2], polar_shift)
+    forced, first, last = lax.optimization_barrier((forced, first, last))
+    around = last_exchange(
+        0, *boundary_rows(first, last), circle, column, *couplings[:2], polar_shift
+    )
     return tuple(
         pl.pallas_call(
             functools.partial(last_kernel, 0),

time: 130 us -> 133 us (1.023); the launches traced: 129 us -> 130 us
  starting transfers between devices: 44.1 us -> 63.3 us
  waiting for transfers between devices: 21 us -> 10.2 us
  Pallas kernels: 59.7 us -> 53.1 us
  local copies, waits for them, and re-layouts: 2.34 us -> 0.98 us
    ppermute x2, waiting for transfers between devices: 15.4 us -> 0.01 us  [first_exchange(): lax.ppermute(x, AXES, circles((lat,), k))]
    ppermute x4, starting transfers between devices: 8.7 us -> 21.2 us  [boundary_rows(): return (lax.ppermute(first, 'lat', down), lax.ppermute(last, 'lat', up))]
    pallas_call x2, Pallas kernels: 21.4 us -> 12.3 us  [forcing(): pl.pallas_call(functools.partial(streamed_forcing_kernel if streamed else...]
    ppermute x2, waiting for transfers between devices: 2.24 us -> 7.86 us  [west_edge(): lax.ppermute(edge, 'lon', [(i, (i - 1) % count) for i in range(count)])]
    ppermute x2, starting transfers between devices: 3.71 us -> 7.44 us  [first_exchange(): lax.ppermute(x, AXES, circles((lat,), k))]
    all_to_all x1, starting transfers between devices: 3.55 us -> 5.68 us  [per_device(): circle = lax.all_to_all(polar, 'lon', 0, 0, tiled=True)]
    ppermute x1, waiting for transfers between devices: 2.5 us -> 0.61 us  [per_device(): lax.ppermute(polar, AXES, circles((0, lax.axis_size('lat') - 1), 1))]
    pallas_call x2 -> x3, Pallas kernels: 5.37 us -> 7.13 us  [the longest x1 4.38 us: first_exchange(): pl.pallas_call(functools.partial(turn_kernel, step), out_shape=[pltpu.HBM...]
  transfers between devices with their start and end apart: 12 -> 12, of which waited for: 4 -> 4; matrix products, arithmetic and copies ran while one was open for 0% -> 0% of each run, Pallas kernels for 26% -> 23%
where the time goes in v5:
time: 133 us; the launch traced here: 130 us
  starting transfers between devices  63.3 us (48%)
  Pallas kernels  53.1 us (40%)
  waiting for transfers between devices  10.2 us (8%)
  between operations  2.36 us (2%)
    ppermute x4, starting transfers between devices, boundary_rows(): return (lax.ppermute(first, 'lat', down), lax.ppermute(last, 'lat', up))  21.2 us
    pallas_call x2, Pallas kernels, forcing(): pl.pallas_call(functools.partial(streamed_forcing_kernel if streamed else...  12.3 us
    all_to_all x1, starting transfers between devices, per_device(): got = lax.all_to_all(sent, AXES, 0, 0, tiled=True)  8.52 us
    pallas_call x1, Pallas kernels, per_device(): pl.pallas_call(functools.partial(middle_kernel, 1), out_shape=[*solved_sh...  8.24 us
    ppermute x2, starting transfers between devices, west_edge(): lax.ppermute(edge, 'lon', [(i, (i - 1) % count) for i in range(count)])  8.06 us
    ppermute x2, waiting for transfers between devices, west_edge(): lax.ppermute(edge, 'lon', [(i, (i - 1) % count) for i in range(count)])  7.86 us
    pallas_call x1, Pallas kernels, per_device(): pl.pallas_call(functools.partial(last_kernel, 0), out_shape=[pltpu.HBM(co...  7.76 us
    pallas_call x1, Pallas kernels, per_device(): pl.pallas_call(functools.partial(first_kernel, 1), out_shape=solved_shape...  7.7 us
  transfers between devices with their start and end apart: 12, of which 4 were waited for; matrix products, arithmetic and copies ran while one was open for 0% of the time, Pallas kernels for 23%

profile of v5, /device:TPU:0, one launch (start us, length us, event | category | flops | bytes accessed | tf_op | source)
XLA Modules:
  0.0 130.0 jit_solution(7792482979553573122)
XLA Ops:
  0.7 7.7 %first.1 = (f32[72,8,8,256]{3,2,1,0:T(8,128)}, f32[72,8,256]{2,1,0:T(8,128)}, f32[72,8,256]{2,1,0:T(8,128)}, f32[73,8,256]{2,1,0:T(8,128)}, f32[9,8,128]{2,1,0:T(8,128)S(1)}) custom-call(f32[72,8,8,256]{3,2,1,0:T(8,128)} %costate.1, f32[2,71,8,256]{3,2,1,0:T(8,128)} %diffusion.1, f32[2,8,256]{2,1,0:T(8,128)} %north.7, f32[2,8,256]{2,1,0:T(8,128)} %south.7, ...), custom_call_target="tpu_custom_call" | custom-call | tf_op jit(solution)/shard_map/first/pallas_call | solution.py:959
  8.4 0.0 copy-start.2
  8.4 7.0 %collective-permute-start.16 = (f32[73,8,256]{2,1,0:T(8,128)}, f32[73,8,256]{2,1,0:T(8,128)S(1)}, u32[]{:S(2)}, u32[]{:S(2)}) collective-permute-start(f32[73,8,256]{2,1,0:T(8,128)} %get-tuple-element.66.polar_in), channel_id=1, source_target_pairs={{16,0},{32,16},{48,32},{64,48},{80,64},{96,80},{112,96},{0,112},{3... | collective-permute-start | bytes 1794056 | tf_op jit(solution)/shard_map/ppermute | solution.py:980
  15.5 0.1 copy.13.counts
  15.6 7.0 %pack.1 = f32[128,24,128]{2,1,0:T(8,128)} custom-call(s32[2,1]{1,0:T(2,128)S(1)} %copy.13.counts, s32[2,1,1280]{2,1,0:T(1,128)S(1)} %bitcast.3, s32[2,1280]{1,0:T(2,128)S(1)} %copy-done.7, f32[2,72,1280]{2,1,0:T(8,128)S(1)} %copy-done.1, f32[2,8,1280]{2,1,0:T(8,128)S(1)} %copy-done.5), custom_call_target="tpu_custom_call" | custom-call | tf_op jit(solution)/shard_map/pack/pallas_call | solution.py:177
  22.6 0.6 collective-permute-done.16.nearby_in
  23.3 0.8 copy-done.9
  24.1 8.5 %all-to-all-start = ((f32[128,24,128]{2,1,0:T(8,128)}), f32[128,24,128]{2,1,0:T(8,128)S(1)}, u32[]{:S(2)}, u32[]{:S(2)}) async-start(f32[128,24,128]{2,1,0:T(8,128)} %pack.1), calls=%async_computation | async-start | bytes 3145728 | tf_op jit(solution)/shard_map/all_to_all | solution.py:984
  32.6 0.0 copy-start
  32.6 1.4 %collective-permute-start.17 = (f32[72,8,256]{2,1,0:T(8,128)}, f32[72,8,256]{2,1,0:T(8,128)S(1)}, u32[]{:S(2)}, u32[]{:S(2)}) collective-permute-start(f32[72,8,256]{2,1,0:T(8,128)} %get-tuple-element.68), channel_id=1, source_target_pairs={{1,0},{2,1},{3,2},{4,3},{5,4},{6,5},{7,6},{8,7},{9,8},{10,9},{11,1... | collective-permute-start | bytes 1769480 | tf_op jit(solution)/shard_map/ppermute | solution.py:830
  34.1 3.9 %collective-permute-start.18 = (f32[72,8,256]{2,1,0:T(8,128)}, f32[72,8,256]{2,1,0:T(8,128)}, u32[]{:S(2)}, u32[]{:S(2)}) collective-permute-start(f32[72,8,256]{2,1,0:T(8,128)} %get-tuple-element.69), channel_id=1, source_target_pairs={{0,1},{1,2},{2,3},{3,4},{4,5},{5,6},{6,7},{7,8},{8,9},{9,10},{10,1... | collective-permute-start | bytes 1769480 | tf_op jit(solution)/shard_map/ppermute | solution.py:830
  38.0 4.4 %turn.1 = (f32[72,8,256]{2,1,0:T(8,128)}, s32[1,1]{1,0:T(1,128)}, s32[1,1]{1,0:T(1,128)}) custom-call(s32[2,128]{1,0:T(2,128)S(1)} %copy-done.8, f32[73,8,256]{2,1,0:T(8,128)} %get-tuple-element.66.polar_in, f32[73,8,256]{2,1,0:T(8,128)} %copy-done.9), custom_call_target="tpu_custom_call" | custom-call | tf_op jit(solution)/shard_map/turn/pallas_call | solution.py:866
  43.6 1.5 %conditional.3 = (f32[72,8,256]{2,1,0:T(8,128)}) conditional(s32[]{:T(128)} %bitcast.2, f32[72,8,256]{2,1,0:T(8,128)} %get-tuple-element.72, f32[72,8,256]{2,1,0:T(8,128)} %get-tuple-element.72, f32[72,8,256]{2,1,0:T(8,128)} %get-tuple-element.72, f32[72,8,256]{2,1,0:T(8,128)} %get-tuple-element.72, ...), branch_computations={%region_8.0_spmd, %region_9.0_spmd, %region_10.0_spmd, %region_11.... | conditional | bytes 2359344 | solution.py:887
  43.6 1.5 %collective-permute-start.12 = (f32[72,8,256]{2,1,0:T(8,128)}, f32[72,8,256]{2,1,0:T(8,128)}, u32[]{:S(2)}, u32[]{:S(2)}) collective-permute-start(f32[72,8,256]{2,1,0:T(8,128)} %param.12), channel_id=1, source_target_pairs={{79,15},{95,31},{111,47},{127,63},{15,79},{31,95},{47,111},{63,127}} | collective-permute-start | bytes 1769480 | tf_op jit(solution)/shard_map/cond/branch_4_fun/ppermute | solution.py:891
  45.1 5.9 %conditional.2 = (f32[72,8,256]{2,1,0:T(8,128)}) conditional(s32[]{:T(128)} %bitcast.1, f32[72,8,256]{2,1,0:T(8,128)} %get-tuple-element.72, f32[72,8,256]{2,1,0:T(8,128)} %get-tuple-element.72, f32[72,8,256]{2,1,0:T(8,128)} %get-tuple-element.72, f32[72,8,256]{2,1,0:T(8,128)} %get-tuple-element.72, ...), branch_computations={%region_0.0_spmd, %region_1.0_spmd, %region_2.0_spmd, %region_3.0_... | conditional | bytes 2359344 | solution.py:887
  45.1 5.9 %collective-permute-start = (f32[72,8,256]{2,1,0:T(8,128)}, f32[72,8,256]{2,1,0:T(8,128)}, u32[]{:S(2)}, u32[]{:S(2)}) collective-permute-start(f32[72,8,256]{2,1,0:T(8,128)} %param), channel_id=1, source_target_pairs={{0,0},{16,16},{32,32},{48,48},{64,64},{80,80},{96,96},{112,112}} | collective-permute-start | bytes 1769480 | tf_op jit(solution)/shard_map/cond/branch_0_fun/ppermute | solution.py:891
  51.1 1.8 %edge.2 = f32[9,8,128]{2,1,0:T(8,128)S(1)} custom-call(f32[9,8,128]{2,1,0:T(8,128)S(1)} %get-tuple-element.78.column, f32[2,8,256]{2,1,0:T(8,128)S(1)} %copy-done.2, f32[2,8,256]{2,1,0:T(8,128)S(1)} %copy-done.3, f32[72,8,256]{2,1,0:T(8,128)S(1)} %collective-permute-done.17.after_in, f32[72,8,256]{2,1,0:T(8,128)} %collective-permute-done.18.before_in), custom_call_target="tpu_custom_call" | custom-call | tf_op jit(solution)/shard_map/edge/pallas_call | solution.py:845
  52.9 3.9 %collective-permute-start.19 = (f32[9,8,128]{2,1,0:T(8,128)S(1)}, f32[9,8,128]{2,1,0:T(8,128)S(1)}, u32[]{:S(2)}, u32[]{:S(2)}) collective-permute-start(f32[9,8,128]{2,1,0:T(8,128)S(1)} %edge.2), channel_id=1, source_target_pairs={{0,112},{16,0},{32,16},{48,32},{64,48},{80,64},{96,80},{112,96},{1... | collective-permute-start | bytes 110600 | tf_op jit(solution)/shard_map/ppermute | solution.py:859
  56.8 1.0 all-to-all-done.received
  57.9 5.5 %forcing.2.forced = f32[72,8,8,256]{3,2,1,0:T(8,128)S(1)} custom-call(f32[128,24,128]{2,1,0:T(8,128)S(1)} %all-to-all-done.received), custom_call_target="tpu_custom_call" | custom-call | tf_op jit(solution)/shard_map/forcing/pallas_call | solution.py:303
  63.4 8.2 %middle.1 = (f32[72,8,8,256]{3,2,1,0:T(8,128)}, f32[72,8,256]{2,1,0:T(8,128)}, f32[72,8,256]{2,1,0:T(8,128)}, f32[8,10,8,256]{3,2,1,0:T(8,128)}, f32[9,8,128]{2,1,0:T(8,128)S(1)}, /*index=5*/f32[8,8,256]{2,1,0:T(8,128)S(1)}) custom-call(f32[72,8,8,256]{3,2,1,0:T(8,128)} %get-tuple-element.63.before_step, f32[72,8,8,256]{3,2,1,0:T(8,128)S(1)} %forcing.2.forced, ...), custom_call_target="tpu_custom_call" | custom-call | tf_op jit(solution)/shard_map/middle/pallas_call | solution.py:992
  71.7 5.7 %all-to-all-start.1 = ((f32[8,10,8,256]{3,2,1,0:T(8,128)}), f32[8,10,8,256]{3,2,1,0:T(8,128)S(1)}, u32[]{:S(2)}, u32[]{:S(2)}) async-start(f32[8,10,8,256]{3,2,1,0:T(8,128)} %get-tuple-element.87), calls=%async_computation.1 | async-start | bytes 1310720 | tf_op jit(solution)/shard_map/all_to_all | solution.py:1015
  77.3 6.8 %forcing.3.forcing_in = f32[72,8,8,256]{3,2,1,0:T(8,128)} custom-call(f32[128,24,128]{2,1,0:T(8,128)S(1)} %all-to-all-done.received), custom_call_target="tpu_custom_call" | custom-call | tf_op jit(solution)/shard_map/forcing/pallas_call | solution.py:303
  84.1 1.3 collective-permute-start.20
  85.4 14.6 %collective-permute-start.21 = (f32[72,8,256]{2,1,0:T(8,128)S(1)}, f32[72,8,256]{2,1,0:T(8,128)S(1)}, u32[]{:S(2)}, u32[]{:S(2)}) collective-permute-start(f32[72,8,256]{2,1,0:T(8,128)S(1)} %copy-done.10), channel_id=1, source_target_pairs={{0,1},{1,2},{2,3},{3,4},{4,5},{5,6},{6,7},{7,8},{8,9},{9,10},{10,1... | collective-permute-start | bytes 1769480 | tf_op jit(solution)/shard_map/ppermute | solution.py:830
  100.0 3.0 %rotate.1 = f32[8,9,8,256]{3,2,1,0:T(8,128)} custom-call(s32[2,128]{1,0:T(2,128)S(1)} %copy-done.8, f32[8,10,8,256]{3,2,1,0:T(8,128)S(1)} %all-to-all-done.1.circle_in), custom_call_target="tpu_custom_call" | custom-call | tf_op jit(solution)/shard_map/rotate/pallas_call | solution.py:907
  103.0 5.4 %all-to-all-start.2 = ((f32[8,9,8,256]{3,2,1,0:T(8,128)}), f32[8,9,8,256]{3,2,1,0:T(8,128)S(1)}, u32[]{:S(2)}, u32[]{:S(2)}) async-start(f32[8,9,8,256]{3,2,1,0:T(8,128)} %rotate.1), calls=%async_computation.2 | async-start | bytes 1179648 | tf_op jit(solution)/shard_map/all_to_all | solution.py:921
  108.4 0.9 edge.3
  109.4 4.2 %collective-permute-start.22 = (f32[9,8,128]{2,1,0:T(8,128)S(1)}, f32[9,8,128]{2,1,0:T(8,128)S(1)}, u32[]{:S(2)}, u32[]{:S(2)}) collective-permute-start(f32[9,8,128]{2,1,0:T(8,128)S(1)} %edge.3), channel_id=1, source_target_pairs={{0,112},{16,0},{32,16},{48,32},{64,48},{80,64},{96,80},{112,96},{1... | collective-permute-start | bytes 110600 | tf_op jit(solution)/shard_map/ppermute | solution.py:859
  113.5 7.9 %collective-permute-done.22.edge = f32[9,8,128]{2,1,0:T(8,128)S(1)} collective-permute-done((f32[9,8,128]{2,1,0:T(8,128)S(1)}, f32[9,8,128]{2,1,0:T(8,128)S(1)}, u32[]{:S(2)}, u32[]{:S(2)}) %collective-permute-start.22) | collective-permute-done | bytes 36896 | tf_op jit(solution)/shard_map/ppermute | solution.py:859
  121.4 0.6 all-to-all-done.2.pole_in
  122.1 7.8 %last.1 = (f32[72,8,8,256]{3,2,1,0:T(8,128)}, f32[8,8,256]{2,1,0:T(8,128)}) custom-call(f32[72,8,8,256]{3,2,1,0:T(8,128)} %get-tuple-element.79.before_step, f32[72,8,8,256]{3,2,1,0:T(8,128)} %forcing.3.forcing_in, f32[72,8,256]{2,1,0:T(8,128)S(1)} %collective-permute-done.20.after_in, f32[72,8,256]{2,1,0:T(8,128)S(1)} %collective-permute-done.21.before_in, ...), custom_call_target="tpu_custom_call" | custom-call | tf_op jit(solution)/shard_map/last/pallas_call | solution.py:1023
  (29 shorter events, 0.1 us)
Async XLA Ops:
  0.6 14.8 %copy-start.11 = (s32[2,1]{0,1:T(1,128)S(1)}, s32[2,1]{0,1:T(1,128)}, u32[]{:S(2)}) copy-start(s32[2,1]{0,1:T(1,128)} %param.35) | copy-start | bytes 28
  0.6 14.9 %copy-start.5 = (f32[2,8,1280]{2,1,0:T(8,128)S(1)}, f32[2,8,1280]{2,1,0:T(8,128)}, u32[]{:S(2)}) copy-start(f32[2,8,1280]{2,1,0:T(8,128)} %misfits.1) | copy-start | bytes 245764
  0.7 14.9 %copy-start.1 = (f32[2,72,1280]{2,1,0:T(8,128)S(1)}, f32[2,72,1280]{2,1,0:T(8,128)}, u32[]{:S(2)}) copy-start(f32[2,72,1280]{2,1,0:T(8,128)} %kernels.1) | copy-start | bytes 2211844
  0.7 14.9 %copy-start.7 = (s32[2,1280]{1,0:T(2,128)S(1)}, s32[2,1280]{1,0:T(2,128)}, u32[]{:S(2)}) copy-start(s32[2,1280]{1,0:T(2,128)} %columns.1) | copy-start | bytes 30724
  0.7 14.9 %copy-start.6 = (s32[2,1280,1]{1,2,0:T(1,128)S(1)}, s32[2,1280,1]{1,2,0:T(1,128)}, u32[]{:S(2)}) copy-start(s32[2,1280,1]{1,2,0:T(1,128)} %param.33) | copy-start | bytes 30724
  0.7 37.3 %copy-start.8 = (s32[2,128]{1,0:T(2,128)S(1)}, s32[2,128]{1,0:T(2,128)}, u32[]{:S(2)}) copy-start(s32[2,128]{1,0:T(2,128)} %shift.3) | copy-start | bytes 3076
  8.4 42.7 %copy-start.2 = (f32[2,8,256]{2,1,0:T(8,128)S(1)}, f32[2,8,256]{2,1,0:T(8,128)}, u32[]{:S(2)}) copy-start(f32[2,8,256]{2,1,0:T(8,128)} %north.7) | copy-start | bytes 49156
  8.4 42.7 %copy-start.3 = (f32[2,8,256]{2,1,0:T(8,128)S(1)}, f32[2,8,256]{2,1,0:T(8,128)}, u32[]{:S(2)}) copy-start(f32[2,8,256]{2,1,0:T(8,128)} %south.7) | copy-start | bytes 49156
  8.4 14.8 %collective-permute-start.16 = (f32[73,8,256]{2,1,0:T(8,128)}, f32[73,8,256]{2,1,0:T(8,128)S(1)}, u32[]{:S(2)}, u32[]{:S(2)}) collective-permute-start(f32[73,8,256]{2,1,0:T(8,128)} %get-tuple-element.66.polar_in), channel_id=1, source_target_pairs={{16,0},{32,16},{48,32},{64,48},{80,64},{96,80},{112,96},{0,112},{3... | collective-permute-start | bytes 1794056 | tf_op jit(solution)/shard_map/ppermute | solution.py:980
  23.3 0.8 copy-start.9
  24.1 33.8 %all-to-all-start = ((f32[128,24,128]{2,1,0:T(8,128)}), f32[128,24,128]{2,1,0:T(8,128)S(1)}, u32[]{:S(2)}, u32[]{:S(2)}) async-start(f32[128,24,128]{2,1,0:T(8,128)} %pack.1), calls=%async_computation | async-start | bytes 3145728 | tf_op jit(solution)/shard_map/all_to_all | solution.py:984
  32.6 30.8 %copy-start = (f32[2,71,8,256]{3,2,1,0:T(8,128)S(1)}, f32[2,71,8,256]{3,2,1,0:T(8,128)}, u32[]{:S(2)}) copy-start(f32[2,71,8,256]{3,2,1,0:T(8,128)} %diffusion.1) | copy-start | bytes 3489796
  32.6 30.8 %copy-start.4 = (f32[2,8,256]{2,1,0:T(8,128)S(1)}, f32[2,8,256]{2,1,0:T(8,128)}, u32[]{:S(2)}) copy-start(f32[2,8,256]{2,1,0:T(8,128)} %east.3) | copy-start | bytes 49156
  32.6 18.5 %collective-permute-start.17 = (f32[72,8,256]{2,1,0:T(8,128)}, f32[72,8,256]{2,1,0:T(8,128)S(1)}, u32[]{:S(2)}, u32[]{:S(2)}) collective-permute-start(f32[72,8,256]{2,1,0:T(8,128)} %get-tuple-element.68), channel_id=1, source_target_pairs={{1,0},{2,1},{3,2},{4,3},{5,4},{6,5},{7,6},{8,7},{9,8},{10,9},{11,1... | collective-permute-start | bytes 1769480 | tf_op jit(solution)/shard_map/ppermute | solution.py:830
  34.1 17.0 %collective-permute-start.18 = (f32[72,8,256]{2,1,0:T(8,128)}, f32[72,8,256]{2,1,0:T(8,128)}, u32[]{:S(2)}, u32[]{:S(2)}) collective-permute-start(f32[72,8,256]{2,1,0:T(8,128)} %get-tuple-element.69), channel_id=1, source_target_pairs={{0,1},{1,2},{2,3},{3,4},{4,5},{5,6},{6,7},{7,8},{8,9},{9,10},{10,1... | collective-permute-start | bytes 1769480 | tf_op jit(solution)/shard_map/ppermute | solution.py:830
  43.6 1.5 %collective-permute-start.12 = (f32[72,8,256]{2,1,0:T(8,128)}, f32[72,8,256]{2,1,0:T(8,128)}, u32[]{:S(2)}, u32[]{:S(2)}) collective-permute-start(f32[72,8,256]{2,1,0:T(8,128)} %param.12), channel_id=1, source_target_pairs={{79,15},{95,31},{111,47},{127,63},{15,79},{31,95},{47,111},{63,127}} | collective-permute-start | bytes 1769480 | tf_op jit(solution)/shard_map/cond/branch_4_fun/ppermute | solution.py:891
  45.1 5.9 %collective-permute-start = (f32[72,8,256]{2,1,0:T(8,128)}, f32[72,8,256]{2,1,0:T(8,128)}, u32[]{:S(2)}, u32[]{:S(2)}) collective-permute-start(f32[72,8,256]{2,1,0:T(8,128)} %param), channel_id=1, source_target_pairs={{0,0},{16,16},{32,32},{48,48},{64,64},{80,80},{96,96},{112,112}} | collective-permute-start | bytes 1769480 | tf_op jit(solution)/shard_map/cond/branch_0_fun/ppermute | solution.py:891
  52.9 10.4 %collective-permute-start.19 = (f32[9,8,128]{2,1,0:T(8,128)S(1)}, f32[9,8,128]{2,1,0:T(8,128)S(1)}, u32[]{:S(2)}, u32[]{:S(2)}) collective-permute-start(f32[9,8,128]{2,1,0:T(8,128)S(1)} %edge.2), channel_id=1, source_target_pairs={{0,112},{16,0},{32,16},{48,32},{64,48},{80,64},{96,80},{112,96},{1... | collective-permute-start | bytes 110600 | tf_op jit(solution)/shard_map/ppermute | solution.py:859
  71.6 13.8 %copy-start.10 = (f32[72,8,256]{2,1,0:T(8,128)S(1)}, f32[72,8,256]{2,1,0:T(8,128)}, u32[]{:S(2)}) copy-start(f32[72,8,256]{2,1,0:T(8,128)} %get-tuple-element.86) | copy-start | bytes 1769476
  71.7 28.4 %all-to-all-start.1 = ((f32[8,10,8,256]{3,2,1,0:T(8,128)}), f32[8,10,8,256]{3,2,1,0:T(8,128)S(1)}, u32[]{:S(2)}, u32[]{:S(2)}) async-start(f32[8,10,8,256]{3,2,1,0:T(8,128)} %get-tuple-element.87), calls=%async_computation.1 | async-start | bytes 1310720 | tf_op jit(solution)/shard_map/all_to_all | solution.py:1015
  84.1 24.3 %collective-permute-start.20 = (f32[72,8,256]{2,1,0:T(8,128)}, f32[72,8,256]{2,1,0:T(8,128)S(1)}, u32[]{:S(2)}, u32[]{:S(2)}) collective-permute-start(f32[72,8,256]{2,1,0:T(8,128)} %get-tuple-element.85), channel_id=1, source_target_pairs={{1,0},{2,1},{3,2},{4,3},{5,4},{6,5},{7,6},{8,7},{9,8},{10,9},{11,1... | collective-permute-start | bytes 1769480 | tf_op jit(solution)/shard_map/ppermute | solution.py:830
  85.4 23.0 %collective-permute-start.21 = (f32[72,8,256]{2,1,0:T(8,128)S(1)}, f32[72,8,256]{2,1,0:T(8,128)S(1)}, u32[]{:S(2)}, u32[]{:S(2)}) collective-permute-start(f32[72,8,256]{2,1,0:T(8,128)S(1)} %copy-done.10), channel_id=1, source_target_pairs={{0,1},{1,2},{2,3},{3,4},{4,5},{5,6},{6,7},{7,8},{8,9},{9,10},{10,1... | collective-permute-start | bytes 1769480 | tf_op jit(solution)/shard_map/ppermute | solution.py:830
  103.0 19.0 %all-to-all-start.2 = ((f32[8,9,8,256]{3,2,1,0:T(8,128)}), f32[8,9,8,256]{3,2,1,0:T(8,128)S(1)}, u32[]{:S(2)}, u32[]{:S(2)}) async-start(f32[8,9,8,256]{3,2,1,0:T(8,128)} %rotate.1), calls=%async_computation.2 | async-start | bytes 1179648 | tf_op jit(solution)/shard_map/all_to_all | solution.py:921
  109.4 12.1 %collective-permute-start.22 = (f32[9,8,128]{2,1,0:T(8,128)S(1)}, f32[9,8,128]{2,1,0:T(8,128)S(1)}, u32[]{:S(2)}, u32[]{:S(2)}) collective-permute-start(f32[9,8,128]{2,1,0:T(8,128)S(1)} %edge.3), channel_id=1, source_target_pairs={{0,112},{16,0},{32,16},{48,32},{64,48},{80,64},{96,80},{112,96},{1... | collective-permute-start | bytes 110600 | tf_op jit(solution)/shard_map/ppermute | solution.py:859

commit v6 on v4

--- a/solution.py
+++ b/solution.py
@@ -256,15 +256,15 @@
         place[:, b * LANES : (b + 1) * LANES] = jnp.where(live, at, -1.0)
     counts = [jnp.max(filled[r : r + 1, :]).astype(jnp.int32) for r in range(rows)]
     used = sum(counts)
-    wide = 2 * LANES
+    wide = 4 * LANES
 
     def sort(i, carry):
-        hot = one_hot(place[...] - (i * wide).astype(F32), wide)
+        hot = tall_one_hot(place[...] - (i * wide).astype(F32), wide)
         both = dot(hot, fields[...])
         ordered[pl.ds(pl.multiple_of(i * wide, wide), wide), :] = both[:, :LANES] + both[:, LANES:]
         return carry
 
-    lax.fori_loop(0, (used + 1) // 2, sort, 0)
+    lax.fori_loop(0, (used + 3) // 4, sort, 0)
     out[...] = jnp.zeros_like(out)
     name = lax.broadcasted_iota(jnp.int32, (LANES, cells), 1).astype(F32)
     first = jnp.int32(0)
@@ -306,7 +306,7 @@
         in_specs=[vmem()],
         out_specs=hbm() if streamed else vmem(),
         scratch_shapes=scratch,
-        compiler_params=params(16 if streamed else 12),
+        compiler_params=params(20 if streamed else 16),
         name="forcing",
     )(held(received))
 
@@ -1033,11 +1033,13 @@
         compiler_params=params(20),
         name="middle",
     )(pinned(diffused), forced, *around, diffusion, *couplings)
-    around = (*boundary_rows(first, last), lax.all_to_all(polar, "lon", 0, 0, tiled=True))
+    circle = lax.all_to_all(polar, "lon", 0, 0, tiled=True)
     got, column = lax.optimization_barrier((got, column))
     forced = forcing(0, got, shape, True)
-    forced, *around = lax.optimization_barrier((forced, *around))
-    around = last_exchange(0, *around, column, *couplings[:2], polar_shift)
+    forced, first, last = lax.optimization_barrier((forced, first, last))
+    around = last_exchange(
+        0, *boundary_rows(first, last), circle, column, *couplings[:2], polar_shift
+    )
     return tuple(
         pl.pallas_call(
             functools.partial(last_kernel, 0),

time: 130 us -> 129 us (level); the launches traced: 129 us -> 127 us
  Pallas kernels: 59.7 us -> 50.7 us
  starting transfers between devices: 44.1 us -> 50.6 us
  local copies, waits for them, and re-layouts: 2.34 us -> 0.97 us
    pallas_call x2, Pallas kernels: 21.4 us -> 11.7 us  [forcing(): pl.pallas_call(functools.partial(streamed_forcing_kernel if streamed else...]
    all_to_all x1, starting transfers between devices: 4.48 us -> 10 us  [last_exchange(): pole = lax.all_to_all(turned, 'lon', 0, 0, tiled=True)]
    unnamed x30 -> x28, local copies, waits for them, and re-layouts: 2.25 us -> 0.87 us
  transfers between devices with their start and end apart: 12 -> 12, of which waited for: 4 -> 4; matrix products, arithmetic and copies ran while one was open for 0% -> 0% of each run, Pallas kernels for 26% -> 21%
where the time goes in v6:
time: 129 us; the launch traced here: 127 us
  Pallas kernels  50.7 us (39%)
  starting transfers between devices  50.6 us (39%)
  waiting for transfers between devices  22.1 us (17%)
  between operations  2.42 us (2%)
    ppermute x2, waiting for transfers between devices, first_exchange(): lax.ppermute(x, AXES, circles((lat,), k))  16.2 us
    pallas_call x2, Pallas kernels, forcing(): pl.pallas_call(functools.partial(streamed_forcing_kernel if streamed else...  11.7 us
    all_to_all x1, starting transfers between devices, last_exchange(): pole = lax.all_to_all(turned, 'lon', 0, 0, tiled=True)  10 us
    ppermute x4, starting transfers between devices, boundary_rows(): return (lax.ppermute(first, 'lat', down), lax.ppermute(last, 'lat', up))  8.72 us
    all_to_all x1, starting transfers between devices, per_device(): got = lax.all_to_all(sent, AXES, 0, 0, tiled=True)  8.52 us
    pallas_call x1, Pallas kernels, per_device(): pl.pallas_call(functools.partial(middle_kernel, 1), out_shape=[*solved_sh...  8.21 us
    ppermute x2, starting transfers between devices, westward(): lax.ppermute(edge, 'lon', [(i, (i - 1) % count) for i in range(count)])  8.06 us
    pallas_call x1, Pallas kernels, per_device(): pl.pallas_call(functools.partial(first_kernel, 1), out_shape=solved_shape...  7.81 us
  transfers between devices with their start and end apart: 12, of which 4 were waited for; matrix products, arithmetic and copies ran while one was open for 0% of the time, Pallas kernels for 21%

profile of v6, /device:TPU:0, one launch (start us, length us, event | category | flops | bytes accessed | tf_op | source)
XLA Modules:
  0.0 126.9 jit_solution(13223771739285725753)
XLA Ops:
  0.7 7.8 %first.1 = (f32[72,8,8,256]{3,2,1,0:T(8,128)}, f32[72,8,256]{2,1,0:T(8,128)}, f32[72,8,256]{2,1,0:T(8,128)}, f32[73,8,256]{2,1,0:T(8,128)}, f32[9,8,128]{2,1,0:T(8,128)S(1)}) custom-call(f32[72,8,8,256]{3,2,1,0:T(8,128)} %costate.1, f32[2,71,8,256]{3,2,1,0:T(8,128)} %diffusion.1, f32[2,8,256]{2,1,0:T(8,128)} %north.7, f32[2,8,256]{2,1,0:T(8,128)} %south.7, ...), custom_call_target="tpu_custom_call" | custom-call | tf_op jit(solution)/shard_map/first/pallas_call | solution.py:981
  8.5 7.0 %collective-permute-start.18 = (f32[73,8,256]{2,1,0:T(8,128)}, f32[73,8,256]{2,1,0:T(8,128)S(1)}, u32[]{:S(2)}, u32[]{:S(2)}) collective-permute-start(f32[73,8,256]{2,1,0:T(8,128)} %get-tuple-element.67.polar_in), channel_id=1, source_target_pairs={{16,0},{32,16},{48,32},{64,48},{80,64},{96,80},{112,96},{0,112},{3... | collective-permute-start | bytes 1794056 | tf_op jit(solution)/shard_map/ppermute | solution.py:1002
  15.6 1.3 %collective-permute-start.16 = (f32[72,8,256]{2,1,0:T(8,128)}, f32[72,8,256]{2,1,0:T(8,128)S(1)}, u32[]{:S(2)}, u32[]{:S(2)}) collective-permute-start(f32[72,8,256]{2,1,0:T(8,128)} %get-tuple-element.65), channel_id=1, source_target_pairs={{1,0},{2,1},{3,2},{4,3},{5,4},{6,5},{7,6},{8,7},{9,8},{10,9},{11,1... | collective-permute-start | bytes 1769480 | tf_op jit(solution)/shard_map/ppermute | solution.py:852
  16.9 3.1 %collective-permute-start.17 = (f32[72,8,256]{2,1,0:T(8,128)}, f32[72,8,256]{2,1,0:T(8,128)S(1)}, u32[]{:S(2)}, u32[]{:S(2)}) collective-permute-start(f32[72,8,256]{2,1,0:T(8,128)} %get-tuple-element.66), channel_id=1, source_target_pairs={{0,1},{1,2},{2,3},{3,4},{4,5},{5,6},{6,7},{7,8},{8,9},{9,10},{10,1... | collective-permute-start | bytes 1769480 | tf_op jit(solution)/shard_map/ppermute | solution.py:852
  20.0 0.1 copy.13.counts
  20.1 7.1 %pack.1 = f32[128,24,128]{2,1,0:T(8,128)} custom-call(s32[2,1]{1,0:T(2,128)S(1)} %copy.13.counts, s32[2,1,1280]{2,1,0:T(1,128)S(1)} %bitcast.3, s32[2,1280]{1,0:T(2,128)S(1)} %copy-done.7, f32[2,72,1280]{2,1,0:T(8,128)S(1)} %copy-done.1, f32[2,8,1280]{2,1,0:T(8,128)S(1)} %copy-done.5), custom_call_target="tpu_custom_call" | custom-call | tf_op jit(solution)/shard_map/pack/pallas_call | solution.py:177
  27.1 0.0 collective-permute-done.16.after_in
  27.2 2.5 %collective-permute-done.18.nearby_in = f32[73,8,256]{2,1,0:T(8,128)S(1)} collective-permute-done((f32[73,8,256]{2,1,0:T(8,128)}, f32[73,8,256]{2,1,0:T(8,128)S(1)}, u32[]{:S(2)}, u32[]{:S(2)}) %collective-permute-start.18) | collective-permute-done | bytes 598048 | tf_op jit(solution)/shard_map/ppermute | solution.py:1002
  29.7 0.8 copy-done.11
  30.5 8.5 %all-to-all-start = ((f32[128,24,128]{2,1,0:T(8,128)}), f32[128,24,128]{2,1,0:T(8,128)S(1)}, u32[]{:S(2)}, u32[]{:S(2)}) async-start(f32[128,24,128]{2,1,0:T(8,128)} %pack.1), calls=%async_computation | async-start | bytes 3145728 | tf_op jit(solution)/shard_map/all_to_all | solution.py:1007
  39.1 0.0 copy-start
  39.1 0.0 copy-start.4
  39.1 4.4 %borders.1 = (f32[9,8,128]{2,1,0:T(8,128)S(1)}, f32[72,8,256]{2,1,0:T(8,128)}, s32[1,1]{1,0:T(1,128)}, s32[1,1]{1,0:T(1,128)}) custom-call(s32[2,128]{1,0:T(2,128)S(1)} %copy-done.8, f32[9,8,128]{2,1,0:T(8,128)S(1)} %get-tuple-element.71.column, f32[2,8,256]{2,1,0:T(8,128)S(1)} %copy-done.2, f32[2,8,256]{2,1,0:T(8,128)S(1)} %copy-done.3, ...), custom_call_target="tpu_custom_call" | custom-call | tf_op jit(solution)/shard_map/borders/pallas_call | solution.py:873
  43.5 3.9 %collective-permute-start.19 = (f32[9,8,128]{2,1,0:T(8,128)S(1)}, f32[9,8,128]{2,1,0:T(8,128)S(1)}, u32[]{:S(2)}, u32[]{:S(2)}) collective-permute-start(f32[9,8,128]{2,1,0:T(8,128)S(1)} %get-tuple-element.76), channel_id=1, source_target_pairs={{0,112},{16,0},{32,16},{48,32},{64,48},{80,64},{96,80},{112,96},{1... | collective-permute-start | bytes 110600 | tf_op jit(solution)/shard_map/ppermute | solution.py:867
  48.7 1.5 %conditional.3 = (f32[72,8,256]{2,1,0:T(8,128)}) conditional(s32[]{:T(128)} %bitcast.2, f32[72,8,256]{2,1,0:T(8,128)} %get-tuple-element.74, f32[72,8,256]{2,1,0:T(8,128)} %get-tuple-element.74, f32[72,8,256]{2,1,0:T(8,128)} %get-tuple-element.74, f32[72,8,256]{2,1,0:T(8,128)} %get-tuple-element.74, ...), branch_computations={%region_8.0_spmd, %region_9.0_spmd, %region_10.0_spmd, %region_11.... | conditional | bytes 2359344 | solution.py:898
  48.7 1.5 %collective-permute-start.12 = (f32[72,8,256]{2,1,0:T(8,128)}, f32[72,8,256]{2,1,0:T(8,128)}, u32[]{:S(2)}, u32[]{:S(2)}) collective-permute-start(f32[72,8,256]{2,1,0:T(8,128)} %param.12), channel_id=1, source_target_pairs={{79,15},{95,31},{111,47},{127,63},{15,79},{31,95},{47,111},{63,127}} | collective-permute-start | bytes 1769480 | tf_op jit(solution)/shard_map/cond/branch_4_fun/ppermute | solution.py:902
  50.2 18.1 %conditional.2 = (f32[72,8,256]{2,1,0:T(8,128)}) conditional(s32[]{:T(128)} %bitcast.1, f32[72,8,256]{2,1,0:T(8,128)} %get-tuple-element.74, f32[72,8,256]{2,1,0:T(8,128)} %get-tuple-element.74, f32[72,8,256]{2,1,0:T(8,128)} %get-tuple-element.74, f32[72,8,256]{2,1,0:T(8,128)} %get-tuple-element.74, ...), branch_computations={%region_0.0_spmd, %region_1.0_spmd, %region_2.0_spmd, %region_3.0_... | conditional | bytes 2359344 | solution.py:898
  50.2 1.9 %collective-permute-start.7 = (f32[72,8,256]{2,1,0:T(8,128)}, f32[72,8,256]{2,1,0:T(8,128)}, u32[]{:S(2)}, u32[]{:S(2)}) collective-permute-start(f32[72,8,256]{2,1,0:T(8,128)} %param.7), channel_id=1, source_target_pairs={{112,0},{0,16},{16,32},{32,48},{48,64},{64,80},{80,96},{96,112}} | collective-permute-start | bytes 1769480 | tf_op jit(solution)/shard_map/cond/branch_7_fun/ppermute | solution.py:902
  52.1 16.2 %collective-permute-done.7 = f32[72,8,256]{2,1,0:T(8,128)} collective-permute-done((f32[72,8,256]{2,1,0:T(8,128)}, f32[72,8,256]{2,1,0:T(8,128)}, u32[]{:S(2)}, u32[]{:S(2)}) %collective-permute-start.7) | collective-permute-done | bytes 589856 | tf_op jit(solution)/shard_map/cond/branch_7_fun/ppermute | solution.py:902
  68.3 5.2 %forcing.2.forced = f32[72,8,8,256]{3,2,1,0:T(8,128)S(1)} custom-call(f32[128,24,128]{2,1,0:T(8,128)S(1)} %all-to-all-done.received), custom_call_target="tpu_custom_call" | custom-call | tf_op jit(solution)/shard_map/forcing/pallas_call | solution.py:303
  73.5 8.2 %middle.1 = (f32[72,8,8,256]{3,2,1,0:T(8,128)}, f32[72,8,256]{2,1,0:T(8,128)}, f32[72,8,256]{2,1,0:T(8,128)}, f32[8,10,8,256]{3,2,1,0:T(8,128)}, f32[9,8,128]{2,1,0:T(8,128)S(1)}, /*index=5*/f32[8,8,256]{2,1,0:T(8,128)S(1)}) custom-call(f32[72,8,8,256]{3,2,1,0:T(8,128)} %get-tuple-element.62.before_step, f32[72,8,8,256]{3,2,1,0:T(8,128)S(1)} %forcing.2.forced, ...), custom_call_target="tpu_custom_call" | custom-call | tf_op jit(solution)/shard_map/middle/pallas_call | solution.py:1013
  81.8 4.8 %all-to-all-start.1 = ((f32[8,10,8,256]{3,2,1,0:T(8,128)}), f32[8,10,8,256]{3,2,1,0:T(8,128)S(1)}, u32[]{:S(2)}, u32[]{:S(2)}) async-start(f32[8,10,8,256]{3,2,1,0:T(8,128)} %get-tuple-element.85), calls=%async_computation.1 | async-start | bytes 1310720 | tf_op jit(solution)/shard_map/all_to_all | solution.py:1036
  86.6 6.5 %forcing.3.forcing_in = f32[72,8,8,256]{3,2,1,0:T(8,128)} custom-call(f32[128,24,128]{2,1,0:T(8,128)S(1)} %all-to-all-done.received), custom_call_target="tpu_custom_call" | custom-call | tf_op jit(solution)/shard_map/forcing/pallas_call | solution.py:303
  93.1 1.3 %collective-permute-start.20 = (f32[72,8,256]{2,1,0:T(8,128)}, f32[72,8,256]{2,1,0:T(8,128)S(1)}, u32[]{:S(2)}, u32[]{:S(2)}) collective-permute-start(f32[72,8,256]{2,1,0:T(8,128)} %get-tuple-element.83), channel_id=1, source_target_pairs={{1,0},{2,1},{3,2},{4,3},{5,4},{6,5},{7,6},{8,7},{9,8},{10,9},{11,1... | collective-permute-start | bytes 1769480 | tf_op jit(solution)/shard_map/ppermute | solution.py:852
  94.4 3.1 %collective-permute-start.21 = (f32[72,8,256]{2,1,0:T(8,128)S(1)}, f32[72,8,256]{2,1,0:T(8,128)S(1)}, u32[]{:S(2)}, u32[]{:S(2)}) collective-permute-start(f32[72,8,256]{2,1,0:T(8,128)S(1)} %copy-done.12), channel_id=1, source_target_pairs={{0,1},{1,2},{2,3},{3,4},{4,5},{5,6},{6,7},{7,8},{8,9},{9,10},{10,1... | collective-permute-start | bytes 1769480 | tf_op jit(solution)/shard_map/ppermute | solution.py:852
  97.5 3.0 %rotate.1 = f32[8,9,8,256]{3,2,1,0:T(8,128)} custom-call(s32[2,128]{1,0:T(2,128)S(1)} %copy-done.8, f32[8,10,8,256]{3,2,1,0:T(8,128)S(1)} %all-to-all-done.1.circle_in), custom_call_target="tpu_custom_call" | custom-call | tf_op jit(solution)/shard_map/rotate/pallas_call | solution.py:916
  100.5 10.0 %all-to-all-start.2 = ((f32[8,9,8,256]{3,2,1,0:T(8,128)}), f32[8,9,8,256]{3,2,1,0:T(8,128)S(1)}, u32[]{:S(2)}, u32[]{:S(2)}) async-start(f32[8,9,8,256]{3,2,1,0:T(8,128)} %rotate.1), calls=%async_computation.2 | async-start | bytes 1179648 | tf_op jit(solution)/shard_map/all_to_all | solution.py:930
  110.5 0.9 edge.1
  111.4 4.2 %collective-permute-start.22 = (f32[9,8,128]{2,1,0:T(8,128)S(1)}, f32[9,8,128]{2,1,0:T(8,128)S(1)}, u32[]{:S(2)}, u32[]{:S(2)}) collective-permute-start(f32[9,8,128]{2,1,0:T(8,128)S(1)} %edge.1), channel_id=1, source_target_pairs={{0,112},{16,0},{32,16},{48,32},{64,48},{80,64},{96,80},{112,96},{1... | collective-permute-start | bytes 110600 | tf_op jit(solution)/shard_map/ppermute | solution.py:867
  115.6 2.2 %collective-permute-done.22.edge = f32[9,8,128]{2,1,0:T(8,128)S(1)} collective-permute-done((f32[9,8,128]{2,1,0:T(8,128)S(1)}, f32[9,8,128]{2,1,0:T(8,128)S(1)}, u32[]{:S(2)}, u32[]{:S(2)}) %collective-permute-start.22) | collective-permute-done | bytes 36896 | tf_op jit(solution)/shard_map/ppermute | solution.py:867
  117.8 1.2 all-to-all-done.2.pole_in
  119.0 7.7 %last.1 = (f32[72,8,8,256]{3,2,1,0:T(8,128)}, f32[8,8,256]{2,1,0:T(8,128)}) custom-call(f32[72,8,8,256]{3,2,1,0:T(8,128)} %get-tuple-element.77.before_step, f32[72,8,8,256]{3,2,1,0:T(8,128)} %forcing.3.forcing_in, f32[72,8,256]{2,1,0:T(8,128)S(1)} %collective-permute-done.20.after_in, f32[72,8,256]{2,1,0:T(8,128)S(1)} %collective-permute-done.21.before_in, ...), custom_call_target="tpu_custom_call" | custom-call | tf_op jit(solution)/shard_map/last/pallas_call | solution.py:1044
  (32 shorter events, 0.1 us)
Async XLA Ops:
  0.6 38.4 %copy-start.3 = (f32[2,8,256]{2,1,0:T(8,128)S(1)}, f32[2,8,256]{2,1,0:T(8,128)}, u32[]{:S(2)}) copy-start(f32[2,8,256]{2,1,0:T(8,128)} %south.7) | copy-start | bytes 49156
  0.6 38.4 %copy-start.2 = (f32[2,8,256]{2,1,0:T(8,128)S(1)}, f32[2,8,256]{2,1,0:T(8,128)}, u32[]{:S(2)}) copy-start(f32[2,8,256]{2,1,0:T(8,128)} %north.7) | copy-start | bytes 49156
  0.7 19.3 %copy-start.13 = (s32[2,1]{0,1:T(1,128)S(1)}, s32[2,1]{0,1:T(1,128)}, u32[]{:S(2)}) copy-start(s32[2,1]{0,1:T(1,128)} %param.35) | copy-start | bytes 28
  0.7 19.4 %copy-start.5 = (f32[2,8,1280]{2,1,0:T(8,128)S(1)}, f32[2,8,1280]{2,1,0:T(8,128)}, u32[]{:S(2)}) copy-start(f32[2,8,1280]{2,1,0:T(8,128)} %misfits.1) | copy-start | bytes 245764
  0.7 19.4 %copy-start.1 = (f32[2,72,1280]{2,1,0:T(8,128)S(1)}, f32[2,72,1280]{2,1,0:T(8,128)}, u32[]{:S(2)}) copy-start(f32[2,72,1280]{2,1,0:T(8,128)} %kernels.1) | copy-start | bytes 2211844
  0.7 19.4 %copy-start.7 = (s32[2,1280]{1,0:T(2,128)S(1)}, s32[2,1280]{1,0:T(2,128)}, u32[]{:S(2)}) copy-start(s32[2,1280]{1,0:T(2,128)} %columns.1) | copy-start | bytes 30724
  0.7 19.4 %copy-start.6 = (s32[2,1280,1]{1,2,0:T(1,128)S(1)}, s32[2,1280,1]{1,2,0:T(1,128)}, u32[]{:S(2)}) copy-start(s32[2,1280,1]{1,2,0:T(1,128)} %param.33) | copy-start | bytes 30724
  0.7 38.4 %copy-start.8 = (s32[2,128]{1,0:T(2,128)S(1)}, s32[2,128]{1,0:T(2,128)}, u32[]{:S(2)}) copy-start(s32[2,128]{1,0:T(2,128)} %shift.3) | copy-start | bytes 3076
  8.5 21.2 %collective-permute-start.18 = (f32[73,8,256]{2,1,0:T(8,128)}, f32[73,8,256]{2,1,0:T(8,128)S(1)}, u32[]{:S(2)}, u32[]{:S(2)}) collective-permute-start(f32[73,8,256]{2,1,0:T(8,128)} %get-tuple-element.67.polar_in), channel_id=1, source_target_pairs={{16,0},{32,16},{48,32},{64,48},{80,64},{96,80},{112,96},{0,112},{3... | collective-permute-start | bytes 1794056 | tf_op jit(solution)/shard_map/ppermute | solution.py:1002
  15.6 11.6 %collective-permute-start.16 = (f32[72,8,256]{2,1,0:T(8,128)}, f32[72,8,256]{2,1,0:T(8,128)S(1)}, u32[]{:S(2)}, u32[]{:S(2)}) collective-permute-start(f32[72,8,256]{2,1,0:T(8,128)} %get-tuple-element.65), channel_id=1, source_target_pairs={{1,0},{2,1},{3,2},{4,3},{5,4},{6,5},{7,6},{8,7},{9,8},{10,9},{11,1... | collective-permute-start | bytes 1769480 | tf_op jit(solution)/shard_map/ppermute | solution.py:852
  16.9 10.3 %collective-permute-start.17 = (f32[72,8,256]{2,1,0:T(8,128)}, f32[72,8,256]{2,1,0:T(8,128)S(1)}, u32[]{:S(2)}, u32[]{:S(2)}) collective-permute-start(f32[72,8,256]{2,1,0:T(8,128)} %get-tuple-element.66), channel_id=1, source_target_pairs={{0,1},{1,2},{2,3},{3,4},{4,5},{5,6},{6,7},{7,8},{8,9},{9,10},{10,1... | collective-permute-start | bytes 1769480 | tf_op jit(solution)/shard_map/ppermute | solution.py:852
  27.2 11.9 %copy-start.9 = (f32[72,8,256]{2,1,0:T(8,128)}, f32[72,8,256]{2,1,0:T(8,128)S(1)}, u32[]{:S(2)}) copy-start(f32[72,8,256]{2,1,0:T(8,128)S(1)} %collective-permute-done.16.after_in) | copy-start | bytes 1769476
  27.2 2.5 %copy-start.10 = (f32[72,8,256]{2,1,0:T(8,128)}, f32[72,8,256]{2,1,0:T(8,128)S(1)}, u32[]{:S(2)}) copy-start(f32[72,8,256]{2,1,0:T(8,128)S(1)} %collective-permute-done.17.before_in) | copy-start | bytes 1769476
  29.7 0.8 copy-start.11
  30.5 37.8 %all-to-all-start = ((f32[128,24,128]{2,1,0:T(8,128)}), f32[128,24,128]{2,1,0:T(8,128)S(1)}, u32[]{:S(2)}, u32[]{:S(2)}) async-start(f32[128,24,128]{2,1,0:T(8,128)} %pack.1), calls=%async_computation | async-start | bytes 3145728 | tf_op jit(solution)/shard_map/all_to_all | solution.py:1007
  39.1 34.4 %copy-start = (f32[2,71,8,256]{3,2,1,0:T(8,128)S(1)}, f32[2,71,8,256]{3,2,1,0:T(8,128)}, u32[]{:S(2)}) copy-start(f32[2,71,8,256]{3,2,1,0:T(8,128)} %diffusion.1) | copy-start | bytes 3489796
  39.1 34.4 %copy-start.4 = (f32[2,8,256]{2,1,0:T(8,128)S(1)}, f32[2,8,256]{2,1,0:T(8,128)}, u32[]{:S(2)}) copy-start(f32[2,8,256]{2,1,0:T(8,128)} %east.3) | copy-start | bytes 49156
  43.5 30.0 %collective-permute-start.19 = (f32[9,8,128]{2,1,0:T(8,128)S(1)}, f32[9,8,128]{2,1,0:T(8,128)S(1)}, u32[]{:S(2)}, u32[]{:S(2)}) collective-permute-start(f32[9,8,128]{2,1,0:T(8,128)S(1)} %get-tuple-element.76), channel_id=1, source_target_pairs={{0,112},{16,0},{32,16},{48,32},{64,48},{80,64},{96,80},{112,96},{1... | collective-permute-start | bytes 110600 | tf_op jit(solution)/shard_map/ppermute | solution.py:867
  48.7 1.5 %collective-permute-start.12 = (f32[72,8,256]{2,1,0:T(8,128)}, f32[72,8,256]{2,1,0:T(8,128)}, u32[]{:S(2)}, u32[]{:S(2)}) collective-permute-start(f32[72,8,256]{2,1,0:T(8,128)} %param.12), channel_id=1, source_target_pairs={{79,15},{95,31},{111,47},{127,63},{15,79},{31,95},{47,111},{63,127}} | collective-permute-start | bytes 1769480 | tf_op jit(solution)/shard_map/cond/branch_4_fun/ppermute | solution.py:902
  50.2 18.1 %collective-permute-start.7 = (f32[72,8,256]{2,1,0:T(8,128)}, f32[72,8,256]{2,1,0:T(8,128)}, u32[]{:S(2)}, u32[]{:S(2)}) collective-permute-start(f32[72,8,256]{2,1,0:T(8,128)} %param.7), channel_id=1, source_target_pairs={{112,0},{0,16},{16,32},{32,48},{48,64},{64,80},{80,96},{96,112}} | collective-permute-start | bytes 1769480 | tf_op jit(solution)/shard_map/cond/branch_7_fun/ppermute | solution.py:902
  81.7 12.7 %copy-start.12 = (f32[72,8,256]{2,1,0:T(8,128)S(1)}, f32[72,8,256]{2,1,0:T(8,128)}, u32[]{:S(2)}) copy-start(f32[72,8,256]{2,1,0:T(8,128)} %get-tuple-element.84) | copy-start | bytes 1769476
  81.8 15.7 %all-to-all-start.1 = ((f32[8,10,8,256]{3,2,1,0:T(8,128)}), f32[8,10,8,256]{3,2,1,0:T(8,128)S(1)}, u32[]{:S(2)}, u32[]{:S(2)}) async-start(f32[8,10,8,256]{3,2,1,0:T(8,128)} %get-tuple-element.85), calls=%async_computation.1 | async-start | bytes 1310720 | tf_op jit(solution)/shard_map/all_to_all | solution.py:1036
  93.1 17.4 %collective-permute-start.20 = (f32[72,8,256]{2,1,0:T(8,128)}, f32[72,8,256]{2,1,0:T(8,128)S(1)}, u32[]{:S(2)}, u32[]{:S(2)}) collective-permute-start(f32[72,8,256]{2,1,0:T(8,128)} %get-tuple-element.83), channel_id=1, source_target_pairs={{1,0},{2,1},{3,2},{4,3},{5,4},{6,5},{7,6},{8,7},{9,8},{10,9},{11,1... | collective-permute-start | bytes 1769480 | tf_op jit(solution)/shard_map/ppermute | solution.py:852
  94.4 16.1 %collective-permute-start.21 = (f32[72,8,256]{2,1,0:T(8,128)S(1)}, f32[72,8,256]{2,1,0:T(8,128)S(1)}, u32[]{:S(2)}, u32[]{:S(2)}) collective-permute-start(f32[72,8,256]{2,1,0:T(8,128)S(1)} %copy-done.12), channel_id=1, source_target_pairs={{0,1},{1,2},{2,3},{3,4},{4,5},{5,6},{6,7},{7,8},{8,9},{9,10},{10,1... | collective-permute-start | bytes 1769480 | tf_op jit(solution)/shard_map/ppermute | solution.py:852
  100.5 18.6 %all-to-all-start.2 = ((f32[8,9,8,256]{3,2,1,0:T(8,128)}), f32[8,9,8,256]{3,2,1,0:T(8,128)S(1)}, u32[]{:S(2)}, u32[]{:S(2)}) async-start(f32[8,9,8,256]{3,2,1,0:T(8,128)} %rotate.1), calls=%async_computation.2 | async-start | bytes 1179648 | tf_op jit(solution)/shard_map/all_to_all | solution.py:930
  111.4 6.4 %collective-permute-start.22 = (f32[9,8,128]{2,1,0:T(8,128)S(1)}, f32[9,8,128]{2,1,0:T(8,128)S(1)}, u32[]{:S(2)}, u32[]{:S(2)}) collective-permute-start(f32[9,8,128]{2,1,0:T(8,128)S(1)} %edge.1), channel_id=1, source_target_pairs={{0,112},{16,0},{32,16},{48,32},{64,48},{80,64},{96,80},{112,96},{1... | collective-permute-start | bytes 110600 | tf_op jit(solution)/shard_map/ppermute | solution.py:867

commit v7 on v6

--- a/solution.py
+++ b/solution.py
@@ -891,7 +891,6 @@
         compiler_params=params(8),
         name="borders",
     )(shift, column, north, south, after, before, pinned(polar), nearby)
-    edge = westward(edge)
     moved = []
     for lat, hop in zip(poles, hops):
         moved.append(
@@ -906,7 +905,8 @@
                 turned,
             )
         )
-    return after, before, pinned(moved[0]), pinned(moved[1]), edge
+    edge, *moved = lax.optimization_barrier((edge, *moved))
+    return after, before, pinned(moved[0]), pinned(moved[1]), westward(edge)
 
 
 def last_exchange(step, after, before, circle, column, north, south, shift):

time: 129 us -> 129 us (level); the launches traced: 127 us -> 129 us
  starting transfers between devices: 50.6 us -> 54 us
  waiting for transfers between devices: 22.1 us -> 20.6 us
    ppermute x2, starting transfers between devices: 3.39 us -> 7.19 us  [first_exchange(): lax.ppermute(x, AXES, circles((lat,), k))]
    ppermute x2, starting transfers between devices: 8.06 us -> 5.68 us  [westward(): lax.ppermute(edge, 'lon', [(i, (i - 1) % count) for i in range(count)])]
    all_to_all x1, starting transfers between devices: 4.84 us -> 7.18 us  [per_device(): circle = lax.all_to_all(polar, 'lon', 0, 0, tiled=True)]
    ppermute x2, waiting for transfers between devices: 16.2 us -> 14.7 us  [first_exchange(): lax.ppermute(x, AXES, circles((lat,), k))]
where the time goes in v7:
time: 129 us
  starting transfers between devices  54 us (42%)
  Pallas kernels  50.9 us (39%)
  waiting for transfers between devices  20.6 us (16%)
  between operations  2.41 us (2%)
    ppermute x2, waiting for transfers between devices, first_exchange(): lax.ppermute(x, AXES, circles((lat,), k))  14.7 us
    pallas_call x2, Pallas kernels, forcing(): pl.pallas_call(functools.partial(streamed_forcing_kernel if streamed else...  11.7 us
    all_to_all x1, starting transfers between devices, last_exchange(): pole = lax.all_to_all(turned, 'lon', 0, 0, tiled=True)  9.69 us
    ppermute x4, starting transfers between devices, boundary_rows(): return (lax.ppermute(first, 'lat', down), lax.ppermute(last, 'lat', up))  8.72 us
    all_to_all x1, starting transfers between devices, per_device(): got = lax.all_to_all(sent, AXES, 0, 0, tiled=True)  8.52 us
    pallas_call x1, Pallas kernels, per_device(): pl.pallas_call(functools.partial(middle_kernel, 1), out_shape=[*solved_sh...  8.29 us
    pallas_call x1, Pallas kernels, per_device(): pl.pallas_call(functools.partial(first_kernel, 1), out_shape=solved_shape...  7.81 us
    pallas_call x1, Pallas kernels, per_device(): pl.pallas_call(functools.partial(last_kernel, 0), out_shape=[pltpu.HBM(co...  7.76 us
  transfers between devices with their start and end apart: 12, of which 4 were waited for; matrix products, arithmetic and copies ran while one was open for 0% of the time, Pallas kernels for 21%

profile of v7, /device:TPU:0, one launch (start us, length us, event | category | flops | bytes accessed | tf_op | source)
XLA Modules:
  0.0 129.0 jit_solution(7488005268243732902)
XLA Ops:
  0.7 7.8 %first.1 = (f32[72,8,8,256]{3,2,1,0:T(8,128)}, f32[72,8,256]{2,1,0:T(8,128)}, f32[72,8,256]{2,1,0:T(8,128)}, f32[73,8,256]{2,1,0:T(8,128)}, f32[9,8,128]{2,1,0:T(8,128)S(1)}) custom-call(f32[72,8,8,256]{3,2,1,0:T(8,128)} %costate.1, f32[2,71,8,256]{3,2,1,0:T(8,128)} %diffusion.1, f32[2,8,256]{2,1,0:T(8,128)} %north.7, f32[2,8,256]{2,1,0:T(8,128)} %south.7, ...), custom_call_target="tpu_custom_call" | custom-call | tf_op jit(solution)/shard_map/first/pallas_call | solution.py:981
  8.5 7.0 %collective-permute-start.18 = (f32[73,8,256]{2,1,0:T(8,128)}, f32[73,8,256]{2,1,0:T(8,128)S(1)}, u32[]{:S(2)}, u32[]{:S(2)}) collective-permute-start(f32[73,8,256]{2,1,0:T(8,128)} %get-tuple-element.70.polar_in), channel_id=1, source_target_pairs={{16,0},{32,16},{48,32},{64,48},{80,64},{96,80},{112,96},{0,112},{3... | collective-permute-start | bytes 1794056 | tf_op jit(solution)/shard_map/ppermute | solution.py:1002
  15.6 1.3 %collective-permute-start.16 = (f32[72,8,256]{2,1,0:T(8,128)}, f32[72,8,256]{2,1,0:T(8,128)S(1)}, u32[]{:S(2)}, u32[]{:S(2)}) collective-permute-start(f32[72,8,256]{2,1,0:T(8,128)} %get-tuple-element.68), channel_id=1, source_target_pairs={{1,0},{2,1},{3,2},{4,3},{5,4},{6,5},{7,6},{8,7},{9,8},{10,9},{11,1... | collective-permute-start | bytes 1769480 | tf_op jit(solution)/shard_map/ppermute | solution.py:852
  16.9 3.1 %collective-permute-start.17 = (f32[72,8,256]{2,1,0:T(8,128)}, f32[72,8,256]{2,1,0:T(8,128)S(1)}, u32[]{:S(2)}, u32[]{:S(2)}) collective-permute-start(f32[72,8,256]{2,1,0:T(8,128)} %get-tuple-element.69), channel_id=1, source_target_pairs={{0,1},{1,2},{2,3},{3,4},{4,5},{5,6},{6,7},{7,8},{8,9},{9,10},{10,1... | collective-permute-start | bytes 1769480 | tf_op jit(solution)/shard_map/ppermute | solution.py:852
  20.0 0.1 copy.13.counts
  20.1 7.1 %pack.1 = f32[128,24,128]{2,1,0:T(8,128)} custom-call(s32[2,1]{1,0:T(2,128)S(1)} %copy.13.counts, s32[2,1,1280]{2,1,0:T(1,128)S(1)} %bitcast.3, s32[2,1280]{1,0:T(2,128)S(1)} %copy-done.7, f32[2,72,1280]{2,1,0:T(8,128)S(1)} %copy-done.1, f32[2,8,1280]{2,1,0:T(8,128)S(1)} %copy-done.5), custom_call_target="tpu_custom_call" | custom-call | tf_op jit(solution)/shard_map/pack/pallas_call | solution.py:177
  27.2 0.0 collective-permute-done.17.before_in
  27.2 2.5 %collective-permute-done.18.nearby_in = f32[73,8,256]{2,1,0:T(8,128)S(1)} collective-permute-done((f32[73,8,256]{2,1,0:T(8,128)}, f32[73,8,256]{2,1,0:T(8,128)S(1)}, u32[]{:S(2)}, u32[]{:S(2)}) %collective-permute-start.18) | collective-permute-done | bytes 598048 | tf_op jit(solution)/shard_map/ppermute | solution.py:1002
  29.7 0.8 copy-done.11
  30.5 8.5 %all-to-all-start = ((f32[128,24,128]{2,1,0:T(8,128)}), f32[128,24,128]{2,1,0:T(8,128)S(1)}, u32[]{:S(2)}, u32[]{:S(2)}) async-start(f32[128,24,128]{2,1,0:T(8,128)} %pack.1), calls=%async_computation | async-start | bytes 3145728 | tf_op jit(solution)/shard_map/all_to_all | solution.py:1007
  39.1 0.0 copy-start
  39.1 0.0 copy-start.4
  39.1 4.4 %borders.1 = (f32[9,8,128]{2,1,0:T(8,128)S(1)}, f32[72,8,256]{2,1,0:T(8,128)}, s32[1,1]{1,0:T(1,128)}, s32[1,1]{1,0:T(1,128)}) custom-call(s32[2,128]{1,0:T(2,128)S(1)} %copy-done.8, f32[9,8,128]{2,1,0:T(8,128)S(1)} %get-tuple-element.74.column, f32[2,8,256]{2,1,0:T(8,128)S(1)} %copy-done.2, f32[2,8,256]{2,1,0:T(8,128)S(1)} %copy-done.3, ...), custom_call_target="tpu_custom_call" | custom-call | tf_op jit(solution)/shard_map/borders/pallas_call | solution.py:873
  44.8 1.5 %conditional.3 = (f32[72,8,256]{2,1,0:T(8,128)}) conditional(s32[]{:T(128)} %bitcast.2, f32[72,8,256]{2,1,0:T(8,128)} %get-tuple-element.78, f32[72,8,256]{2,1,0:T(8,128)} %get-tuple-element.78, f32[72,8,256]{2,1,0:T(8,128)} %get-tuple-element.78, f32[72,8,256]{2,1,0:T(8,128)} %get-tuple-element.78, ...), branch_computations={%region_8.0_spmd, %region_9.0_spmd, %region_10.0_spmd, %region_11.... | conditional | bytes 2359344 | solution.py:897
  44.8 1.5 %collective-permute-start.12 = (f32[72,8,256]{2,1,0:T(8,128)}, f32[72,8,256]{2,1,0:T(8,128)}, u32[]{:S(2)}, u32[]{:S(2)}) collective-permute-start(f32[72,8,256]{2,1,0:T(8,128)} %param.12), channel_id=1, source_target_pairs={{79,15},{95,31},{111,47},{127,63},{15,79},{31,95},{47,111},{63,127}} | collective-permute-start | bytes 1769480 | tf_op jit(solution)/shard_map/cond/branch_4_fun/ppermute | solution.py:901
  46.3 20.4 %conditional.2 = (f32[72,8,256]{2,1,0:T(8,128)}) conditional(s32[]{:T(128)} %bitcast.1, f32[72,8,256]{2,1,0:T(8,128)} %get-tuple-element.78, f32[72,8,256]{2,1,0:T(8,128)} %get-tuple-element.78, f32[72,8,256]{2,1,0:T(8,128)} %get-tuple-element.78, f32[72,8,256]{2,1,0:T(8,128)} %get-tuple-element.78, ...), branch_computations={%region_0.0_spmd, %region_1.0_spmd, %region_2.0_spmd, %region_3.0_... | conditional | bytes 2359344 | solution.py:897
  46.3 5.7 %collective-permute-start.2 = (f32[72,8,256]{2,1,0:T(8,128)}, f32[72,8,256]{2,1,0:T(8,128)}, u32[]{:S(2)}, u32[]{:S(2)}) collective-permute-start(f32[72,8,256]{2,1,0:T(8,128)} %param.2), channel_id=1, source_target_pairs={{32,0},{48,16},{64,32},{80,48},{96,64},{112,80},{0,96},{16,112}} | collective-permute-start | bytes 1769480 | tf_op jit(solution)/shard_map/cond/branch_2_fun/ppermute | solution.py:901
  52.0 14.7 %collective-permute-done.2 = f32[72,8,256]{2,1,0:T(8,128)} collective-permute-done((f32[72,8,256]{2,1,0:T(8,128)}, f32[72,8,256]{2,1,0:T(8,128)}, u32[]{:S(2)}, u32[]{:S(2)}) %collective-permute-start.2) | collective-permute-done | bytes 589856 | tf_op jit(solution)/shard_map/cond/branch_2_fun/ppermute | solution.py:901
  66.7 1.5 %collective-permute-start.19 = (f32[9,8,128]{2,1,0:T(8,128)S(1)}, f32[9,8,128]{2,1,0:T(8,128)S(1)}, u32[]{:S(2)}, u32[]{:S(2)}) collective-permute-start(f32[9,8,128]{2,1,0:T(8,128)S(1)} %get-tuple-element.82), channel_id=1, source_target_pairs={{0,112},{16,0},{32,16},{48,32},{64,48},{80,64},{96,80},{112,96},{1... | collective-permute-start | bytes 110600 | tf_op jit(solution)/shard_map/ppermute | solution.py:867
  68.2 5.2 %forcing.2.forced = f32[72,8,8,256]{3,2,1,0:T(8,128)S(1)} custom-call(f32[128,24,128]{2,1,0:T(8,128)S(1)} %all-to-all-done.received), custom_call_target="tpu_custom_call" | custom-call | tf_op jit(solution)/shard_map/forcing/pallas_call | solution.py:303
  73.4 8.3 %middle.1 = (f32[72,8,8,256]{3,2,1,0:T(8,128)}, f32[72,8,256]{2,1,0:T(8,128)}, f32[72,8,256]{2,1,0:T(8,128)}, f32[8,10,8,256]{3,2,1,0:T(8,128)}, f32[9,8,128]{2,1,0:T(8,128)S(1)}, /*index=5*/f32[8,8,256]{2,1,0:T(8,128)S(1)}) custom-call(f32[72,8,8,256]{3,2,1,0:T(8,128)} %get-tuple-element.65.before_step, f32[72,8,8,256]{3,2,1,0:T(8,128)S(1)} %forcing.2.forced, ...), custom_call_target="tpu_custom_call" | custom-call | tf_op jit(solution)/shard_map/middle/pallas_call | solution.py:1013
  81.7 7.2 %all-to-all-start.1 = ((f32[8,10,8,256]{3,2,1,0:T(8,128)}), f32[8,10,8,256]{3,2,1,0:T(8,128)S(1)}, u32[]{:S(2)}, u32[]{:S(2)}) async-start(f32[8,10,8,256]{3,2,1,0:T(8,128)} %get-tuple-element.91), calls=%async_computation.1 | async-start | bytes 1310720 | tf_op jit(solution)/shard_map/all_to_all | solution.py:1036
  88.9 6.5 %forcing.3.forcing_in = f32[72,8,8,256]{3,2,1,0:T(8,128)} custom-call(f32[128,24,128]{2,1,0:T(8,128)S(1)} %all-to-all-done.received), custom_call_target="tpu_custom_call" | custom-call | tf_op jit(solution)/shard_map/forcing/pallas_call | solution.py:303
  95.4 1.3 %collective-permute-start.20 = (f32[72,8,256]{2,1,0:T(8,128)}, f32[72,8,256]{2,1,0:T(8,128)S(1)}, u32[]{:S(2)}, u32[]{:S(2)}) collective-permute-start(f32[72,8,256]{2,1,0:T(8,128)} %get-tuple-element.89), channel_id=1, source_target_pairs={{1,0},{2,1},{3,2},{4,3},{5,4},{6,5},{7,6},{8,7},{9,8},{10,9},{11,1... | collective-permute-start | bytes 1769480 | tf_op jit(solution)/shard_map/ppermute | solution.py:852
  96.8 3.1 %collective-permute-start.21 = (f32[72,8,256]{2,1,0:T(8,128)S(1)}, f32[72,8,256]{2,1,0:T(8,128)S(1)}, u32[]{:S(2)}, u32[]{:S(2)}) collective-permute-start(f32[72,8,256]{2,1,0:T(8,128)S(1)} %copy-done.12), channel_id=1, source_target_pairs={{0,1},{1,2},{2,3},{3,4},{4,5},{5,6},{6,7},{7,8},{8,9},{9,10},{10,1... | collective-permute-start | bytes 1769480 | tf_op jit(solution)/shard_map/ppermute | solution.py:852
  99.8 3.0 %rotate.1 = f32[8,9,8,256]{3,2,1,0:T(8,128)} custom-call(s32[2,128]{1,0:T(2,128)S(1)} %copy-done.8, f32[8,10,8,256]{3,2,1,0:T(8,128)S(1)} %all-to-all-done.1.circle_in), custom_call_target="tpu_custom_call" | custom-call | tf_op jit(solution)/shard_map/rotate/pallas_call | solution.py:916
  102.8 9.7 %all-to-all-start.2 = ((f32[8,9,8,256]{3,2,1,0:T(8,128)}), f32[8,9,8,256]{3,2,1,0:T(8,128)S(1)}, u32[]{:S(2)}, u32[]{:S(2)}) async-start(f32[8,9,8,256]{3,2,1,0:T(8,128)} %rotate.1), calls=%async_computation.2 | async-start | bytes 1179648 | tf_op jit(solution)/shard_map/all_to_all | solution.py:930
  112.5 0.9 edge.1
  113.5 4.2 %collective-permute-start.22 = (f32[9,8,128]{2,1,0:T(8,128)S(1)}, f32[9,8,128]{2,1,0:T(8,128)S(1)}, u32[]{:S(2)}, u32[]{:S(2)}) collective-permute-start(f32[9,8,128]{2,1,0:T(8,128)S(1)} %edge.1), channel_id=1, source_target_pairs={{0,112},{16,0},{32,16},{48,32},{64,48},{80,64},{96,80},{112,96},{1... | collective-permute-start | bytes 110600 | tf_op jit(solution)/shard_map/ppermute | solution.py:867
  117.7 2.4 %collective-permute-done.22.edge = f32[9,8,128]{2,1,0:T(8,128)S(1)} collective-permute-done((f32[9,8,128]{2,1,0:T(8,128)S(1)}, f32[9,8,128]{2,1,0:T(8,128)S(1)}, u32[]{:S(2)}, u32[]{:S(2)}) %collective-permute-start.22) | collective-permute-done | bytes 36896 | tf_op jit(solution)/shard_map/ppermute | solution.py:867
  120.1 1.0 all-to-all-done.2.pole_in
  121.1 7.8 %last.1 = (f32[72,8,8,256]{3,2,1,0:T(8,128)}, f32[8,8,256]{2,1,0:T(8,128)}) custom-call(f32[72,8,8,256]{3,2,1,0:T(8,128)} %get-tuple-element.83.before_step, f32[72,8,8,256]{3,2,1,0:T(8,128)} %forcing.3.forcing_in, f32[72,8,256]{2,1,0:T(8,128)S(1)} %collective-permute-done.20.after_in, f32[72,8,256]{2,1,0:T(8,128)S(1)} %collective-permute-done.21.before_in, ...), custom_call_target="tpu_custom_call" | custom-call | tf_op jit(solution)/shard_map/last/pallas_call | solution.py:1044
  (32 shorter events, 0.1 us)
Async XLA Ops:
  0.6 38.4 %copy-start.3 = (f32[2,8,256]{2,1,0:T(8,128)S(1)}, f32[2,8,256]{2,1,0:T(8,128)}, u32[]{:S(2)}) copy-start(f32[2,8,256]{2,1,0:T(8,128)} %south.7) | copy-start | bytes 49156
  0.6 38.4 %copy-start.2 = (f32[2,8,256]{2,1,0:T(8,128)S(1)}, f32[2,8,256]{2,1,0:T(8,128)}, u32[]{:S(2)}) copy-start(f32[2,8,256]{2,1,0:T(8,128)} %north.7) | copy-start | bytes 49156
  0.7 19.3 %copy-start.13 = (s32[2,1]{0,1:T(1,128)S(1)}, s32[2,1]{0,1:T(1,128)}, u32[]{:S(2)}) copy-start(s32[2,1]{0,1:T(1,128)} %param.35) | copy-start | bytes 28
  0.7 19.4 %copy-start.5 = (f32[2,8,1280]{2,1,0:T(8,128)S(1)}, f32[2,8,1280]{2,1,0:T(8,128)}, u32[]{:S(2)}) copy-start(f32[2,8,1280]{2,1,0:T(8,128)} %misfits.1) | copy-start | bytes 245764
  0.7 19.4 %copy-start.1 = (f32[2,72,1280]{2,1,0:T(8,128)S(1)}, f32[2,72,1280]{2,1,0:T(8,128)}, u32[]{:S(2)}) copy-start(f32[2,72,1280]{2,1,0:T(8,128)} %kernels.1) | copy-start | bytes 2211844
  0.7 19.4 %copy-start.7 = (s32[2,1280]{1,0:T(2,128)S(1)}, s32[2,1280]{1,0:T(2,128)}, u32[]{:S(2)}) copy-start(s32[2,1280]{1,0:T(2,128)} %columns.1) | copy-start | bytes 30724
  0.7 19.4 %copy-start.6 = (s32[2,1280,1]{1,2,0:T(1,128)S(1)}, s32[2,1280,1]{1,2,0:T(1,128)}, u32[]{:S(2)}) copy-start(s32[2,1280,1]{1,2,0:T(1,128)} %param.33) | copy-start | bytes 30724
  0.7 38.4 %copy-start.8 = (s32[2,128]{1,0:T(2,128)S(1)}, s32[2,128]{1,0:T(2,128)}, u32[]{:S(2)}) copy-start(s32[2,128]{1,0:T(2,128)} %shift.3) | copy-start | bytes 3076
  8.5 21.2 %collective-permute-start.18 = (f32[73,8,256]{2,1,0:T(8,128)}, f32[73,8,256]{2,1,0:T(8,128)S(1)}, u32[]{:S(2)}, u32[]{:S(2)}) collective-permute-start(f32[73,8,256]{2,1,0:T(8,128)} %get-tuple-element.70.polar_in), channel_id=1, source_target_pairs={{16,0},{32,16},{48,32},{64,48},{80,64},{96,80},{112,96},{0,112},{3... | collective-permute-start | bytes 1794056 | tf_op jit(solution)/shard_map/ppermute | solution.py:1002
  15.6 11.6 %collective-permute-start.16 = (f32[72,8,256]{2,1,0:T(8,128)}, f32[72,8,256]{2,1,0:T(8,128)S(1)}, u32[]{:S(2)}, u32[]{:S(2)}) collective-permute-start(f32[72,8,256]{2,1,0:T(8,128)} %get-tuple-element.68), channel_id=1, source_target_pairs={{1,0},{2,1},{3,2},{4,3},{5,4},{6,5},{7,6},{8,7},{9,8},{10,9},{11,1... | collective-permute-start | bytes 1769480 | tf_op jit(solution)/shard_map/ppermute | solution.py:852
  16.9 10.3 %collective-permute-start.17 = (f32[72,8,256]{2,1,0:T(8,128)}, f32[72,8,256]{2,1,0:T(8,128)S(1)}, u32[]{:S(2)}, u32[]{:S(2)}) collective-permute-start(f32[72,8,256]{2,1,0:T(8,128)} %get-tuple-element.69), channel_id=1, source_target_pairs={{0,1},{1,2},{2,3},{3,4},{4,5},{5,6},{6,7},{7,8},{8,9},{9,10},{10,1... | collective-permute-start | bytes 1769480 | tf_op jit(solution)/shard_map/ppermute | solution.py:852
  27.1 11.9 %copy-start.9 = (f32[72,8,256]{2,1,0:T(8,128)}, f32[72,8,256]{2,1,0:T(8,128)S(1)}, u32[]{:S(2)}) copy-start(f32[72,8,256]{2,1,0:T(8,128)S(1)} %collective-permute-done.16.after_in) | copy-start | bytes 1769476
  27.2 2.5 %copy-start.10 = (f32[72,8,256]{2,1,0:T(8,128)}, f32[72,8,256]{2,1,0:T(8,128)S(1)}, u32[]{:S(2)}) copy-start(f32[72,8,256]{2,1,0:T(8,128)S(1)} %collective-permute-done.17.before_in) | copy-start | bytes 1769476
  29.7 0.8 copy-start.11
  30.5 37.7 %all-to-all-start = ((f32[128,24,128]{2,1,0:T(8,128)}), f32[128,24,128]{2,1,0:T(8,128)S(1)}, u32[]{:S(2)}, u32[]{:S(2)}) async-start(f32[128,24,128]{2,1,0:T(8,128)} %pack.1), calls=%async_computation | async-start | bytes 3145728 | tf_op jit(solution)/shard_map/all_to_all | solution.py:1007
  39.1 34.4 %copy-start = (f32[2,71,8,256]{3,2,1,0:T(8,128)S(1)}, f32[2,71,8,256]{3,2,1,0:T(8,128)}, u32[]{:S(2)}) copy-start(f32[2,71,8,256]{3,2,1,0:T(8,128)} %diffusion.1) | copy-start | bytes 3489796
  39.1 34.3 %copy-start.4 = (f32[2,8,256]{2,1,0:T(8,128)S(1)}, f32[2,8,256]{2,1,0:T(8,128)}, u32[]{:S(2)}) copy-start(f32[2,8,256]{2,1,0:T(8,128)} %east.3) | copy-start | bytes 49156
  44.8 1.5 %collective-permute-start.12 = (f32[72,8,256]{2,1,0:T(8,128)}, f32[72,8,256]{2,1,0:T(8,128)}, u32[]{:S(2)}, u32[]{:S(2)}) collective-permute-start(f32[72,8,256]{2,1,0:T(8,128)} %param.12), channel_id=1, source_target_pairs={{79,15},{95,31},{111,47},{127,63},{15,79},{31,95},{47,111},{63,127}} | collective-permute-start | bytes 1769480 | tf_op jit(solution)/shard_map/cond/branch_4_fun/ppermute | solution.py:901
  46.3 20.4 %collective-permute-start.2 = (f32[72,8,256]{2,1,0:T(8,128)}, f32[72,8,256]{2,1,0:T(8,128)}, u32[]{:S(2)}, u32[]{:S(2)}) collective-permute-start(f32[72,8,256]{2,1,0:T(8,128)} %param.2), channel_id=1, source_target_pairs={{32,0},{48,16},{64,32},{80,48},{96,64},{112,80},{0,96},{16,112}} | collective-permute-start | bytes 1769480 | tf_op jit(solution)/shard_map/cond/branch_2_fun/ppermute | solution.py:901
  66.7 6.7 %collective-permute-start.19 = (f32[9,8,128]{2,1,0:T(8,128)S(1)}, f32[9,8,128]{2,1,0:T(8,128)S(1)}, u32[]{:S(2)}, u32[]{:S(2)}) collective-permute-start(f32[9,8,128]{2,1,0:T(8,128)S(1)} %get-tuple-element.82), channel_id=1, source_target_pairs={{0,112},{16,0},{32,16},{48,32},{64,48},{80,64},{96,80},{112,96},{1... | collective-permute-start | bytes 110600 | tf_op jit(solution)/shard_map/ppermute | solution.py:867
  81.7 15.0 %copy-start.12 = (f32[72,8,256]{2,1,0:T(8,128)S(1)}, f32[72,8,256]{2,1,0:T(8,128)}, u32[]{:S(2)}) copy-start(f32[72,8,256]{2,1,0:T(8,128)} %get-tuple-element.90) | copy-start | bytes 1769476
  81.7 18.1 %all-to-all-start.1 = ((f32[8,10,8,256]{3,2,1,0:T(8,128)}), f32[8,10,8,256]{3,2,1,0:T(8,128)S(1)}, u32[]{:S(2)}, u32[]{:S(2)}) async-start(f32[8,10,8,256]{3,2,1,0:T(8,128)} %get-tuple-element.91), calls=%async_computation.1 | async-start | bytes 1310720 | tf_op jit(solution)/shard_map/all_to_all | solution.py:1036
  95.4 17.1 %collective-permute-start.20 = (f32[72,8,256]{2,1,0:T(8,128)}, f32[72,8,256]{2,1,0:T(8,128)S(1)}, u32[]{:S(2)}, u32[]{:S(2)}) collective-permute-start(f32[72,8,256]{2,1,0:T(8,128)} %get-tuple-element.89), channel_id=1, source_target_pairs={{1,0},{2,1},{3,2},{4,3},{5,4},{6,5},{7,6},{8,7},{9,8},{10,9},{11,1... | collective-permute-start | bytes 1769480 | tf_op jit(solution)/shard_map/ppermute | solution.py:852
  96.8 15.8 %collective-permute-start.21 = (f32[72,8,256]{2,1,0:T(8,128)S(1)}, f32[72,8,256]{2,1,0:T(8,128)S(1)}, u32[]{:S(2)}, u32[]{:S(2)}) collective-permute-start(f32[72,8,256]{2,1,0:T(8,128)S(1)} %copy-done.12), channel_id=1, source_target_pairs={{0,1},{1,2},{2,3},{3,4},{4,5},{5,6},{6,7},{7,8},{8,9},{9,10},{10,1... | collective-permute-start | bytes 1769480 | tf_op jit(solution)/shard_map/ppermute | solution.py:852
  102.8 18.2 %all-to-all-start.2 = ((f32[8,9,8,256]{3,2,1,0:T(8,128)}), f32[8,9,8,256]{3,2,1,0:T(8,128)S(1)}, u32[]{:S(2)}, u32[]{:S(2)}) async-start(f32[8,9,8,256]{3,2,1,0:T(8,128)} %rotate.1), calls=%async_computation.2 | async-start | bytes 1179648 | tf_op jit(solution)/shard_map/all_to_all | solution.py:930
  113.5 6.6 %collective-permute-start.22 = (f32[9,8,128]{2,1,0:T(8,128)S(1)}, f32[9,8,128]{2,1,0:T(8,128)S(1)}, u32[]{:S(2)}, u32[]{:S(2)}) collective-permute-start(f32[9,8,128]{2,1,0:T(8,128)S(1)} %edge.1), channel_id=1, source_target_pairs={{0,112},{16,0},{32,16},{48,32},{64,48},{80,64},{96,80},{112,96},{1... | collective-permute-start | bytes 110600 | tf_op jit(solution)/shard_map/ppermute | solution.py:867

commit v8 on v7

--- a/solution.py
+++ b/solution.py
@@ -561,13 +561,10 @@
         matrix = shift_matrix(lax.rem(amount, cells), cells)
         tracers = turned.shape[1]
         weight = shifted(polar[levels], nearby[levels], matrix)[:1, :cells]
-        size = 3 * GROUP
-        for i in range(levels // size):
-            at = slice(i * size, (i + 1) * size)
-            low, high = [x[at].reshape(size * tracers, cells) for x in (polar, nearby)]
-            row = shifted(low, high, matrix)
-            row = row[:, :cells] + weight * (row[:, cells:] - row[:, :cells])
-            turned[at] = row.reshape(size, tracers, cells)
+        low, high = [x[:levels].reshape(levels * tracers, cells) for x in (polar, nearby)]
+        row = shifted(low, high, matrix)
+        row = row[:, :cells] + weight * (row[:, cells:] - row[:, :cells])
+        turned[...] = row.reshape(levels, tracers, cells)
         sending.start()
 
     finish()
@@ -649,15 +646,11 @@
             far = lax.rem(part + hops + 1, parts)
             pairs[at, :cells] = circle[near].reshape(height, cells)
             pairs[at, cells:] = circle[far].reshape(height, cells)
-        batch = parts // 2
-        for i in range(2):
-            rows_at = slice(i * batch * height, (i + 1) * batch * height)
-            row = shifted(pairs[rows_at, :cells], pairs[rows_at, cells:], matrix)
-            row = row.reshape(batch, groups + 1, group, 2 * cells)
-            weight = row[:, groups:, :1, :cells]
-            row = row[:, :groups]
-            row = row[..., :cells] + weight * (row[..., cells:] - row[..., :cells])
-            turned[i * batch : (i + 1) * batch] = row
+        row = shifted(pairs[:, :cells], pairs[:, cells:], matrix)
+        row = row.reshape(parts, groups + 1, group, 2 * cells)
+        weight = row[:, groups:, :1, :cells]
+        row = row[:, :groups]
+        turned[...] = row[..., :cells] + weight * (row[..., cells:] - row[..., :cells])
         send = pltpu.make_async_copy(turned, out, ready.at[1])
         send.start()
         send.wait()
@@ -888,7 +881,7 @@
             pltpu.VMEM((levels, tracers, cells), F32),
             pltpu.SemaphoreType.DMA((5,)),
         ],
-        compiler_params=params(8),
+        compiler_params=params(14),
         name="borders",
     )(shift, column, north, south, after, before, pinned(polar), nearby)
     moved = []
@@ -924,7 +917,7 @@
             pltpu.VMEM(shape, F32),
             pltpu.SemaphoreType.DMA((2,)),
         ],
-        compiler_params=params(14),
+        compiler_params=params(18),
         name="rotate",
     )(shift, circle)
     pole = lax.all_to_all(turned, "lon", 0, 0, tiled=True)

time: 129 us -> 129 us (level)
  starting transfers between devices: 54 us -> 51.9 us
  waiting for transfers between devices: 20.6 us -> 22.3 us
    ppermute x2, starting transfers between devices: 7.19 us -> 5.42 us  [first_exchange(): lax.ppermute(x, AXES, circles((lat,), k))]
    ppermute x2, waiting for transfers between devices: 14.7 us -> 16.4 us  [first_exchange(): lax.ppermute(x, AXES, circles((lat,), k))]
where the time goes in v8:
time: 129 us; the launch traced here: 128 us
  starting transfers between devices  51.9 us (40%)
  Pallas kernels  50.9 us (39%)
  waiting for transfers between devices  22.3 us (17%)
  between operations  2.41 us (2%)
    ppermute x2, waiting for transfers between devices, first_exchange(): lax.ppermute(x, AXES, circles((lat,), k))  16.4 us
    pallas_call x2, Pallas kernels, forcing(): pl.pallas_call(functools.partial(streamed_forcing_kernel if streamed else...  11.7 us
    all_to_all x1, starting transfers between devices, last_exchange(): pole = lax.all_to_all(turned, 'lon', 0, 0, tiled=True)  9.11 us
    ppermute x4, starting transfers between devices, boundary_rows(): return (lax.ppermute(first, 'lat', down), lax.ppermute(last, 'lat', up))  8.72 us
    all_to_all x1, starting transfers between devices, per_device(): got = lax.all_to_all(sent, AXES, 0, 0, tiled=True)  8.52 us
    pallas_call x1, Pallas kernels, per_device(): pl.pallas_call(functools.partial(middle_kernel, 1), out_shape=[*solved_sh...  8.29 us
    pallas_call x1, Pallas kernels, per_device(): pl.pallas_call(functools.partial(first_kernel, 1), out_shape=solved_shape...  7.81 us
    pallas_call x1, Pallas kernels, per_device(): pl.pallas_call(functools.partial(last_kernel, 0), out_shape=[pltpu.HBM(co...  7.76 us
  transfers between devices with their start and end apart: 12, of which 4 were waited for; matrix products, arithmetic and copies ran while one was open for 0% of the time, Pallas kernels for 21%

profile of v8, /device:TPU:0, one launch (start us, length us, event | category | flops | bytes accessed | tf_op | source)
XLA Modules:
  0.0 128.4 jit_solution(9238140303190992159)
XLA Ops:
  0.7 7.8 %first.1 = (f32[72,8,8,256]{3,2,1,0:T(8,128)}, f32[72,8,256]{2,1,0:T(8,128)}, f32[72,8,256]{2,1,0:T(8,128)}, f32[73,8,256]{2,1,0:T(8,128)}, f32[9,8,128]{2,1,0:T(8,128)S(1)}) custom-call(f32[72,8,8,256]{3,2,1,0:T(8,128)} %costate.1, f32[2,71,8,256]{3,2,1,0:T(8,128)} %diffusion.1, f32[2,8,256]{2,1,0:T(8,128)} %north.7, f32[2,8,256]{2,1,0:T(8,128)} %south.7, ...), custom_call_target="tpu_custom_call" | custom-call | tf_op jit(solution)/shard_map/first/pallas_call | solution.py:974
  8.5 7.0 %collective-permute-start.18 = (f32[73,8,256]{2,1,0:T(8,128)}, f32[73,8,256]{2,1,0:T(8,128)S(1)}, u32[]{:S(2)}, u32[]{:S(2)}) collective-permute-start(f32[73,8,256]{2,1,0:T(8,128)} %get-tuple-element.70.polar_in), channel_id=1, source_target_pairs={{16,0},{32,16},{48,32},{64,48},{80,64},{96,80},{112,96},{0,112},{3... | collective-permute-start | bytes 1794056 | tf_op jit(solution)/shard_map/ppermute | solution.py:995
  15.6 1.3 %collective-permute-start.16 = (f32[72,8,256]{2,1,0:T(8,128)}, f32[72,8,256]{2,1,0:T(8,128)S(1)}, u32[]{:S(2)}, u32[]{:S(2)}) collective-permute-start(f32[72,8,256]{2,1,0:T(8,128)} %get-tuple-element.68), channel_id=1, source_target_pairs={{1,0},{2,1},{3,2},{4,3},{5,4},{6,5},{7,6},{8,7},{9,8},{10,9},{11,1... | collective-permute-start | bytes 1769480 | tf_op jit(solution)/shard_map/ppermute | solution.py:845
  16.9 3.1 %collective-permute-start.17 = (f32[72,8,256]{2,1,0:T(8,128)}, f32[72,8,256]{2,1,0:T(8,128)S(1)}, u32[]{:S(2)}, u32[]{:S(2)}) collective-permute-start(f32[72,8,256]{2,1,0:T(8,128)} %get-tuple-element.69), channel_id=1, source_target_pairs={{0,1},{1,2},{2,3},{3,4},{4,5},{5,6},{6,7},{7,8},{8,9},{9,10},{10,1... | collective-permute-start | bytes 1769480 | tf_op jit(solution)/shard_map/ppermute | solution.py:845
  20.0 0.1 copy.13.counts
  20.1 7.1 %pack.1 = f32[128,24,128]{2,1,0:T(8,128)} custom-call(s32[2,1]{1,0:T(2,128)S(1)} %copy.13.counts, s32[2,1,1280]{2,1,0:T(1,128)S(1)} %bitcast.3, s32[2,1280]{1,0:T(2,128)S(1)} %copy-done.7, f32[2,72,1280]{2,1,0:T(8,128)S(1)} %copy-done.1, f32[2,8,1280]{2,1,0:T(8,128)S(1)} %copy-done.5), custom_call_target="tpu_custom_call" | custom-call | tf_op jit(solution)/shard_map/pack/pallas_call | solution.py:177
  27.1 0.0 collective-permute-done.16.after_in
  27.2 2.5 %collective-permute-done.18.nearby_in = f32[73,8,256]{2,1,0:T(8,128)S(1)} collective-permute-done((f32[73,8,256]{2,1,0:T(8,128)}, f32[73,8,256]{2,1,0:T(8,128)S(1)}, u32[]{:S(2)}, u32[]{:S(2)}) %collective-permute-start.18) | collective-permute-done | bytes 598048 | tf_op jit(solution)/shard_map/ppermute | solution.py:995
  29.7 0.8 copy-done.11
  30.5 8.5 %all-to-all-start = ((f32[128,24,128]{2,1,0:T(8,128)}), f32[128,24,128]{2,1,0:T(8,128)S(1)}, u32[]{:S(2)}, u32[]{:S(2)}) async-start(f32[128,24,128]{2,1,0:T(8,128)} %pack.1), calls=%async_computation | async-start | bytes 3145728 | tf_op jit(solution)/shard_map/all_to_all | solution.py:1000
  39.1 0.0 copy-start
  39.1 0.0 copy-start.4
  39.1 4.4 %borders.1 = (f32[9,8,128]{2,1,0:T(8,128)S(1)}, f32[72,8,256]{2,1,0:T(8,128)}, s32[1,1]{1,0:T(1,128)}, s32[1,1]{1,0:T(1,128)}) custom-call(s32[2,128]{1,0:T(2,128)S(1)} %copy-done.8, f32[9,8,128]{2,1,0:T(8,128)S(1)} %get-tuple-element.74.column, f32[2,8,256]{2,1,0:T(8,128)S(1)} %copy-done.2, f32[2,8,256]{2,1,0:T(8,128)S(1)} %copy-done.3, ...), custom_call_target="tpu_custom_call" | custom-call | tf_op jit(solution)/shard_map/borders/pallas_call | solution.py:866
  44.8 1.5 %conditional.3 = (f32[72,8,256]{2,1,0:T(8,128)}) conditional(s32[]{:T(128)} %bitcast.2, f32[72,8,256]{2,1,0:T(8,128)} %get-tuple-element.78, f32[72,8,256]{2,1,0:T(8,128)} %get-tuple-element.78, f32[72,8,256]{2,1,0:T(8,128)} %get-tuple-element.78, f32[72,8,256]{2,1,0:T(8,128)} %get-tuple-element.78, ...), branch_computations={%region_8.0_spmd, %region_9.0_spmd, %region_10.0_spmd, %region_11.... | conditional | bytes 2359344 | solution.py:890
  44.8 1.5 %collective-permute-start.12 = (f32[72,8,256]{2,1,0:T(8,128)}, f32[72,8,256]{2,1,0:T(8,128)}, u32[]{:S(2)}, u32[]{:S(2)}) collective-permute-start(f32[72,8,256]{2,1,0:T(8,128)} %param.12), channel_id=1, source_target_pairs={{79,15},{95,31},{111,47},{127,63},{15,79},{31,95},{47,111},{63,127}} | collective-permute-start | bytes 1769480 | tf_op jit(solution)/shard_map/cond/branch_4_fun/ppermute | solution.py:894
  46.3 20.3 %conditional.2 = (f32[72,8,256]{2,1,0:T(8,128)}) conditional(s32[]{:T(128)} %bitcast.1, f32[72,8,256]{2,1,0:T(8,128)} %get-tuple-element.78, f32[72,8,256]{2,1,0:T(8,128)} %get-tuple-element.78, f32[72,8,256]{2,1,0:T(8,128)} %get-tuple-element.78, f32[72,8,256]{2,1,0:T(8,128)} %get-tuple-element.78, ...), branch_computations={%region_0.0_spmd, %region_1.0_spmd, %region_2.0_spmd, %region_3.0_... | conditional | bytes 2359344 | solution.py:890
  46.3 3.9 %collective-permute-start.3 = (f32[72,8,256]{2,1,0:T(8,128)}, f32[72,8,256]{2,1,0:T(8,128)}, u32[]{:S(2)}, u32[]{:S(2)}) collective-permute-start(f32[72,8,256]{2,1,0:T(8,128)} %param.3), channel_id=1, source_target_pairs={{48,0},{64,16},{80,32},{96,48},{112,64},{0,80},{16,96},{32,112}} | collective-permute-start | bytes 1769480 | tf_op jit(solution)/shard_map/cond/branch_3_fun/ppermute | solution.py:894
  50.2 16.4 %collective-permute-done.3 = f32[72,8,256]{2,1,0:T(8,128)} collective-permute-done((f32[72,8,256]{2,1,0:T(8,128)}, f32[72,8,256]{2,1,0:T(8,128)}, u32[]{:S(2)}, u32[]{:S(2)}) %collective-permute-start.3) | collective-permute-done | bytes 589856 | tf_op jit(solution)/shard_map/cond/branch_3_fun/ppermute | solution.py:894
  66.6 2.0 %collective-permute-start.19 = (f32[9,8,128]{2,1,0:T(8,128)S(1)}, f32[9,8,128]{2,1,0:T(8,128)S(1)}, u32[]{:S(2)}, u32[]{:S(2)}) collective-permute-start(f32[9,8,128]{2,1,0:T(8,128)S(1)} %get-tuple-element.82), channel_id=1, source_target_pairs={{0,112},{16,0},{32,16},{48,32},{64,48},{80,64},{96,80},{112,96},{1... | collective-permute-start | bytes 110600 | tf_op jit(solution)/shard_map/ppermute | solution.py:860
  68.6 5.2 %forcing.2.forced = f32[72,8,8,256]{3,2,1,0:T(8,128)S(1)} custom-call(f32[128,24,128]{2,1,0:T(8,128)S(1)} %all-to-all-done.received), custom_call_target="tpu_custom_call" | custom-call | tf_op jit(solution)/shard_map/forcing/pallas_call | solution.py:303
  73.8 8.3 %middle.1 = (f32[72,8,8,256]{3,2,1,0:T(8,128)}, f32[72,8,256]{2,1,0:T(8,128)}, f32[72,8,256]{2,1,0:T(8,128)}, f32[8,10,8,256]{3,2,1,0:T(8,128)}, f32[9,8,128]{2,1,0:T(8,128)S(1)}, /*index=5*/f32[8,8,256]{2,1,0:T(8,128)S(1)}) custom-call(f32[72,8,8,256]{3,2,1,0:T(8,128)} %get-tuple-element.65.before_step, f32[72,8,8,256]{3,2,1,0:T(8,128)S(1)} %forcing.2.forced, ...), custom_call_target="tpu_custom_call" | custom-call | tf_op jit(solution)/shard_map/middle/pallas_call | solution.py:1006
  82.1 6.8 %all-to-all-start.1 = ((f32[8,10,8,256]{3,2,1,0:T(8,128)}), f32[8,10,8,256]{3,2,1,0:T(8,128)S(1)}, u32[]{:S(2)}, u32[]{:S(2)}) async-start(f32[8,10,8,256]{3,2,1,0:T(8,128)} %get-tuple-element.91), calls=%async_computation.1 | async-start | bytes 1310720 | tf_op jit(solution)/shard_map/all_to_all | solution.py:1029
  89.0 6.5 %forcing.3.forcing_in = f32[72,8,8,256]{3,2,1,0:T(8,128)} custom-call(f32[128,24,128]{2,1,0:T(8,128)S(1)} %all-to-all-done.received), custom_call_target="tpu_custom_call" | custom-call | tf_op jit(solution)/shard_map/forcing/pallas_call | solution.py:303
  95.5 1.3 %collective-permute-start.20 = (f32[72,8,256]{2,1,0:T(8,128)}, f32[72,8,256]{2,1,0:T(8,128)S(1)}, u32[]{:S(2)}, u32[]{:S(2)}) collective-permute-start(f32[72,8,256]{2,1,0:T(8,128)} %get-tuple-element.89), channel_id=1, source_target_pairs={{1,0},{2,1},{3,2},{4,3},{5,4},{6,5},{7,6},{8,7},{9,8},{10,9},{11,1... | collective-permute-start | bytes 1769480 | tf_op jit(solution)/shard_map/ppermute | solution.py:845
  96.8 3.1 %collective-permute-start.21 = (f32[72,8,256]{2,1,0:T(8,128)S(1)}, f32[72,8,256]{2,1,0:T(8,128)S(1)}, u32[]{:S(2)}, u32[]{:S(2)}) collective-permute-start(f32[72,8,256]{2,1,0:T(8,128)S(1)} %copy-done.12), channel_id=1, source_target_pairs={{0,1},{1,2},{2,3},{3,4},{4,5},{5,6},{6,7},{7,8},{8,9},{9,10},{10,1... | collective-permute-start | bytes 1769480 | tf_op jit(solution)/shard_map/ppermute | solution.py:845
  99.9 3.0 %rotate.1 = f32[8,9,8,256]{3,2,1,0:T(8,128)} custom-call(s32[2,128]{1,0:T(2,128)S(1)} %copy-done.8, f32[8,10,8,256]{3,2,1,0:T(8,128)S(1)} %all-to-all-done.1.circle_in), custom_call_target="tpu_custom_call" | custom-call | tf_op jit(solution)/shard_map/rotate/pallas_call | solution.py:909
  102.8 9.1 %all-to-all-start.2 = ((f32[8,9,8,256]{3,2,1,0:T(8,128)}), f32[8,9,8,256]{3,2,1,0:T(8,128)S(1)}, u32[]{:S(2)}, u32[]{:S(2)}) async-start(f32[8,9,8,256]{3,2,1,0:T(8,128)} %rotate.1), calls=%async_computation.2 | async-start | bytes 1179648 | tf_op jit(solution)/shard_map/all_to_all | solution.py:923
  112.0 0.9 edge.1
  112.9 4.2 %collective-permute-start.22 = (f32[9,8,128]{2,1,0:T(8,128)S(1)}, f32[9,8,128]{2,1,0:T(8,128)S(1)}, u32[]{:S(2)}, u32[]{:S(2)}) collective-permute-start(f32[9,8,128]{2,1,0:T(8,128)S(1)} %edge.1), channel_id=1, source_target_pairs={{0,112},{16,0},{32,16},{48,32},{64,48},{80,64},{96,80},{112,96},{1... | collective-permute-start | bytes 110600 | tf_op jit(solution)/shard_map/ppermute | solution.py:860
  117.1 2.3 %collective-permute-done.22.edge = f32[9,8,128]{2,1,0:T(8,128)S(1)} collective-permute-done((f32[9,8,128]{2,1,0:T(8,128)S(1)}, f32[9,8,128]{2,1,0:T(8,128)S(1)}, u32[]{:S(2)}, u32[]{:S(2)}) %collective-permute-start.22) | collective-permute-done | bytes 36896 | tf_op jit(solution)/shard_map/ppermute | solution.py:860
  119.4 1.1 all-to-all-done.2.pole_in
  120.5 7.8 %last.1 = (f32[72,8,8,256]{3,2,1,0:T(8,128)}, f32[8,8,256]{2,1,0:T(8,128)}) custom-call(f32[72,8,8,256]{3,2,1,0:T(8,128)} %get-tuple-element.83.before_step, f32[72,8,8,256]{3,2,1,0:T(8,128)} %forcing.3.forcing_in, f32[72,8,256]{2,1,0:T(8,128)S(1)} %collective-permute-done.20.after_in, f32[72,8,256]{2,1,0:T(8,128)S(1)} %collective-permute-done.21.before_in, ...), custom_call_target="tpu_custom_call" | custom-call | tf_op jit(solution)/shard_map/last/pallas_call | solution.py:1037
  (32 shorter events, 0.1 us)
Async XLA Ops:
  0.6 38.4 %copy-start.3 = (f32[2,8,256]{2,1,0:T(8,128)S(1)}, f32[2,8,256]{2,1,0:T(8,128)}, u32[]{:S(2)}) copy-start(f32[2,8,256]{2,1,0:T(8,128)} %south.7) | copy-start | bytes 49156
  0.6 38.4 %copy-start.2 = (f32[2,8,256]{2,1,0:T(8,128)S(1)}, f32[2,8,256]{2,1,0:T(8,128)}, u32[]{:S(2)}) copy-start(f32[2,8,256]{2,1,0:T(8,128)} %north.7) | copy-start | bytes 49156
  0.7 19.3 %copy-start.13 = (s32[2,1]{0,1:T(1,128)S(1)}, s32[2,1]{0,1:T(1,128)}, u32[]{:S(2)}) copy-start(s32[2,1]{0,1:T(1,128)} %param.35) | copy-start | bytes 28
  0.7 19.4 %copy-start.5 = (f32[2,8,1280]{2,1,0:T(8,128)S(1)}, f32[2,8,1280]{2,1,0:T(8,128)}, u32[]{:S(2)}) copy-start(f32[2,8,1280]{2,1,0:T(8,128)} %misfits.1) | copy-start | bytes 245764
  0.7 19.4 %copy-start.1 = (f32[2,72,1280]{2,1,0:T(8,128)S(1)}, f32[2,72,1280]{2,1,0:T(8,128)}, u32[]{:S(2)}) copy-start(f32[2,72,1280]{2,1,0:T(8,128)} %kernels.1) | copy-start | bytes 2211844
  0.7 19.4 %copy-start.7 = (s32[2,1280]{1,0:T(2,128)S(1)}, s32[2,1280]{1,0:T(2,128)}, u32[]{:S(2)}) copy-start(s32[2,1280]{1,0:T(2,128)} %columns.1) | copy-start | bytes 30724
  0.7 19.4 %copy-start.6 = (s32[2,1280,1]{1,2,0:T(1,128)S(1)}, s32[2,1280,1]{1,2,0:T(1,128)}, u32[]{:S(2)}) copy-start(s32[2,1280,1]{1,2,0:T(1,128)} %param.33) | copy-start | bytes 30724
  0.7 38.4 %copy-start.8 = (s32[2,128]{1,0:T(2,128)S(1)}, s32[2,128]{1,0:T(2,128)}, u32[]{:S(2)}) copy-start(s32[2,128]{1,0:T(2,128)} %shift.3) | copy-start | bytes 3076
  8.5 21.2 %collective-permute-start.18 = (f32[73,8,256]{2,1,0:T(8,128)}, f32[73,8,256]{2,1,0:T(8,128)S(1)}, u32[]{:S(2)}, u32[]{:S(2)}) collective-permute-start(f32[73,8,256]{2,1,0:T(8,128)} %get-tuple-element.70.polar_in), channel_id=1, source_target_pairs={{16,0},{32,16},{48,32},{64,48},{80,64},{96,80},{112,96},{0,112},{3... | collective-permute-start | bytes 1794056 | tf_op jit(solution)/shard_map/ppermute | solution.py:995
  15.6 11.6 %collective-permute-start.16 = (f32[72,8,256]{2,1,0:T(8,128)}, f32[72,8,256]{2,1,0:T(8,128)S(1)}, u32[]{:S(2)}, u32[]{:S(2)}) collective-permute-start(f32[72,8,256]{2,1,0:T(8,128)} %get-tuple-element.68), channel_id=1, source_target_pairs={{1,0},{2,1},{3,2},{4,3},{5,4},{6,5},{7,6},{8,7},{9,8},{10,9},{11,1... | collective-permute-start | bytes 1769480 | tf_op jit(solution)/shard_map/ppermute | solution.py:845
  16.9 10.3 %collective-permute-start.17 = (f32[72,8,256]{2,1,0:T(8,128)}, f32[72,8,256]{2,1,0:T(8,128)S(1)}, u32[]{:S(2)}, u32[]{:S(2)}) collective-permute-start(f32[72,8,256]{2,1,0:T(8,128)} %get-tuple-element.69), channel_id=1, source_target_pairs={{0,1},{1,2},{2,3},{3,4},{4,5},{5,6},{6,7},{7,8},{8,9},{9,10},{10,1... | collective-permute-start | bytes 1769480 | tf_op jit(solution)/shard_map/ppermute | solution.py:845
  27.1 11.9 %copy-start.9 = (f32[72,8,256]{2,1,0:T(8,128)}, f32[72,8,256]{2,1,0:T(8,128)S(1)}, u32[]{:S(2)}) copy-start(f32[72,8,256]{2,1,0:T(8,128)S(1)} %collective-permute-done.16.after_in) | copy-start | bytes 1769476
  27.2 2.5 %copy-start.10 = (f32[72,8,256]{2,1,0:T(8,128)}, f32[72,8,256]{2,1,0:T(8,128)S(1)}, u32[]{:S(2)}) copy-start(f32[72,8,256]{2,1,0:T(8,128)S(1)} %collective-permute-done.17.before_in) | copy-start | bytes 1769476
  29.7 0.8 copy-start.11
  30.5 38.1 %all-to-all-start = ((f32[128,24,128]{2,1,0:T(8,128)}), f32[128,24,128]{2,1,0:T(8,128)S(1)}, u32[]{:S(2)}, u32[]{:S(2)}) async-start(f32[128,24,128]{2,1,0:T(8,128)} %pack.1), calls=%async_computation | async-start | bytes 3145728 | tf_op jit(solution)/shard_map/all_to_all | solution.py:1000
  39.1 34.7 %copy-start = (f32[2,71,8,256]{3,2,1,0:T(8,128)S(1)}, f32[2,71,8,256]{3,2,1,0:T(8,128)}, u32[]{:S(2)}) copy-start(f32[2,71,8,256]{3,2,1,0:T(8,128)} %diffusion.1) | copy-start | bytes 3489796
  39.1 34.7 %copy-start.4 = (f32[2,8,256]{2,1,0:T(8,128)S(1)}, f32[2,8,256]{2,1,0:T(8,128)}, u32[]{:S(2)}) copy-start(f32[2,8,256]{2,1,0:T(8,128)} %east.3) | copy-start | bytes 49156
  44.8 1.5 %collective-permute-start.12 = (f32[72,8,256]{2,1,0:T(8,128)}, f32[72,8,256]{2,1,0:T(8,128)}, u32[]{:S(2)}, u32[]{:S(2)}) collective-permute-start(f32[72,8,256]{2,1,0:T(8,128)} %param.12), channel_id=1, source_target_pairs={{79,15},{95,31},{111,47},{127,63},{15,79},{31,95},{47,111},{63,127}} | collective-permute-start | bytes 1769480 | tf_op jit(solution)/shard_map/cond/branch_4_fun/ppermute | solution.py:894
  46.3 20.3 %collective-permute-start.3 = (f32[72,8,256]{2,1,0:T(8,128)}, f32[72,8,256]{2,1,0:T(8,128)}, u32[]{:S(2)}, u32[]{:S(2)}) collective-permute-start(f32[72,8,256]{2,1,0:T(8,128)} %param.3), channel_id=1, source_target_pairs={{48,0},{64,16},{80,32},{96,48},{112,64},{0,80},{16,96},{32,112}} | collective-permute-start | bytes 1769480 | tf_op jit(solution)/shard_map/cond/branch_3_fun/ppermute | solution.py:894
  66.6 7.2 %collective-permute-start.19 = (f32[9,8,128]{2,1,0:T(8,128)S(1)}, f32[9,8,128]{2,1,0:T(8,128)S(1)}, u32[]{:S(2)}, u32[]{:S(2)}) collective-permute-start(f32[9,8,128]{2,1,0:T(8,128)S(1)} %get-tuple-element.82), channel_id=1, source_target_pairs={{0,112},{16,0},{32,16},{48,32},{64,48},{80,64},{96,80},{112,96},{1... | collective-permute-start | bytes 110600 | tf_op jit(solution)/shard_map/ppermute | solution.py:860
  82.1 14.6 %copy-start.12 = (f32[72,8,256]{2,1,0:T(8,128)S(1)}, f32[72,8,256]{2,1,0:T(8,128)}, u32[]{:S(2)}) copy-start(f32[72,8,256]{2,1,0:T(8,128)} %get-tuple-element.90) | copy-start | bytes 1769476
  82.1 17.7 %all-to-all-start.1 = ((f32[8,10,8,256]{3,2,1,0:T(8,128)}), f32[8,10,8,256]{3,2,1,0:T(8,128)S(1)}, u32[]{:S(2)}, u32[]{:S(2)}) async-start(f32[8,10,8,256]{3,2,1,0:T(8,128)} %get-tuple-element.91), calls=%async_computation.1 | async-start | bytes 1310720 | tf_op jit(solution)/shard_map/all_to_all | solution.py:1029
  95.5 16.5 %collective-permute-start.20 = (f32[72,8,256]{2,1,0:T(8,128)}, f32[72,8,256]{2,1,0:T(8,128)S(1)}, u32[]{:S(2)}, u32[]{:S(2)}) collective-permute-start(f32[72,8,256]{2,1,0:T(8,128)} %get-tuple-element.89), channel_id=1, source_target_pairs={{1,0},{2,1},{3,2},{4,3},{5,4},{6,5},{7,6},{8,7},{9,8},{10,9},{11,1... | collective-permute-start | bytes 1769480 | tf_op jit(solution)/shard_map/ppermute | solution.py:845
  96.8 15.2 %collective-permute-start.21 = (f32[72,8,256]{2,1,0:T(8,128)S(1)}, f32[72,8,256]{2,1,0:T(8,128)S(1)}, u32[]{:S(2)}, u32[]{:S(2)}) collective-permute-start(f32[72,8,256]{2,1,0:T(8,128)S(1)} %copy-done.12), channel_id=1, source_target_pairs={{0,1},{1,2},{2,3},{3,4},{4,5},{5,6},{6,7},{7,8},{8,9},{9,10},{10,1... | collective-permute-start | bytes 1769480 | tf_op jit(solution)/shard_map/ppermute | solution.py:845
  102.8 17.7 %all-to-all-start.2 = ((f32[8,9,8,256]{3,2,1,0:T(8,128)}), f32[8,9,8,256]{3,2,1,0:T(8,128)S(1)}, u32[]{:S(2)}, u32[]{:S(2)}) async-start(f32[8,9,8,256]{3,2,1,0:T(8,128)} %rotate.1), calls=%async_computation.2 | async-start | bytes 1179648 | tf_op jit(solution)/shard_map/all_to_all | solution.py:923
  112.9 6.5 %collective-permute-start.22 = (f32[9,8,128]{2,1,0:T(8,128)S(1)}, f32[9,8,128]{2,1,0:T(8,128)S(1)}, u32[]{:S(2)}, u32[]{:S(2)}) collective-permute-start(f32[9,8,128]{2,1,0:T(8,128)S(1)} %edge.1), channel_id=1, source_target_pairs={{0,112},{16,0},{32,16},{48,32},{64,48},{80,64},{96,80},{112,96},{1... | collective-permute-start | bytes 110600 | tf_op jit(solution)/shard_map/ppermute | solution.py:860

commit v9 on v7

--- a/solution.py
+++ b/solution.py
@@ -125,7 +125,7 @@
     owner = target[0:1, :] >> (CAP.bit_length() - 1)
     lower = jnp.where((target[0:1, :] >= 0) & (slot < half), owner * half + slot, -1)
     upper = jnp.where((target[0:1, :] >= 0) & (slot >= half), owner * half + slot - half, -1)
-    owned = 512 // CAP
+    owned = 1024 // CAP
     tiles = out.shape[0] // owned
 
     def copy(i):
@@ -183,9 +183,9 @@
             pltpu.VMEM((2, 2 * LANES, 2 * slots), BF16),
             pltpu.VMEM((steps, slots), jnp.int32),
             pltpu.VMEM((devices, CAP + CAP // 2, LANES), F32),
-            pltpu.SemaphoreType.DMA((devices * CAP // 512,)),
+            pltpu.SemaphoreType.DMA((devices * CAP // 1024,)),
         ],
-        compiler_params=params(20),
+        compiler_params=params(32),
         name="pack",
     )(counts, held(owners), held(columns), held(kernels), held(misfits))
 

time: 129 us -> 129 us (level)
  waiting for transfers between devices: 20.6 us -> 22.6 us
    ppermute x2, starting transfers between devices: 7.19 us -> 5.42 us  [first_exchange(): lax.ppermute(x, AXES, circles((lat,), k))]
    ppermute x2, waiting for transfers between devices: 14.7 us -> 16.4 us  [first_exchange(): lax.ppermute(x, AXES, circles((lat,), k))]
where the time goes in v9:
time: 129 us
  starting transfers between devices  52.8 us (41%)
  Pallas kernels  50.4 us (39%)
  waiting for transfers between devices  22.6 us (18%)
  between operations  2.41 us (2%)
    ppermute x2, waiting for transfers between devices, first_exchange(): lax.ppermute(x, AXES, circles((lat,), k))  16.4 us
    pallas_call x2, Pallas kernels, forcing(): pl.pallas_call(functools.partial(streamed_forcing_kernel if streamed else...  11.5 us
    all_to_all x1, starting transfers between devices, last_exchange(): pole = lax.all_to_all(turned, 'lon', 0, 0, tiled=True)  9.99 us
    ppermute x4, starting transfers between devices, boundary_rows(): return (lax.ppermute(first, 'lat', down), lax.ppermute(last, 'lat', up))  8.72 us
    all_to_all x1, starting transfers between devices, per_device(): got = lax.all_to_all(sent, AXES, 0, 0, tiled=True)  8.52 us
    pallas_call x1, Pallas kernels, per_device(): pl.pallas_call(functools.partial(middle_kernel, 1), out_shape=[*solved_sh...  8.29 us
    pallas_call x1, Pallas kernels, per_device(): pl.pallas_call(functools.partial(first_kernel, 1), out_shape=solved_shape...  7.81 us
    pallas_call x1, Pallas kernels, per_device(): pl.pallas_call(functools.partial(last_kernel, 0), out_shape=[pltpu.HBM(co...  7.76 us
  transfers between devices with their start and end apart: 12, of which 4 were waited for; matrix products, arithmetic and copies ran while one was open for 0% of the time, Pallas kernels for 21%

profile of v9, /device:TPU:0, one launch (start us, length us, event | category | flops | bytes accessed | tf_op | source)
XLA Modules:
  0.0 129.2 jit_solution(8147735056459642621)
XLA Ops:
  0.7 7.8 %first.1 = (f32[72,8,8,256]{3,2,1,0:T(8,128)}, f32[72,8,256]{2,1,0:T(8,128)}, f32[72,8,256]{2,1,0:T(8,128)}, f32[73,8,256]{2,1,0:T(8,128)}, f32[9,8,128]{2,1,0:T(8,128)S(1)}) custom-call(f32[72,8,8,256]{3,2,1,0:T(8,128)} %costate.1, f32[2,71,8,256]{3,2,1,0:T(8,128)} %diffusion.1, f32[2,8,256]{2,1,0:T(8,128)} %north.7, f32[2,8,256]{2,1,0:T(8,128)} %south.7, ...), custom_call_target="tpu_custom_call" | custom-call | tf_op jit(solution)/shard_map/first/pallas_call | solution.py:981
  8.5 7.0 %collective-permute-start.18 = (f32[73,8,256]{2,1,0:T(8,128)}, f32[73,8,256]{2,1,0:T(8,128)S(1)}, u32[]{:S(2)}, u32[]{:S(2)}) collective-permute-start(f32[73,8,256]{2,1,0:T(8,128)} %get-tuple-element.70.polar_in), channel_id=1, source_target_pairs={{16,0},{32,16},{48,32},{64,48},{80,64},{96,80},{112,96},{0,112},{3... | collective-permute-start | bytes 1794056 | tf_op jit(solution)/shard_map/ppermute | solution.py:1002
  15.6 1.3 %collective-permute-start.16 = (f32[72,8,256]{2,1,0:T(8,128)}, f32[72,8,256]{2,1,0:T(8,128)S(1)}, u32[]{:S(2)}, u32[]{:S(2)}) collective-permute-start(f32[72,8,256]{2,1,0:T(8,128)} %get-tuple-element.68), channel_id=1, source_target_pairs={{1,0},{2,1},{3,2},{4,3},{5,4},{6,5},{7,6},{8,7},{9,8},{10,9},{11,1... | collective-permute-start | bytes 1769480 | tf_op jit(solution)/shard_map/ppermute | solution.py:852
  16.9 3.1 %collective-permute-start.17 = (f32[72,8,256]{2,1,0:T(8,128)}, f32[72,8,256]{2,1,0:T(8,128)S(1)}, u32[]{:S(2)}, u32[]{:S(2)}) collective-permute-start(f32[72,8,256]{2,1,0:T(8,128)} %get-tuple-element.69), channel_id=1, source_target_pairs={{0,1},{1,2},{2,3},{3,4},{4,5},{5,6},{6,7},{7,8},{8,9},{9,10},{10,1... | collective-permute-start | bytes 1769480 | tf_op jit(solution)/shard_map/ppermute | solution.py:852
  20.0 0.1 copy.13.counts
  20.1 6.7 %pack.1 = f32[128,24,128]{2,1,0:T(8,128)} custom-call(s32[2,1]{1,0:T(2,128)S(1)} %copy.13.counts, s32[2,1,1280]{2,1,0:T(1,128)S(1)} %bitcast.3, s32[2,1280]{1,0:T(2,128)S(1)} %copy-done.7, f32[2,72,1280]{2,1,0:T(8,128)S(1)} %copy-done.1, f32[2,8,1280]{2,1,0:T(8,128)S(1)} %copy-done.5), custom_call_target="tpu_custom_call" | custom-call | tf_op jit(solution)/shard_map/pack/pallas_call | solution.py:177
  26.8 0.0 collective-permute-done.16.after_in
  26.9 2.8 %collective-permute-done.18.nearby_in = f32[73,8,256]{2,1,0:T(8,128)S(1)} collective-permute-done((f32[73,8,256]{2,1,0:T(8,128)}, f32[73,8,256]{2,1,0:T(8,128)S(1)}, u32[]{:S(2)}, u32[]{:S(2)}) %collective-permute-start.18) | collective-permute-done | bytes 598048 | tf_op jit(solution)/shard_map/ppermute | solution.py:1002
  29.7 0.8 copy-done.11
  30.5 8.5 %all-to-all-start = ((f32[128,24,128]{2,1,0:T(8,128)}), f32[128,24,128]{2,1,0:T(8,128)S(1)}, u32[]{:S(2)}, u32[]{:S(2)}) async-start(f32[128,24,128]{2,1,0:T(8,128)} %pack.1), calls=%async_computation | async-start | bytes 3145728 | tf_op jit(solution)/shard_map/all_to_all | solution.py:1007
  39.1 0.0 copy-start
  39.1 0.0 copy-start.4
  39.1 4.4 %borders.1 = (f32[9,8,128]{2,1,0:T(8,128)S(1)}, f32[72,8,256]{2,1,0:T(8,128)}, s32[1,1]{1,0:T(1,128)}, s32[1,1]{1,0:T(1,128)}) custom-call(s32[2,128]{1,0:T(2,128)S(1)} %copy-done.8, f32[9,8,128]{2,1,0:T(8,128)S(1)} %get-tuple-element.74.column, f32[2,8,256]{2,1,0:T(8,128)S(1)} %copy-done.2, f32[2,8,256]{2,1,0:T(8,128)S(1)} %copy-done.3, ...), custom_call_target="tpu_custom_call" | custom-call | tf_op jit(solution)/shard_map/borders/pallas_call | solution.py:873
  44.8 1.5 %conditional.3 = (f32[72,8,256]{2,1,0:T(8,128)}) conditional(s32[]{:T(128)} %bitcast.2, f32[72,8,256]{2,1,0:T(8,128)} %get-tuple-element.78, f32[72,8,256]{2,1,0:T(8,128)} %get-tuple-element.78, f32[72,8,256]{2,1,0:T(8,128)} %get-tuple-element.78, f32[72,8,256]{2,1,0:T(8,128)} %get-tuple-element.78, ...), branch_computations={%region_8.0_spmd, %region_9.0_spmd, %region_10.0_spmd, %region_11.... | conditional | bytes 2359344 | solution.py:897
  44.8 1.5 %collective-permute-start.12 = (f32[72,8,256]{2,1,0:T(8,128)}, f32[72,8,256]{2,1,0:T(8,128)}, u32[]{:S(2)}, u32[]{:S(2)}) collective-permute-start(f32[72,8,256]{2,1,0:T(8,128)} %param.12), channel_id=1, source_target_pairs={{79,15},{95,31},{111,47},{127,63},{15,79},{31,95},{47,111},{63,127}} | collective-permute-start | bytes 1769480 | tf_op jit(solution)/shard_map/cond/branch_4_fun/ppermute | solution.py:901
  46.3 20.3 %conditional.2 = (f32[72,8,256]{2,1,0:T(8,128)}) conditional(s32[]{:T(128)} %bitcast.1, f32[72,8,256]{2,1,0:T(8,128)} %get-tuple-element.78, f32[72,8,256]{2,1,0:T(8,128)} %get-tuple-element.78, f32[72,8,256]{2,1,0:T(8,128)} %get-tuple-element.78, f32[72,8,256]{2,1,0:T(8,128)} %get-tuple-element.78, ...), branch_computations={%region_0.0_spmd, %region_1.0_spmd, %region_2.0_spmd, %region_3.0_... | conditional | bytes 2359344 | solution.py:897
  46.3 3.9 %collective-permute-start.3 = (f32[72,8,256]{2,1,0:T(8,128)}, f32[72,8,256]{2,1,0:T(8,128)}, u32[]{:S(2)}, u32[]{:S(2)}) collective-permute-start(f32[72,8,256]{2,1,0:T(8,128)} %param.3), channel_id=1, source_target_pairs={{48,0},{64,16},{80,32},{96,48},{112,64},{0,80},{16,96},{32,112}} | collective-permute-start | bytes 1769480 | tf_op jit(solution)/shard_map/cond/branch_3_fun/ppermute | solution.py:901
  50.3 16.4 %collective-permute-done.3 = f32[72,8,256]{2,1,0:T(8,128)} collective-permute-done((f32[72,8,256]{2,1,0:T(8,128)}, f32[72,8,256]{2,1,0:T(8,128)}, u32[]{:S(2)}, u32[]{:S(2)}) %collective-permute-start.3) | collective-permute-done | bytes 589856 | tf_op jit(solution)/shard_map/cond/branch_3_fun/ppermute | solution.py:901
  66.6 2.0 %collective-permute-start.19 = (f32[9,8,128]{2,1,0:T(8,128)S(1)}, f32[9,8,128]{2,1,0:T(8,128)S(1)}, u32[]{:S(2)}, u32[]{:S(2)}) collective-permute-start(f32[9,8,128]{2,1,0:T(8,128)S(1)} %get-tuple-element.82), channel_id=1, source_target_pairs={{0,112},{16,0},{32,16},{48,32},{64,48},{80,64},{96,80},{112,96},{1... | collective-permute-start | bytes 110600 | tf_op jit(solution)/shard_map/ppermute | solution.py:867
  68.6 5.2 %forcing.2.forced = f32[72,8,8,256]{3,2,1,0:T(8,128)S(1)} custom-call(f32[128,24,128]{2,1,0:T(8,128)S(1)} %all-to-all-done.received), custom_call_target="tpu_custom_call" | custom-call | tf_op jit(solution)/shard_map/forcing/pallas_call | solution.py:303
  73.8 8.3 %middle.1 = (f32[72,8,8,256]{3,2,1,0:T(8,128)}, f32[72,8,256]{2,1,0:T(8,128)}, f32[72,8,256]{2,1,0:T(8,128)}, f32[8,10,8,256]{3,2,1,0:T(8,128)}, f32[9,8,128]{2,1,0:T(8,128)S(1)}, /*index=5*/f32[8,8,256]{2,1,0:T(8,128)S(1)}) custom-call(f32[72,8,8,256]{3,2,1,0:T(8,128)} %get-tuple-element.65.before_step, f32[72,8,8,256]{3,2,1,0:T(8,128)S(1)} %forcing.2.forced, ...), custom_call_target="tpu_custom_call" | custom-call | tf_op jit(solution)/shard_map/middle/pallas_call | solution.py:1013
  82.1 6.9 %all-to-all-start.1 = ((f32[8,10,8,256]{3,2,1,0:T(8,128)}), f32[8,10,8,256]{3,2,1,0:T(8,128)S(1)}, u32[]{:S(2)}, u32[]{:S(2)}) async-start(f32[8,10,8,256]{3,2,1,0:T(8,128)} %get-tuple-element.91), calls=%async_computation.1 | async-start | bytes 1310720 | tf_op jit(solution)/shard_map/all_to_all | solution.py:1036
  89.0 6.3 %forcing.3.forcing_in = f32[72,8,8,256]{3,2,1,0:T(8,128)} custom-call(f32[128,24,128]{2,1,0:T(8,128)S(1)} %all-to-all-done.received), custom_call_target="tpu_custom_call" | custom-call | tf_op jit(solution)/shard_map/forcing/pallas_call | solution.py:303
  95.3 1.3 %collective-permute-start.20 = (f32[72,8,256]{2,1,0:T(8,128)}, f32[72,8,256]{2,1,0:T(8,128)S(1)}, u32[]{:S(2)}, u32[]{:S(2)}) collective-permute-start(f32[72,8,256]{2,1,0:T(8,128)} %get-tuple-element.89), channel_id=1, source_target_pairs={{1,0},{2,1},{3,2},{4,3},{5,4},{6,5},{7,6},{8,7},{9,8},{10,9},{11,1... | collective-permute-start | bytes 1769480 | tf_op jit(solution)/shard_map/ppermute | solution.py:852
  96.6 3.1 %collective-permute-start.21 = (f32[72,8,256]{2,1,0:T(8,128)S(1)}, f32[72,8,256]{2,1,0:T(8,128)S(1)}, u32[]{:S(2)}, u32[]{:S(2)}) collective-permute-start(f32[72,8,256]{2,1,0:T(8,128)S(1)} %copy-done.12), channel_id=1, source_target_pairs={{0,1},{1,2},{2,3},{3,4},{4,5},{5,6},{6,7},{7,8},{8,9},{9,10},{10,1... | collective-permute-start | bytes 1769480 | tf_op jit(solution)/shard_map/ppermute | solution.py:852
  99.7 3.0 %rotate.1 = f32[8,9,8,256]{3,2,1,0:T(8,128)} custom-call(s32[2,128]{1,0:T(2,128)S(1)} %copy-done.8, f32[8,10,8,256]{3,2,1,0:T(8,128)S(1)} %all-to-all-done.1.circle_in), custom_call_target="tpu_custom_call" | custom-call | tf_op jit(solution)/shard_map/rotate/pallas_call | solution.py:916
  102.7 10.0 %all-to-all-start.2 = ((f32[8,9,8,256]{3,2,1,0:T(8,128)}), f32[8,9,8,256]{3,2,1,0:T(8,128)S(1)}, u32[]{:S(2)}, u32[]{:S(2)}) async-start(f32[8,9,8,256]{3,2,1,0:T(8,128)} %rotate.1), calls=%async_computation.2 | async-start | bytes 1179648 | tf_op jit(solution)/shard_map/all_to_all | solution.py:930
  112.7 0.9 edge.1
  113.7 4.2 %collective-permute-start.22 = (f32[9,8,128]{2,1,0:T(8,128)S(1)}, f32[9,8,128]{2,1,0:T(8,128)S(1)}, u32[]{:S(2)}, u32[]{:S(2)}) collective-permute-start(f32[9,8,128]{2,1,0:T(8,128)S(1)} %edge.1), channel_id=1, source_target_pairs={{0,112},{16,0},{32,16},{48,32},{64,48},{80,64},{96,80},{112,96},{1... | collective-permute-start | bytes 110600 | tf_op jit(solution)/shard_map/ppermute | solution.py:867
  117.9 2.2 %collective-permute-done.22.edge = f32[9,8,128]{2,1,0:T(8,128)S(1)} collective-permute-done((f32[9,8,128]{2,1,0:T(8,128)S(1)}, f32[9,8,128]{2,1,0:T(8,128)S(1)}, u32[]{:S(2)}, u32[]{:S(2)}) %collective-permute-start.22) | collective-permute-done | bytes 36896 | tf_op jit(solution)/shard_map/ppermute | solution.py:867
  120.0 1.2 all-to-all-done.2.pole_in
  121.2 7.8 %last.1 = (f32[72,8,8,256]{3,2,1,0:T(8,128)}, f32[8,8,256]{2,1,0:T(8,128)}) custom-call(f32[72,8,8,256]{3,2,1,0:T(8,128)} %get-tuple-element.83.before_step, f32[72,8,8,256]{3,2,1,0:T(8,128)} %forcing.3.forcing_in, f32[72,8,256]{2,1,0:T(8,128)S(1)} %collective-permute-done.20.after_in, f32[72,8,256]{2,1,0:T(8,128)S(1)} %collective-permute-done.21.before_in, ...), custom_call_target="tpu_custom_call" | custom-call | tf_op jit(solution)/shard_map/last/pallas_call | solution.py:1044
  (32 shorter events, 0.1 us)
Async XLA Ops:
  0.6 38.4 %copy-start.3 = (f32[2,8,256]{2,1,0:T(8,128)S(1)}, f32[2,8,256]{2,1,0:T(8,128)}, u32[]{:S(2)}) copy-start(f32[2,8,256]{2,1,0:T(8,128)} %south.7) | copy-start | bytes 49156
  0.6 38.4 %copy-start.2 = (f32[2,8,256]{2,1,0:T(8,128)S(1)}, f32[2,8,256]{2,1,0:T(8,128)}, u32[]{:S(2)}) copy-start(f32[2,8,256]{2,1,0:T(8,128)} %north.7) | copy-start | bytes 49156
  0.7 19.3 %copy-start.13 = (s32[2,1]{0,1:T(1,128)S(1)}, s32[2,1]{0,1:T(1,128)}, u32[]{:S(2)}) copy-start(s32[2,1]{0,1:T(1,128)} %param.35) | copy-start | bytes 28
  0.7 19.4 %copy-start.5 = (f32[2,8,1280]{2,1,0:T(8,128)S(1)}, f32[2,8,1280]{2,1,0:T(8,128)}, u32[]{:S(2)}) copy-start(f32[2,8,1280]{2,1,0:T(8,128)} %misfits.1) | copy-start | bytes 245764
  0.7 19.4 %copy-start.1 = (f32[2,72,1280]{2,1,0:T(8,128)S(1)}, f32[2,72,1280]{2,1,0:T(8,128)}, u32[]{:S(2)}) copy-start(f32[2,72,1280]{2,1,0:T(8,128)} %kernels.1) | copy-start | bytes 2211844
  0.7 19.4 %copy-start.7 = (s32[2,1280]{1,0:T(2,128)S(1)}, s32[2,1280]{1,0:T(2,128)}, u32[]{:S(2)}) copy-start(s32[2,1280]{1,0:T(2,128)} %columns.1) | copy-start | bytes 30724
  0.7 19.4 %copy-start.6 = (s32[2,1280,1]{1,2,0:T(1,128)S(1)}, s32[2,1280,1]{1,2,0:T(1,128)}, u32[]{:S(2)}) copy-start(s32[2,1280,1]{1,2,0:T(1,128)} %param.33) | copy-start | bytes 30724
  0.7 38.4 %copy-start.8 = (s32[2,128]{1,0:T(2,128)S(1)}, s32[2,128]{1,0:T(2,128)}, u32[]{:S(2)}) copy-start(s32[2,128]{1,0:T(2,128)} %shift.3) | copy-start | bytes 3076
  8.5 21.2 %collective-permute-start.18 = (f32[73,8,256]{2,1,0:T(8,128)}, f32[73,8,256]{2,1,0:T(8,128)S(1)}, u32[]{:S(2)}, u32[]{:S(2)}) collective-permute-start(f32[73,8,256]{2,1,0:T(8,128)} %get-tuple-element.70.polar_in), channel_id=1, source_target_pairs={{16,0},{32,16},{48,32},{64,48},{80,64},{96,80},{112,96},{0,112},{3... | collective-permute-start | bytes 1794056 | tf_op jit(solution)/shard_map/ppermute | solution.py:1002
  15.6 11.3 %collective-permute-start.16 = (f32[72,8,256]{2,1,0:T(8,128)}, f32[72,8,256]{2,1,0:T(8,128)S(1)}, u32[]{:S(2)}, u32[]{:S(2)}) collective-permute-start(f32[72,8,256]{2,1,0:T(8,128)} %get-tuple-element.68), channel_id=1, source_target_pairs={{1,0},{2,1},{3,2},{4,3},{5,4},{6,5},{7,6},{8,7},{9,8},{10,9},{11,1... | collective-permute-start | bytes 1769480 | tf_op jit(solution)/shard_map/ppermute | solution.py:852
  16.9 10.0 %collective-permute-start.17 = (f32[72,8,256]{2,1,0:T(8,128)}, f32[72,8,256]{2,1,0:T(8,128)S(1)}, u32[]{:S(2)}, u32[]{:S(2)}) collective-permute-start(f32[72,8,256]{2,1,0:T(8,128)} %get-tuple-element.69), channel_id=1, source_target_pairs={{0,1},{1,2},{2,3},{3,4},{4,5},{5,6},{6,7},{7,8},{8,9},{9,10},{10,1... | collective-permute-start | bytes 1769480 | tf_op jit(solution)/shard_map/ppermute | solution.py:852
  26.8 12.2 %copy-start.9 = (f32[72,8,256]{2,1,0:T(8,128)}, f32[72,8,256]{2,1,0:T(8,128)S(1)}, u32[]{:S(2)}) copy-start(f32[72,8,256]{2,1,0:T(8,128)S(1)} %collective-permute-done.16.after_in) | copy-start | bytes 1769476
  26.9 2.8 %copy-start.10 = (f32[72,8,256]{2,1,0:T(8,128)}, f32[72,8,256]{2,1,0:T(8,128)S(1)}, u32[]{:S(2)}) copy-start(f32[72,8,256]{2,1,0:T(8,128)S(1)} %collective-permute-done.17.before_in) | copy-start | bytes 1769476
  29.7 0.8 copy-start.11
  30.5 38.1 %all-to-all-start = ((f32[128,24,128]{2,1,0:T(8,128)}), f32[128,24,128]{2,1,0:T(8,128)S(1)}, u32[]{:S(2)}, u32[]{:S(2)}) async-start(f32[128,24,128]{2,1,0:T(8,128)} %pack.1), calls=%async_computation | async-start | bytes 3145728 | tf_op jit(solution)/shard_map/all_to_all | solution.py:1007
  39.1 34.7 %copy-start = (f32[2,71,8,256]{3,2,1,0:T(8,128)S(1)}, f32[2,71,8,256]{3,2,1,0:T(8,128)}, u32[]{:S(2)}) copy-start(f32[2,71,8,256]{3,2,1,0:T(8,128)} %diffusion.1) | copy-start | bytes 3489796
  39.1 34.7 %copy-start.4 = (f32[2,8,256]{2,1,0:T(8,128)S(1)}, f32[2,8,256]{2,1,0:T(8,128)}, u32[]{:S(2)}) copy-start(f32[2,8,256]{2,1,0:T(8,128)} %east.3) | copy-start | bytes 49156
  44.8 1.5 %collective-permute-start.12 = (f32[72,8,256]{2,1,0:T(8,128)}, f32[72,8,256]{2,1,0:T(8,128)}, u32[]{:S(2)}, u32[]{:S(2)}) collective-permute-start(f32[72,8,256]{2,1,0:T(8,128)} %param.12), channel_id=1, source_target_pairs={{79,15},{95,31},{111,47},{127,63},{15,79},{31,95},{47,111},{63,127}} | collective-permute-start | bytes 1769480 | tf_op jit(solution)/shard_map/cond/branch_4_fun/ppermute | solution.py:901
  46.3 20.3 %collective-permute-start.3 = (f32[72,8,256]{2,1,0:T(8,128)}, f32[72,8,256]{2,1,0:T(8,128)}, u32[]{:S(2)}, u32[]{:S(2)}) collective-permute-start(f32[72,8,256]{2,1,0:T(8,128)} %param.3), channel_id=1, source_target_pairs={{48,0},{64,16},{80,32},{96,48},{112,64},{0,80},{16,96},{32,112}} | collective-permute-start | bytes 1769480 | tf_op jit(solution)/shard_map/cond/branch_3_fun/ppermute | solution.py:901
  66.6 7.2 %collective-permute-start.19 = (f32[9,8,128]{2,1,0:T(8,128)S(1)}, f32[9,8,128]{2,1,0:T(8,128)S(1)}, u32[]{:S(2)}, u32[]{:S(2)}) collective-permute-start(f32[9,8,128]{2,1,0:T(8,128)S(1)} %get-tuple-element.82), channel_id=1, source_target_pairs={{0,112},{16,0},{32,16},{48,32},{64,48},{80,64},{96,80},{112,96},{1... | collective-permute-start | bytes 110600 | tf_op jit(solution)/shard_map/ppermute | solution.py:867
  82.1 14.5 %copy-start.12 = (f32[72,8,256]{2,1,0:T(8,128)S(1)}, f32[72,8,256]{2,1,0:T(8,128)}, u32[]{:S(2)}) copy-start(f32[72,8,256]{2,1,0:T(8,128)} %get-tuple-element.90) | copy-start | bytes 1769476
  82.1 17.6 %all-to-all-start.1 = ((f32[8,10,8,256]{3,2,1,0:T(8,128)}), f32[8,10,8,256]{3,2,1,0:T(8,128)S(1)}, u32[]{:S(2)}, u32[]{:S(2)}) async-start(f32[8,10,8,256]{3,2,1,0:T(8,128)} %get-tuple-element.91), calls=%async_computation.1 | async-start | bytes 1310720 | tf_op jit(solution)/shard_map/all_to_all | solution.py:1036
  95.3 17.4 %collective-permute-start.20 = (f32[72,8,256]{2,1,0:T(8,128)}, f32[72,8,256]{2,1,0:T(8,128)S(1)}, u32[]{:S(2)}, u32[]{:S(2)}) collective-permute-start(f32[72,8,256]{2,1,0:T(8,128)} %get-tuple-element.89), channel_id=1, source_target_pairs={{1,0},{2,1},{3,2},{4,3},{5,4},{6,5},{7,6},{8,7},{9,8},{10,9},{11,1... | collective-permute-start | bytes 1769480 | tf_op jit(solution)/shard_map/ppermute | solution.py:852
  96.6 16.1 %collective-permute-start.21 = (f32[72,8,256]{2,1,0:T(8,128)S(1)}, f32[72,8,256]{2,1,0:T(8,128)S(1)}, u32[]{:S(2)}, u32[]{:S(2)}) collective-permute-start(f32[72,8,256]{2,1,0:T(8,128)S(1)} %copy-done.12), channel_id=1, source_target_pairs={{0,1},{1,2},{2,3},{3,4},{4,5},{5,6},{6,7},{7,8},{8,9},{9,10},{10,1... | collective-permute-start | bytes 1769480 | tf_op jit(solution)/shard_map/ppermute | solution.py:852
  102.7 18.5 %all-to-all-start.2 = ((f32[8,9,8,256]{3,2,1,0:T(8,128)}), f32[8,9,8,256]{3,2,1,0:T(8,128)S(1)}, u32[]{:S(2)}, u32[]{:S(2)}) async-start(f32[8,9,8,256]{3,2,1,0:T(8,128)} %rotate.1), calls=%async_computation.2 | async-start | bytes 1179648 | tf_op jit(solution)/shard_map/all_to_all | solution.py:930
  113.7 6.4 %collective-permute-start.22 = (f32[9,8,128]{2,1,0:T(8,128)S(1)}, f32[9,8,128]{2,1,0:T(8,128)S(1)}, u32[]{:S(2)}, u32[]{:S(2)}) collective-permute-start(f32[9,8,128]{2,1,0:T(8,128)S(1)} %edge.1), channel_id=1, source_target_pairs={{0,112},{16,0},{32,16},{48,32},{64,48},{80,64},{96,80},{112,96},{1... | collective-permute-start | bytes 110600 | tf_op jit(solution)/shard_map/ppermute | solution.py:867
